TPU v7x, 256 devices: a whole 4x4x8 slice. The times are simulated.
256 devices in a mesh: context: 32 (over x, z), mirror: 2 (over core), tensor: 4 (over y).
Axes of the slice: x: 4, y: 4, z: 8, core: 2. Of those that a mesh axis runs over, the one named last changes fastest.
Arguments:
- hyena_q: bfloat16 [8192, 8192], P(('context', 'mirror'), 'tensor'), may hold values from -57 to 57
- hyena_k: bfloat16 [8192, 8192], P(('context', 'mirror'), 'tensor'), may hold values from -6 to 6
- hyena_v: bfloat16 [8192, 8192], P(('context', 'mirror'), 'tensor'), may hold values from -6 to 6
- filters: bfloat16 [512, 128], P('tensor'), may hold values from -0.5 to 0.5
- norm_gain: float32 [8192], P('tensor'), may hold values from 0.1 to 1.9
- attn_q: bfloat16 [8192, 8192], P(('context', 'mirror'), 'tensor'), may hold values from -35 to 35
- attn_k: bfloat16 [8192, 8192], P(('context', 'mirror'), 'tensor'), may hold values from -5 to 5
- out_grad: bfloat16 [8192, 8192], P(('context', 'mirror'), 'tensor'), may hold values from -20 to 20
- doc_lengths: int32 [4], replicated, may hold values from 1 to 4096, 8192 in all
Outputs:
- attn_out: bfloat16 [8192, 8192], P(('context', 'mirror'), 'tensor')
- grad_attn_q: bfloat16 [8192, 8192], P(('context', 'mirror'), 'tensor')
- grad_attn_k: bfloat16 [8192, 8192], P(('context', 'mirror'), 'tensor')
- grad_hyena_q: bfloat16 [8192, 8192], P(('context', 'mirror'), 'tensor')
- grad_hyena_k: bfloat16 [8192, 8192], P(('context', 'mirror'), 'tensor')
- grad_hyena_v: bfloat16 [8192, 8192], P(('context', 'mirror'), 'tensor')
- grad_filters: float32 [512, 128], P('tensor')
All inputs are finite; a program needn't handle non-finite values.
Results may differ from a plain program's by a relative error of at most 0.0064.
Values may be sent and summed in bfloat16 or wider, within the bound.
No kernel may reach another device: no remote copies, remote signals or barrier semaphores. Data moves between devices by JAX's collectives and lax.ppermute only.
A program may use at most 128 MiB of HBM per device.

v0:
```python
import jax
import jax.numpy as jnp
from jax import lax
from jax.sharding import PartitionSpec as P

HEAD = 128
D = 8192
REACH = 2


def passed_along(block, axis, distance):
    devices = range(lax.axis_size(axis))
    route = [(i - distance, i) for i in devices if i - distance in devices]
    return lax.ppermute(block, axis, route)


def doc_index(doc_lengths, positions):
    doc_ends = jnp.cumsum(doc_lengths, dtype=jnp.int32)
    return jnp.sum(
        (positions[:, None] >= doc_ends[None, :]).astype(jnp.int32), axis=1, dtype=jnp.int32
    )


def banded(band_table, row_count, col_count):
    repeated = jnp.tile(band_table, (1, row_count + 1))[:, : row_count * col_count]
    return repeated.reshape(band_table.shape[0], row_count, col_count)


def attend(queries, key_heads, allowed, score_scale):
    scores = (
        jnp.einsum("thd,uhd->htu", queries, key_heads, preferred_element_type=jnp.float32)
        * score_scale
    )
    row_top = jnp.max(jnp.where(allowed[None], scores, -1e30), axis=2, keepdims=True)
    row_total = jnp.sum(
        jnp.exp(jnp.where(allowed[None], scores - row_top, -1e30)), axis=2, keepdims=True
    )
    row_lse = row_top + jnp.log(row_total)
    return (jnp.where(allowed[None], jnp.exp(scores - row_lse), 0.0), row_lse)


def body(hyena_q, hyena_k, hyena_v, filters, norm_gain, attn_q, attn_k, out_grad, doc_lengths):
    tok_rows, channels = hyena_q.shape
    groups, tap_count = filters.shape
    group_width = channels // groups
    heads_dev = channels // HEAD
    pad_rows = tok_rows + tap_count
    offset = lax.axis_index(("context", "mirror")) * tok_rows
    score_scale = HEAD ** (-0.5)
    window_span = REACH * tok_rows
    own_pos = offset + jnp.arange(tok_rows, dtype=jnp.int32)
    own_doc = doc_index(doc_lengths, own_pos)
    kv_product = (hyena_k.astype(jnp.float32) * hyena_v.astype(jnp.float32)).astype(jnp.bfloat16)
    left_rim = passed_along(kv_product[tok_rows - (tap_count - 1) :], ("context", "mirror"), 1)
    wide_pad = jnp.concatenate(
        [left_rim, kv_product, jnp.zeros((1, channels), jnp.bfloat16)], axis=0
    )
    wide_pos = offset - (tap_count - 1) + jnp.arange(pad_rows, dtype=jnp.int32)
    fwd_mask = own_doc[:, None] == doc_index(doc_lengths, wide_pos)[None, :]
    zeros_tail = jnp.zeros((groups, pad_rows + 1 - tap_count), jnp.bfloat16)
    fwd_table = jnp.concatenate([filters[:, ::-1], zeros_tail], axis=1)
    fwd_band = banded(fwd_table, tok_rows, pad_rows) * fwd_mask[None].astype(jnp.bfloat16)
    wide_groups = wide_pad.reshape(pad_rows, groups, group_width)
    signal = jnp.einsum(
        "gtu,ugc->tgc", fwd_band, wide_groups, preferred_element_type=jnp.float32
    ).reshape(tok_rows, channels)
    hyena_mix = hyena_q.astype(jnp.float32) * signal
    square_sum = lax.psum(jnp.sum(hyena_mix * hyena_mix, axis=1), "tensor")
    inv_rms = lax.rsqrt(square_sum / D + 1e-06)
    values = (hyena_mix * inv_rms[:, None] * norm_gain[None, :]).astype(jnp.bfloat16)
    earlier = []
    for distance in range(1, REACH + 1):
        earlier.append(passed_along((attn_k, values), ("context", "mirror"), distance))
    key_win = jnp.concatenate([piece[0] for piece in earlier[::-1]] + [attn_k], axis=0)
    value_win = jnp.concatenate([piece[1] for piece in earlier[::-1]] + [values], axis=0)
    window = (REACH + 1) * tok_rows
    key_pos = offset - REACH * tok_rows + jnp.arange(window, dtype=jnp.int32)
    key_doc = doc_index(doc_lengths, key_pos)
    allowed = (
        (key_pos[None, :] >= 0)
        & (key_pos[None, :] <= own_pos[:, None])
        & (own_pos[:, None] - key_pos[None, :] <= window_span)
        & (key_doc[None, :] == own_doc[:, None])
    )
    queries = attn_q.reshape(tok_rows, heads_dev, HEAD)
    grad_heads = out_grad.reshape(tok_rows, heads_dev, HEAD)
    key_heads = key_win.reshape(window, heads_dev, HEAD)
    value_heads = value_win.reshape(window, heads_dev, HEAD)
    attn_prob, row_lse = attend(queries, key_heads, allowed, score_scale)
    prob_half = attn_prob.astype(jnp.bfloat16)
    attn_out = (
        jnp.einsum("htu,uhd->thd", prob_half, value_heads, preferred_element_type=jnp.float32)
        .astype(jnp.bfloat16)
        .reshape(tok_rows, channels)
    )
    grad_prob = jnp.einsum(
        "thd,uhd->htu", grad_heads, value_heads, preferred_element_type=jnp.float32
    )
    row_delta = jnp.sum(attn_prob * grad_prob, axis=2, keepdims=True)
    grad_score = (attn_prob * (grad_prob - row_delta) * score_scale).astype(jnp.bfloat16)
    grad_attn_q = (
        jnp.einsum("htu,uhd->thd", grad_score, key_heads, preferred_element_type=jnp.float32)
        .astype(jnp.bfloat16)
        .reshape(tok_rows, channels)
    )
    own_start = REACH * tok_rows
    key_part = jnp.einsum("htu,thd->uhd", grad_score, queries, preferred_element_type=jnp.float32)
    value_part = jnp.einsum(
        "htu,thd->uhd", prob_half, grad_heads, preferred_element_type=jnp.float32
    )
    grad_keys = key_part[own_start:]
    grad_vals = value_part[own_start:]
    for distance in range(1, REACH + 1):
        low_row = (REACH - distance) * tok_rows
        returned = passed_along(
            (key_part[low_row : low_row + tok_rows], value_part[low_row : low_row + tok_rows]),
            ("context", "mirror"),
            -distance,
        )
        grad_keys = grad_keys + returned[0]
        grad_vals = grad_vals + returned[1]
    grad_attn_k = grad_keys.astype(jnp.bfloat16).reshape(tok_rows, channels)
    grad_values = grad_vals.reshape(tok_rows, channels)
    inner_sum = lax.psum(jnp.sum(norm_gain[None, :] * grad_values * hyena_mix, axis=1), "tensor")
    grad_mix = inv_rms[:, None] * (
        norm_gain[None, :] * grad_values - hyena_mix * (inner_sum * inv_rms * inv_rms / D)[:, None]
    )
    grad_hyena_q = (grad_mix * signal).astype(jnp.bfloat16)
    grad_signal = (grad_mix * hyena_q.astype(jnp.float32)).astype(jnp.bfloat16)
    right_rim = passed_along(grad_signal[: tap_count - 1], ("context", "mirror"), -1)
    back_pad = jnp.concatenate(
        [grad_signal, right_rim, jnp.zeros((1, channels), jnp.bfloat16)], axis=0
    )
    back_pos = offset + jnp.arange(pad_rows, dtype=jnp.int32)
    back_mask = own_doc[:, None] == doc_index(doc_lengths, back_pos)[None, :]
    back_table = jnp.concatenate([filters, zeros_tail], axis=1)
    back_band = banded(back_table, tok_rows, pad_rows) * back_mask[None].astype(jnp.bfloat16)
    grad_kv = jnp.einsum(
        "gtu,ugc->tgc",
        back_band,
        back_pad.reshape(pad_rows, groups, group_width),
        preferred_element_type=jnp.float32,
    ).reshape(tok_rows, channels)
    grad_hyena_k = (grad_kv * hyena_v.astype(jnp.float32)).astype(jnp.bfloat16)
    grad_hyena_v = (grad_kv * hyena_k.astype(jnp.float32)).astype(jnp.bfloat16)
    block_count = 4
    block_size = groups // block_count
    mask_float = fwd_mask.astype(jnp.float32)

    def filter_block(pieces):
        grad_block, wide_block = pieces
        correlation = (
            jnp.einsum("tgc,ugc->gtu", grad_block, wide_block, preferred_element_type=jnp.float32)
            * mask_float[None]
        )
        flattened = jnp.pad(
            correlation.reshape(block_size, tok_rows * pad_rows), ((0, 0), (0, tok_rows))
        )
        diagonal = flattened.reshape(block_size, tok_rows, pad_rows + 1)[:, :, :tap_count]
        return jnp.sum(diagonal, axis=1)[:, ::-1]

    grad_blocks = grad_signal.reshape(tok_rows, block_count, block_size, group_width).transpose(
        1, 0, 2, 3
    )
    wide_blocks = wide_groups.reshape(pad_rows, block_count, block_size, group_width).transpose(
        1, 0, 2, 3
    )
    local_filters = lax.map(filter_block, (grad_blocks, wide_blocks)).reshape(groups, tap_count)
    grad_filters = lax.psum(local_filters, ("context", "mirror"))
    return (
        attn_out,
        grad_attn_q,
        grad_attn_k,
        grad_hyena_q,
        grad_hyena_k,
        grad_hyena_v,
        grad_filters,
    )


def solution(mesh):
    return jax.shard_map(
        body,
        mesh=mesh,
        in_specs=(
            P(("context", "mirror"), "tensor"),
            P(("context", "mirror"), "tensor"),
            P(("context", "mirror"), "tensor"),
            P("tensor", None),
            P("tensor"),
            P(("context", "mirror"), "tensor"),
            P(("context", "mirror"), "tensor"),
            P(("context", "mirror"), "tensor"),
            P(),
        ),
        out_specs=(
            P(("context", "mirror"), "tensor"),
            P(("context", "mirror"), "tensor"),
            P(("context", "mirror"), "tensor"),
            P(("context", "mirror"), "tensor"),
            P(("context", "mirror"), "tensor"),
            P(("context", "mirror"), "tensor"),
            P("tensor", None),
        ),
        check_vma=False,
    )
```

profile of v0, /device:TPU:6, one launch (start us, length us, event | category | flops | bytes accessed | tf_op | source)
XLA Modules:
  0.0 416.8 jit_solution(6076285192775258305)
XLA Ops:
  8.6 2.1 collective-permute-start.4
  10.7 3.8 collective-permute-start.3
  15.9 1.5 copy.66
  19.3 3.6 collective-permute-start
  26.7 4.5 %tile.8 = bf16[128,129,257]{0,2,1:T(8,128)(2,1)} broadcast(bf16[128,257]{0,1:T(8,128)(2,1)S(1)} %concatenate.19.clone), dimensions={0,2} | broadcast | bytes 8552960 | tf_op jit(solution)/shard_map/tile | solution.py:25
  31.2 13.2 %tile.9 = bf16[128,33153]{0,1:T(8,128)(2,1)} reshape(bf16[128,129,257]{0,2,1:T(8,128)(2,1)} %tile.8) | data formatting | bytes 16974336 | tf_op jit(solution)/shard_map/tile | solution.py:25
  44.5 7.1 %slice.49 = bf16[128,32768]{0,1:T(8,128)(2,1)} slice(bf16[128,33153]{0,1:T(8,128)(2,1)} %tile.9), slice={[0:128], [0:32768]} | slice | bytes 16777216 | tf_op jit(solution)/shard_map/slice | solution.py:25
  51.5 12.5 %copy.69 = bf16[128,128,256]{2,1,0:T(8,128)(2,1)} copy(bf16[128,128,256]{0,2,1:T(8,128)(2,1)} %bitcast.165) | data formatting | bytes 16777216 | tf_op jit(solution)/shard_map/reshape | solution.py:26
  64.0 4.5 %tile.20 = bf16[128,129,257]{0,2,1:T(8,128)(2,1)} broadcast(bf16[128,257]{0,1:T(8,128)(2,1)S(1)} %concatenate.23.clone), dimensions={0,2} | broadcast | bytes 8552960 | tf_op jit(solution)/shard_map/tile | solution.py:25
  68.5 13.2 %tile.21 = bf16[128,33153]{0,1:T(8,128)(2,1)} reshape(bf16[128,129,257]{0,2,1:T(8,128)(2,1)} %tile.20) | data formatting | bytes 16974336 | tf_op jit(solution)/shard_map/tile | solution.py:25
  81.7 7.1 %slice.57 = bf16[128,32768]{0,1:T(8,128)(2,1)} slice(bf16[128,33153]{0,1:T(8,128)(2,1)} %tile.21), slice={[0:128], [0:32768]} | slice | bytes 16777216 | tf_op jit(solution)/shard_map/slice | solution.py:25
  88.8 12.6 %copy.84 = bf16[128,128,256]{2,1,0:T(8,128)(2,1)} copy(bf16[128,128,256]{0,2,1:T(8,128)(2,1)} %bitcast.166) | data formatting | bytes 16777216 | tf_op jit(solution)/shard_map/reshape | solution.py:26
  105.9 4.7 %collective-permute-start.8 = (f32[128,16,128]{0,2,1:T(8,128)S(1)}, f32[128,16,128]{0,2,1:T(8,128)S(1)}, u32[]{:S(2)}, u32[]{:S(2)}) collective-permute-start(f32[128,16,128]{0,2,1:T(8,128)S(1)} %get-tuple-element.131), channel_id=1, source_target_pairs={{8,0},{12,4},{16,8},{20,12},{24,16},{28,20},{32,24},{36,28},{40,32... | collective-permute-start | bytes 3145736 | tf_op jit(solution)/shard_map/ppermute | solution.py:14
  110.6 3.5 collective-permute-start.7
  114.2 1.5 maximum_maximum_fusion
  115.7 2.3 fusion.10
  118.0 15.6 %collective-permute-done.8 = f32[128,16,128]{0,2,1:T(8,128)S(1)} collective-permute-done((f32[128,16,128]{0,2,1:T(8,128)S(1)}, f32[128,16,128]{0,2,1:T(8,128)S(1)}, u32[]{:S(2)}, u32[]{:S(2)}) %collective-permute-start.8) | collective-permute-done | bytes 1048608 | tf_op jit(solution)/shard_map/ppermute | solution.py:14
  133.6 10.8 %collective-permute-done.7 = f32[128,16,128]{0,2,1:T(8,128)S(1)} collective-permute-done((f32[128,16,128]{0,2,1:T(8,128)S(1)}, f32[128,16,128]{0,2,1:T(8,128)S(1)}, u32[]{:S(2)}, u32[]{:S(2)}) %collective-permute-start.7) | collective-permute-done | bytes 1048608 | tf_op jit(solution)/shard_map/ppermute | solution.py:14
  145.6 10.7 %all-reduce.3 = (f32[128]{0:T(128)S(1)}, f32[128]{0:T(128)S(1)}) all-reduce(f32[128]{0:T(128)S(1)} %get-tuple-element.111, f32[128]{0:T(128)S(1)} %get-tuple-element.110), channel_id=1, replica_groups=mesh['context'=32,'mirror'=2,'tensor'=4] {'tensor'}, use_global_device_ids=true, to_apply=%region_4.5 | all-reduce | flops 256 | bytes 2048 | tf_op jit(solution)/shard_map/psum | solution.py:68
  156.3 3.4 fusion.45
  159.7 1.9 collective-permute-start.2
  161.6 3.3 collective-permute-start.1
  164.9 4.4 %collective-permute-start.9 = (bf16[127,2048]{0,1:T(8,128)(2,1)}, bf16[127,2048]{0,1:T(8,128)(2,1)}, u32[]{:S(2)}, u32[]{:S(2)}) collective-permute-start(bf16[127,2048]{0,1:T(8,128)(2,1)} %bitcast.150), channel_id=1, source_target_pairs={{4,0},{8,4},{12,8},{16,12},{20,16},{24,20},{28,24},{32,28},{36,32}... | collective-permute-start | bytes 1560584 | tf_op jit(solution)/shard_map/ppermute | solution.py:14
  169.3 67.7 %while.13 = (s32[]{:T(128)}, f32[4,32,128]{2,1,0:T(8,128)}, bf16[4,128,32,16]{1,3,2,0:T(8,128)(2,1)}, bf16[4,256,32,16]{1,3,2,0:T(8,128)(2,1)}, s32[256]{0:T(256...) while((s32[]{:T(128)}, f32[4,32,128]{2,1,0:T(8,128)}, bf16[4,128,32,16]{1,3,2,0:T(8,128)(2,1)}, ...), condition=%wide.region_14.15_spmd.clone, body=%wide.region_12.14_spmd.clone.sunk | while | flops 35188736 | bytes 32246372 | solution.py:168
  169.4 1.8 convolution_multiply_fusion.2
  171.2 2.4 copy.103
  173.6 2.2 pad.33
  175.8 8.0 %reshape.319 = f32[32,128,257]{2,1,0:T(8,128)} reshape(f32[32,32896]{1,0:T(8,128)} %pad.33) | data formatting | bytes 8421376 | tf_op jit(solution)/shard_map/while/body/eval_jaxpr/reshape | solution.py:159
  183.8 1.7 slice_reduce_fusion.2
  186.3 1.8 convolution_multiply_fusion.2
  188.1 2.4 copy.103
  190.5 2.2 pad.33
  192.8 8.0 %reshape.319 = f32[32,128,257]{2,1,0:T(8,128)} reshape(f32[32,32896]{1,0:T(8,128)} %pad.33) | data formatting | bytes 8421376 | tf_op jit(solution)/shard_map/while/body/eval_jaxpr/reshape | solution.py:159
  200.7 1.7 slice_reduce_fusion.2
  203.2 1.8 convolution_multiply_fusion.2
  205.0 2.4 copy.103
  207.4 2.2 pad.33
  209.7 8.0 %reshape.319 = f32[32,128,257]{2,1,0:T(8,128)} reshape(f32[32,32896]{1,0:T(8,128)} %pad.33) | data formatting | bytes 8421376 | tf_op jit(solution)/shard_map/while/body/eval_jaxpr/reshape | solution.py:159
  217.6 1.7 slice_reduce_fusion.2
  220.1 1.8 convolution_multiply_fusion.2
  221.9 2.4 copy.103
  224.4 2.2 pad.33
  226.6 8.0 %reshape.319 = f32[32,128,257]{2,1,0:T(8,128)} reshape(f32[32,32896]{1,0:T(8,128)} %pad.33) | data formatting | bytes 8421376 | tf_op jit(solution)/shard_map/while/body/eval_jaxpr/reshape | solution.py:159
  234.6 1.7 slice_reduce_fusion.2
  237.0 2.0 copy.88
  239.0 1.4 maximum_maximum_fusion.1
  240.5 6.7 %fusion.8 = f32[128,16,128]{2,1,0:T(8,128)} fusion(bf16[256,128,16]{0,2,1:T(8,128)(2,1)S(1)} %bitcast.175, bf16[128,128,256]{2,1,0:T(8,128)(2,1)} %copy.84, bf16[128,256]{1,0:T(8,128)(2,1)S(1)} %get-tuple-element.137), kind=kOutput, calls=%fused_computation.11 | convolution fusion | flops 138412032 | bytes 10551296 | tf_op jit(solution)/shard_map/gtu,ugc->tgc/dot_general | solution.py:138
  247.2 1.6 pad_maximum_fusion
  250.0 2.3 fusion.72
  252.3 6.6 %convolution_bitcast_fusion.1 = f32[384,16,128]{0,2,1:T(8,128)} fusion(bf16[128,16,128]{0,2,1:T(8,128)(2,1)} %bitcast.177, f32[16,384,128]{2,1,0:T(8,128)} %fusion.72, f32[16,384,128]{2,1,0:T(8,128)S(1)} %get-tuple-element.142, f32[16,128]{1,0:T(8,128)S(1)} %log_add_fusion, pred[128,384]{0,1:T(8,128)(4,1)S(1)} %fusion.54), kind=kOutput, calls=%fused_computation.32 | convolution fusion | flops 209979776 | bytes 10018816 | tf_op jit(solution)/shard_map/htu,thd->uhd/dot_general | solution.py:107
  259.0 3.4 fusion.70
  262.3 3.6 collective-permute-start.6
  265.9 2.1 collective-permute-start.5
  269.3 2.0 copy.89
  271.3 2.0 copy.90
  273.4 3.0 convolution_convert_fusion
  276.3 2.0 copy.85
  278.4 6.2 %fusion.44 = bf16[16,128,128]{2,1,0:T(8,128)(2,1)} fusion(bf16[384,16,128]{0,2,1:T(8,128)(2,1)} %bitcast.172, f32[16,384,128]{2,1,0:T(8,128)} %fusion.72, f32[16,384,128]{2,1,0:T(8,128)S(1)} %get-tuple-element.142, f32[16,128]{1,0:T(8,128)S(1)} %log_add_fusion, pred[128,384]{0,1:T(8,128)(4,1)S(1)} %fusion.54), kind=kOutput, calls=%fused_computation.54 | convolution fusion | flops 210241920 | bytes 8445952 | tf_op jit(solution)/shard_map/htu,uhd->thd/dot_general | solution.py:102
  284.6 2.0 copy.86
  286.7 2.3 collective-permute-done.6
  289.0 10.5 %collective-permute-done.5 = f32[128,16,128]{0,2,1:T(8,128)} collective-permute-done((f32[128,16,128]{0,2,1:T(8,128)}, f32[128,16,128]{0,2,1:T(8,128)}, u32[]{:S(2)}, u32[]{:S(2)}) %collective-permute-start.5) | collective-permute-done | bytes 1048608 | tf_op jit(solution)/shard_map/ppermute | solution.py:14
  299.5 2.0 fusion.51
  302.6 105.9 %all-reduce.6.cloned.1.call-done = f32[128,128]{1,0:T(8,128)} async-done(((f32[128,128]{1,0:T(8,128)}), f32[128,128]{1,0:T(8,128)}) %all-reduce.6.cloned.1.call-update) | async-done | bytes 65552 | tf_op jit(solution)/shard_map/psum | solution.py:169
  408.5 1.5 copy.114
  (104 shorter events, 20.4 us)
Async XLA Ops:
  7.2 15.8 %copy-start.19 = (bf16[128,128]{1,0:T(8,128)(2,1)S(1)}, bf16[128,128]{1,0:T(8,128)(2,1)}, u32[]{:S(2)}) copy-start(bf16[128,128]{1,0:T(8,128)(2,1)} %param.14) | copy-start | bytes 98308
  7.2 16.1 %copy-start.16 = (bf16[128,2048]{1,0:T(8,128)(2,1)S(1)}, bf16[128,2048]{1,0:T(8,128)(2,1)}, u32[]{:S(2)}) copy-start(bf16[128,2048]{1,0:T(8,128)(2,1)} %param.11) | copy-start | bytes 1572868
  7.2 401.3 %all-reduce.6.cloned.1.call-start = ((), (), s32[]{:S(2)}) async-start(), calls=%async_computation | async-start | bytes 131072 | tf_op jit(solution)/shard_map/psum | solution.py:169
  8.6 15.6 %copy-start.17 = (bf16[128,2048]{1,0:T(8,128)(2,1)S(1)}, bf16[128,2048]{1,0:T(8,128)(2,1)}, u32[]{:S(2)}) copy-start(bf16[128,2048]{1,0:T(8,128)(2,1)} %param.18) | copy-start | bytes 1572868
  8.6 93.2 %collective-permute-start.4 = (bf16[128,2048]{0,1:T(8,128)(2,1)S(1)}, bf16[128,2048]{0,1:T(8,128)(2,1)}, u32[]{:S(2)}, u32[]{:S(2)}) collective-permute-start(bf16[128,2048]{0,1:T(8,128)(2,1)S(1)} %copy.70), channel_id=1, source_target_pairs={{0,4},{4,8},{8,12},{12,16},{16,20},{20,24},{24,28},{28,32},{32,36}... | collective-permute-start | bytes 1572872 | tf_op jit(solution)/shard_map/ppermute | solution.py:14
  10.7 91.2 %collective-permute-start.3 = (bf16[128,2048]{0,1:T(8,128)(2,1)S(1)}, bf16[128,2048]{0,1:T(8,128)(2,1)}, u32[]{:S(2)}, u32[]{:S(2)}) collective-permute-start(bf16[128,2048]{0,1:T(8,128)(2,1)S(1)} %copy.70), channel_id=1, source_target_pairs={{0,8},{4,12},{8,16},{12,20},{16,24},{20,28},{24,32},{28,36},{32,40... | collective-permute-start | bytes 1572872 | tf_op jit(solution)/shard_map/ppermute | solution.py:14
  15.8 10.8 %copy-start.8 = (bf16[128,2048]{0,1:T(8,128)(2,1)}, bf16[128,2048]{0,1:T(8,128)(2,1)S(1)}, u32[]{:S(2)}) copy-start(bf16[128,2048]{0,1:T(8,128)(2,1)S(1)} %copy.67) | copy-start | bytes 1572868
  15.8 9.4 %copy-start.21 = (s32[4]{0:T(128)S(1)}, s32[4]{0:T(128)}, u32[]{:S(2)}) copy-start(s32[4]{0:T(128)} %param.19) | copy-start | bytes 52
  15.8 9.8 %copy-start.18 = (bf16[128,2048]{1,0:T(8,128)(2,1)S(1)}, bf16[128,2048]{1,0:T(8,128)(2,1)}, u32[]{:S(2)}) copy-start(bf16[128,2048]{1,0:T(8,128)(2,1)} %param.16) | copy-start | bytes 1572868
  17.4 13.9 %copy-start.10 = (bf16[128,2048]{0,1:T(8,128)(2,1)}, bf16[128,2048]{0,1:T(8,128)(2,1)S(1)}, u32[]{:S(2)}) copy-start(bf16[128,2048]{0,1:T(8,128)(2,1)S(1)} %copy.66) | copy-start | bytes 1572868
  17.5 0.8 copy-start.6
  19.3 94.8 %collective-permute-start = (bf16[127,2048]{0,1:T(8,128)(2,1)}, bf16[127,2048]{0,1:T(8,128)(2,1)}, u32[]{:S(2)}, u32[]{:S(2)}) collective-permute-start(bf16[127,2048]{0,1:T(8,128)(2,1)} %slice.48), channel_id=1, source_target_pairs={{0,4},{4,8},{8,12},{12,16},{16,20},{20,24},{24,28},{28,32},{32,36}... | collective-permute-start | bytes 1560584 | tf_op jit(solution)/shard_map/ppermute | solution.py:14
  101.3 1.9 copy-start.15
  103.3 1.5 copy-start.4
  103.3 1.5 copy-start.12
  104.1 11.6 %slice-start = ((s8[8388608]{0:T(1024)(128)(4,1)}), s8[4194304]{0:T(1024)(128)(4,1)S(1)}, s32[]{:S(2)}) async-start(s8[8388608]{0:T(1024)(128)(4,1)} %bitcast.163), calls=%async_computation.1 | async-start | bytes 8388608
  104.8 10.9 %slice-start.1 = ((s8[8388608]{0:T(1024)(128)(4,1)}), s8[4194304]{0:T(1024)(128)(4,1)S(1)}, s32[]{:S(2)}) async-start(s8[8388608]{0:T(1024)(128)(4,1)} %bitcast.163), calls=%async_computation.2 | async-start | bytes 8388608
  105.6 8.5 %copy-start.7 = (bf16[128,2048]{0,1:T(8,128)(2,1)S(1)}, bf16[128,2048]{0,1:T(8,128)(2,1)}, u32[]{:S(2)}) copy-start(bf16[128,2048]{0,1:T(8,128)(2,1)} %copy-done.6) | copy-start | bytes 1572868
  105.9 27.7 %collective-permute-start.8 = (f32[128,16,128]{0,2,1:T(8,128)S(1)}, f32[128,16,128]{0,2,1:T(8,128)S(1)}, u32[]{:S(2)}, u32[]{:S(2)}) collective-permute-start(f32[128,16,128]{0,2,1:T(8,128)S(1)} %get-tuple-element.131), channel_id=1, source_target_pairs={{8,0},{12,4},{16,8},{20,12},{24,16},{28,20},{32,24},{36,28},{40,32... | collective-permute-start | bytes 3145736 | tf_op jit(solution)/shard_map/ppermute | solution.py:14
  110.6 33.8 %collective-permute-start.7 = (f32[128,16,128]{0,2,1:T(8,128)S(1)}, f32[128,16,128]{0,2,1:T(8,128)S(1)}, u32[]{:S(2)}, u32[]{:S(2)}) collective-permute-start(f32[128,16,128]{0,2,1:T(8,128)S(1)} %get-tuple-element.130), channel_id=1, source_target_pairs={{4,0},{8,4},{12,8},{16,12},{20,16},{24,20},{28,24},{32,28},{36,32}... | collective-permute-start | bytes 3145736 | tf_op jit(solution)/shard_map/ppermute | solution.py:14
  115.7 2.3 copy-start
  118.0 27.0 %copy-start.1 = (f32[128,16,128]{2,1,0:T(8,128)}, f32[128,16,128]{2,1,0:T(8,128)S(1)}, u32[]{:S(2)}) copy-start(f32[128,16,128]{2,1,0:T(8,128)S(1)} %fusion.10) | copy-start | bytes 3145732
  118.0 26.6 %copy-start.5 = (bf16[128,2048]{0,1:T(8,128)(2,1)S(1)}, bf16[128,2048]{0,1:T(8,128)(2,1)}, u32[]{:S(2)}) copy-start(bf16[128,2048]{0,1:T(8,128)(2,1)} %copy.65) | copy-start | bytes 1572868
  118.0 26.6 %copy-start.20 = (f32[2048]{0:T(1024)S(1)}, f32[2048]{0:T(1024)}, u32[]{:S(2)}) copy-start(f32[2048]{0:T(1024)} %param.15) | copy-start | bytes 24580
  144.6 1.0 copy-start.2
  159.7 87.6 %collective-permute-start.2 = (bf16[128,2048]{0,1:T(8,128)(2,1)}, bf16[128,2048]{0,1:T(8,128)(2,1)}, u32[]{:S(2)}, u32[]{:S(2)}) collective-permute-start(bf16[128,2048]{0,1:T(8,128)(2,1)} %get-tuple-element.134), channel_id=1, source_target_pairs={{0,4},{4,8},{8,12},{12,16},{16,20},{20,24},{24,28},{28,32},{32,36}... | collective-permute-start | bytes 1572872 | tf_op jit(solution)/shard_map/ppermute | solution.py:14
  161.6 85.6 %collective-permute-start.1 = (bf16[128,2048]{0,1:T(8,128)(2,1)}, bf16[128,2048]{0,1:T(8,128)(2,1)}, u32[]{:S(2)}, u32[]{:S(2)}) collective-permute-start(bf16[128,2048]{0,1:T(8,128)(2,1)} %get-tuple-element.134), channel_id=1, source_target_pairs={{0,8},{4,12},{8,16},{12,20},{16,24},{20,28},{24,32},{28,36},{32,40... | collective-permute-start | bytes 1572872 | tf_op jit(solution)/shard_map/ppermute | solution.py:14
  164.9 74.2 %collective-permute-start.9 = (bf16[127,2048]{0,1:T(8,128)(2,1)}, bf16[127,2048]{0,1:T(8,128)(2,1)}, u32[]{:S(2)}, u32[]{:S(2)}) collective-permute-start(bf16[127,2048]{0,1:T(8,128)(2,1)} %bitcast.150), channel_id=1, source_target_pairs={{4,0},{8,4},{12,8},{16,12},{20,16},{24,20},{28,24},{32,28},{36,32}... | collective-permute-start | bytes 1560584 | tf_op jit(solution)/shard_map/ppermute | solution.py:14
  247.2 2.8 copy-start.13
  248.9 1.2 copy-start.3
  258.9 9.2 %copy-start.9 = (bf16[128,2048]{0,1:T(8,128)(2,1)S(1)}, bf16[128,2048]{0,1:T(8,128)(2,1)}, u32[]{:S(2)}) copy-start(bf16[128,2048]{0,1:T(8,128)(2,1)} %copy-done.8) | copy-start | bytes 1572868
  258.9 9.2 %copy-start.11 = (bf16[128,2048]{0,1:T(8,128)(2,1)S(1)}, bf16[128,2048]{0,1:T(8,128)(2,1)}, u32[]{:S(2)}) copy-start(bf16[128,2048]{0,1:T(8,128)(2,1)} %copy-done.10) | copy-start | bytes 1572868
  258.9 9.2 %copy-start.14 = (f32[128,16,128]{2,1,0:T(8,128)S(1)}, f32[128,16,128]{2,1,0:T(8,128)}, u32[]{:S(2)}) copy-start(f32[128,16,128]{2,1,0:T(8,128)} %fusion.8) | copy-start | bytes 3145732
  262.3 26.7 %collective-permute-start.6 = (f32[128,16,128]{0,2,1:T(8,128)}, f32[128,16,128]{0,2,1:T(8,128)}, u32[]{:S(2)}, u32[]{:S(2)}) collective-permute-start(f32[128,16,128]{0,2,1:T(8,128)} %get-tuple-element.129), channel_id=1, source_target_pairs={{8,0},{12,4},{16,8},{20,12},{24,16},{28,20},{32,24},{36,28},{40,32... | collective-permute-start | bytes 3145736 | tf_op jit(solution)/shard_map/ppermute | solution.py:14
  265.9 33.6 %collective-permute-start.5 = (f32[128,16,128]{0,2,1:T(8,128)}, f32[128,16,128]{0,2,1:T(8,128)}, u32[]{:S(2)}, u32[]{:S(2)}) collective-permute-start(f32[128,16,128]{0,2,1:T(8,128)} %get-tuple-element.128), channel_id=1, source_target_pairs={{4,0},{8,4},{12,8},{16,12},{20,16},{24,20},{28,24},{32,28},{36,32}... | collective-permute-start | bytes 3145736 | tf_op jit(solution)/shard_map/ppermute | solution.py:14
Sparse Core Ops, SparseCore 0:
  239.2 169.2 all-reduce.5
where the time goes:
time: 421 us; the launch traced here: 417 us
  local copies, waits for them, and re-layouts  155 us (37%)
  waiting for transfers between devices  145 us (34%)
  matrix products  35.9 us (9%)
  starting transfers between devices  33.1 us (8%)
  other arithmetic  21.9 us (5%)
  between operations  14.6 us (3%)
  blocking collectives  10.7 us (3%)
    psum x1, waiting for transfers between devices, body(): grad_filters = lax.psum(local_filters, ('context', 'mirror'))  106 us
    ppermute x10, waiting for transfers between devices, passed_along(): return lax.ppermute(block, axis, route)  39.2 us
    another operation x4, local copies, waits for them, and re-layouts, banded(): jnp.tile(band_table, (1, row_count + 1))[:, :row_count * col_count]  35.4 us
    ppermute x10, starting transfers between devices, passed_along(): return lax.ppermute(block, axis, route)  33.1 us
    reshape x4, local copies, waits for them, and re-layouts, filter_block(): flattened.reshape(block_size, tok_rows, pad_rows + 1)[:, :, :tap_count]  31.8 us
    reshape x2, local copies, waits for them, and re-layouts, banded(): return repeated.reshape(band_table.shape[0], row_count, col_count)  25 us
    unnamed x61, local copies, waits for them, and re-layouts  20.7 us
    slice x2, local copies, waits for them, and re-layouts, banded(): jnp.tile(band_table, (1, row_count + 1))[:, :row_count * col_count]  14.1 us
  transfers between devices with their start and end apart: 11, of which 5 were waited for; matrix products, arithmetic and copies ran while one was open for 49% of the time, Pallas kernels for 0%

commit v1 on v0

v1 whole, which is shorter than its diff:
```python
import functools

import jax
import jax.numpy as jnp
from jax import lax
from jax.experimental import pallas as pl
from jax.experimental.pallas import tpu as pltpu
from jax.sharding import PartitionSpec as P

HEAD = 128
D = 8192
T = 128
LANES = 128
GROUP = 16
F32 = jnp.float32
BF16 = jnp.bfloat16
SEQ_AXES = ("context", "mirror")

VMEM = pl.BlockSpec(memory_space=pltpu.VMEM)
SMEM = pl.BlockSpec(memory_space=pltpu.SMEM)


def shifted(block, distance):
    count = lax.axis_size(SEQ_AXES)
    route = [(i - distance, i) for i in range(count) if 0 <= i - distance < count]
    return lax.ppermute(block, SEQ_AXES, route)


def across(block, distance):
    count = lax.axis_size("tensor")
    return lax.ppermute(block, "tensor", [(i, (i + distance) % count) for i in range(count)])


def call(body, ins, outs, flops, scratch=(), exps=0):
    nbytes = sum(a.size * a.dtype.itemsize for a in ins)
    nbytes += sum(o.size * o.dtype.itemsize for o in outs)
    specs = [SMEM if a.dtype == jnp.int32 else VMEM for a in ins]
    return pl.pallas_call(
        body,
        out_shape=tuple(outs),
        in_specs=specs,
        out_specs=tuple(VMEM for _ in outs),
        scratch_shapes=list(scratch),
        cost_estimate=pl.CostEstimate(flops=flops, bytes_accessed=nbytes, transcendentals=exps),
    )(*ins)


def sds(*shape, dtype=F32):
    return jax.ShapeDtypeStruct(shape, dtype)


def doc_of(info, pos):
    doc = (pos >= info[0]).astype(jnp.int32)
    for i in range(1, 4):
        doc = doc + (pos >= info[i]).astype(jnp.int32)
    return doc


def conv_mask(info, first, sign=1):
    rows = info[4] + lax.broadcasted_iota(jnp.int32, (T, 2 * T), 0)
    cols = first + sign * lax.broadcasted_iota(jnp.int32, (T, 2 * T), 1)
    return doc_of(info, rows) == doc_of(info, cols)


def column(row):
    return jnp.transpose(jnp.broadcast_to(row, (T, LANES)))


def banded_matmul(table_ref, mask, window, tile):
    bands = []
    for g in range(LANES // GROUP):
        row = table_ref[pl.ds(tile * 8 + g, 1), :]
        band = pltpu.roll(jnp.broadcast_to(row, (T, 2 * T)), 0, 1, stride=1, stride_axis=0)
        bands.append(jnp.where(mask, band, 0.0).astype(BF16))
    stacked = jnp.concatenate(bands, axis=0)
    full = jnp.dot(stacked, window, preferred_element_type=F32)
    lane_group = lax.broadcasted_iota(jnp.int32, (T, LANES), 1) // GROUP
    out = full[:T]
    for g in range(1, LANES // GROUP):
        out = jnp.where(lane_group == g, full[g * T : (g + 1) * T], out)
    return out


def lanes_of(tile):
    return pl.ds(pl.multiple_of(tile * LANES, LANES), LANES)


def conv_body(info, left, kv, hyena_q, table, signal, square, flipped):
    span = 2 * T
    turned = lax.broadcasted_iota(jnp.int32, (span, span), 0) + lax.broadcasted_iota(
        jnp.int32, (span, span), 1
    )
    turn = jnp.where(turned == span - 1, 1.0, 0.0).astype(BF16)
    mask = conv_mask(info, info[4] - T)
    tiles = kv.shape[1] // LANES

    def step(tile, acc):
        at = lanes_of(tile)
        window = jnp.concatenate([left[:, at], kv[:, at]], axis=0)
        out = banded_matmul(table, mask, window, tile)
        signal[:, at] = out
        flipped[:, at] = jnp.dot(turn, window, preferred_element_type=F32).astype(BF16)
        mix = hyena_q[:, at].astype(F32) * out
        return acc + mix * mix

    acc = lax.fori_loop(0, tiles, step, jnp.zeros((T, LANES), F32))
    square[...] = jnp.broadcast_to(jnp.sum(jnp.transpose(acc), axis=0, keepdims=True), (8, LANES))


def inv_rms_row(squares):
    total = squares[0][0:1, :]
    for s in squares[1:]:
        total = total + s[0:1, :]
    return lax.rsqrt(total / D + 1e-06)


def values_body(signal, hyena_q, gain, s0, s1, s2, s3, values):
    inv = column(inv_rms_row((s0, s1, s2, s3)))

    def step(tile, _):
        at = lanes_of(tile)
        mix = hyena_q[:, at].astype(F32) * signal[:, at]
        values[:, at] = (mix * inv * gain[:, at]).astype(BF16)
        return 0

    lax.fori_loop(0, signal.shape[1] // LANES, step, 0)


def scores_body(info, q, k0, k1, k2, og, prob, own, part1, part2):
    span = 3 * T
    query_pos = info[4] + lax.broadcasted_iota(jnp.int32, (span, T), 1)
    key_pos = info[4] - 2 * T + lax.broadcasted_iota(jnp.int32, (span, T), 0)
    allowed = (
        (key_pos >= 0)
        & (key_pos <= query_pos)
        & (query_pos - key_pos <= 2 * T)
        & (doc_of(info, key_pos) == doc_of(info, query_pos))
    )
    scale = HEAD**-0.5

    def step(h, _):
        at = lanes_of(h)
        keys = jnp.concatenate([k2[:, at], k1[:, at], k0[:, at]], axis=0)
        s = lax.dot_general(keys, q[:, at], (((1,), (1,)), ((), ())), preferred_element_type=F32)
        s = jnp.where(allowed, s * scale, -1e30)
        top = jnp.max(s, axis=0, keepdims=True)
        e = jnp.exp(s - top)
        p = e * (1.0 / jnp.sum(e, axis=0, keepdims=True))
        prob[h] = p
        part = jnp.dot(p.astype(BF16), og[:, at], preferred_element_type=F32)
        part2[:, at] = part[:T].astype(BF16)
        part1[:, at] = part[T : 2 * T].astype(BF16)
        own[:, at] = part[2 * T :]
        return 0

    lax.fori_loop(0, q.shape[1] // HEAD, step, 0)


def inner_body(own, part1, part2, signal, hyena_q, gain, grad_values, inner):
    def step(tile, acc):
        at = lanes_of(tile)
        gv = own[:, at] + part1[:, at].astype(F32) + part2[:, at].astype(F32)
        gv = gv * gain[:, at]
        grad_values[:, at] = gv
        return acc + gv * (hyena_q[:, at].astype(F32) * signal[:, at])

    acc = lax.fori_loop(0, own.shape[1] // LANES, step, jnp.zeros((T, LANES), F32))
    inner[...] = jnp.broadcast_to(jnp.sum(jnp.transpose(acc), axis=0, keepdims=True), (8, LANES))


def signal_grad_body(
    grad_values, signal, hyena_q, s0, s1, s2, s3, i0, i1, i2, i3, grad_hyena_q, grad_signal
):
    inv_row = inv_rms_row((s0, s1, s2, s3))
    inner = i0[0:1, :] + i1[0:1, :] + i2[0:1, :] + i3[0:1, :]
    inv = column(inv_row)
    drop = column(inner * inv_row * inv_row / D)

    def step(tile, _):
        at = lanes_of(tile)
        sig = signal[:, at]
        hq = hyena_q[:, at].astype(F32)
        grad_mix = inv * (grad_values[:, at] - hq * sig * drop)
        grad_hyena_q[:, at] = (grad_mix * sig).astype(BF16)
        grad_signal[:, at] = (grad_mix * hq).astype(BF16)
        return 0

    lax.fori_loop(0, signal.shape[1] // LANES, step, 0)


def filter_body(info, flipped, grad_signal, out):
    mask = conv_mask(info, info[4] + T - 1, -1)
    lane_group = lax.broadcasted_iota(jnp.int32, (T, LANES), 1) // GROUP
    count = LANES // GROUP

    def step(tile, _):
        at = lanes_of(tile)
        gs = grad_signal[:, at].astype(F32)
        stacked = jnp.concatenate(
            [jnp.where(lane_group == g, gs, 0.0).astype(BF16) for g in range(count)], axis=0
        )
        full = lax.dot_general(
            stacked, flipped[:, at], (((1,), (1,)), ((), ())), preferred_element_type=F32
        )
        rows = []
        for g in range(count):
            corr = jnp.where(mask, full[g * T : (g + 1) * T], 0.0)
            aligned = pltpu.roll(corr, T + 1, 1, stride=1, stride_axis=0)
            rows.append(jnp.sum(aligned[:, :LANES], axis=0, keepdims=True))
        out[pl.ds(pl.multiple_of(tile * 8, 8), 8), :] = jnp.concatenate(rows, axis=0)
        return 0

    lax.fori_loop(0, grad_signal.shape[1] // LANES, step, 0)


def conv_back_body(info, grad_signal, right, hyena_k, hyena_v, table, grad_k, grad_v):
    mask = conv_mask(info, info[4])

    def step(tile, _):
        at = lanes_of(tile)
        window = jnp.concatenate([grad_signal[:, at], right[:, at]], axis=0)
        grad_kv = banded_matmul(table, mask, window, tile)
        grad_k[:, at] = (grad_kv * hyena_v[:, at].astype(F32)).astype(BF16)
        grad_v[:, at] = (grad_kv * hyena_k[:, at].astype(F32)).astype(BF16)
        return 0

    lax.fori_loop(0, hyena_k.shape[1] // LANES, step, 0)


def attend_body(
    prob, q, k0, k1, k2, v0, v1, v2, og, attn_out, grad_q, own, part1, part2
):
    scale = HEAD**-0.5
    over_keys = (((0,), (0,)), ((), ()))

    def step(h, _):
        at = lanes_of(h)
        keys = jnp.concatenate([k2[:, at], k1[:, at], k0[:, at]], axis=0)
        vals = jnp.concatenate([v2[:, at], v1[:, at], v0[:, at]], axis=0)
        p = prob[h]
        gp = lax.dot_general(vals, og[:, at], (((1,), (1,)), ((), ())), preferred_element_type=F32)
        delta = jnp.sum(p * gp, axis=0, keepdims=True)
        gs = (p * (gp - delta) * scale).astype(BF16)
        attn_out[:, at] = lax.dot_general(
            p.astype(BF16), vals, over_keys, preferred_element_type=F32
        ).astype(BF16)
        grad_q[:, at] = lax.dot_general(
            gs, keys, over_keys, preferred_element_type=F32
        ).astype(BF16)
        part = jnp.dot(gs, q[:, at], preferred_element_type=F32)
        part2[:, at] = part[:T].astype(BF16)
        part1[:, at] = part[T : 2 * T].astype(BF16)
        own[:, at] = part[2 * T :]
        return 0

    lax.fori_loop(0, q.shape[1] // HEAD, step, 0)


def over_sequence(x):
    def route(f):
        return [(i, f(i // 8, i % 8)) for i in range(32)]

    x = x + lax.ppermute(x, "mirror", [(0, 1), (1, 0)])
    x = x + sum(
        lax.ppermute(x, "context", route(lambda a, b, d=d: ((a + d) % 4) * 8 + b))
        for d in (1, 2, 3)
    )
    x = x + lax.ppermute(x, "context", route(lambda a, b: a * 8 + (b ^ 4)))
    return x + sum(
        lax.ppermute(x, "context", route(lambda a, b, d=d: a * 8 + (b ^ d))) for d in (1, 2, 3)
    )


def body(hyena_q, hyena_k, hyena_v, filters, norm_gain, attn_q, attn_k, out_grad, doc_lengths):
    rows, channels = hyena_q.shape
    heads = channels // HEAD
    big = (rows, channels)
    band_flops = 2 * (channels // GROUP) * T * 2 * T * LANES
    attn_flops = 2 * heads * 3 * T * T * HEAD
    offset = lax.axis_index(SEQ_AXES) * rows
    ends = [doc_lengths[0]]
    for i in range(1, 4):
        ends.append(ends[-1] + doc_lengths[i])
    info = jnp.stack(ends + [offset.astype(jnp.int32)])
    gain = norm_gain[None, :]

    kv = (hyena_k.astype(F32) * hyena_v.astype(F32)).astype(BF16)
    left = shifted(kv, 1)
    k1 = shifted(attn_k, 1)
    k2 = shifted(attn_k, 2)
    groups = filters.shape[0]
    wide = filters.astype(F32)
    back_table = jnp.concatenate([wide, jnp.zeros((groups, T), F32)], axis=1)
    fwd_table = jnp.concatenate(
        [jnp.zeros((groups, 1), F32), wide[:, ::-1], jnp.zeros((groups, T - 1), F32)], axis=1
    )
    signal, square, flipped = call(
        conv_body,
        (info, left, kv, hyena_q, fwd_table),
        (sds(*big), sds(8, LANES), sds(2 * rows, channels, dtype=BF16)),
        band_flops,
    )
    squares = [square] + [across(square, d) for d in (1, 2, 3)]
    (values,) = call(
        values_body,
        (signal, hyena_q, gain, *squares),
        (sds(*big, dtype=BF16),),
        4 * rows * channels,
    )
    prob, value_own, value1, value2 = call(
        scores_body,
        (info, attn_q, attn_k, k1, k2, out_grad),
        (sds(heads, 3 * T, T), sds(*big), sds(*big, dtype=BF16), sds(*big, dtype=BF16)),
        2 * attn_flops,
        exps=heads * 3 * T * T,
    )
    v1 = shifted(values, 1)
    v2 = shifted(values, 2)
    back1 = shifted(value1, -1)
    back2 = shifted(value2, -2)
    gain_grad, inner = call(
        inner_body,
        (value_own, back1, back2, signal, hyena_q, gain),
        (sds(*big), sds(8, LANES)),
        6 * rows * channels,
    )
    inners = [inner] + [across(inner, d) for d in (1, 2, 3)]
    grad_hyena_q, grad_signal = call(
        signal_grad_body,
        (gain_grad, signal, hyena_q, *squares, *inners),
        (sds(*big, dtype=BF16), sds(*big, dtype=BF16)),
        8 * rows * channels,
    )
    right = shifted(grad_signal, -1)
    (local,) = call(
        filter_body, (info, flipped, grad_signal), (sds(groups, LANES),), band_flops
    )
    grad_filters = over_sequence(local)
    attn_out, grad_attn_q, key_own, key1, key2 = call(
        attend_body,
        (prob, attn_q, attn_k, k1, k2, values, v1, v2, out_grad),
        (
            sds(*big, dtype=BF16),
            sds(*big, dtype=BF16),
            sds(*big),
            sds(*big, dtype=BF16),
            sds(*big, dtype=BF16),
        ),
        4 * attn_flops,
    )
    grad_attn_k = (
        key_own + shifted(key1, -1).astype(F32) + shifted(key2, -2).astype(F32)
    ).astype(BF16)
    grad_hyena_k, grad_hyena_v = call(
        conv_back_body,
        (info, grad_signal, right, hyena_k, hyena_v, back_table),
        (sds(*big, dtype=BF16), sds(*big, dtype=BF16)),
        band_flops,
    )
    return (
        attn_out,
        grad_attn_q,
        grad_attn_k,
        grad_hyena_q,
        grad_hyena_k,
        grad_hyena_v,
        grad_filters,
    )


def solution(mesh):
    tokens = P(SEQ_AXES, "tensor")
    return jax.shard_map(
        body,
        mesh=mesh,
        in_specs=(
            tokens,
            tokens,
            tokens,
            P("tensor", None),
            P("tensor"),
            tokens,
            tokens,
            tokens,
            P(),
        ),
        out_specs=(tokens, tokens, tokens, tokens, tokens, tokens, P("tensor", None)),
        check_vma=False,
    )
```

time: 421 us -> 168 us (0.40)
  local copies, waits for them, and re-layouts: 155 us -> 8.95 us
  waiting for transfers between devices: 145 us -> 36.5 us
  Pallas kernels: 0 us -> 61.4 us
  matrix products: 35.9 us -> 0 us
  starting transfers between devices: 33.1 us -> 52.5 us
  other arithmetic: 21.9 us -> 4.6 us
  between operations: 14.6 us -> 3.48 us
  blocking collectives: 10.7 us -> 0 us
    psum x1 -> x0, waiting for transfers between devices: 106 us -> none  [body(): grad_filters = lax.psum(local_filters, ('context', 'mirror'))]
    pallas_call x0 -> x8, Pallas kernels: none -> 61.4 us  [call(): pl.pallas_call(body, out_shape=tuple(outs), in_specs=specs, out_specs=tup...]
    reshape x8 -> x0, local copies, waits for them, and re-layouts: 58.8 us -> none  [the longest x4 31.8 us: filter_block(): flattened.reshape(block_size, tok_rows, pad_rows + 1)[:, :, :tap_count]]
    dot_general x12 -> x0, matrix products: 35.9 us -> none  [the longest x4 7.11 us: filter_block(): jnp.einsum('tgc,ugc->gtu', grad_block, wide_block, preferred_element_type...]
    another operation x4 -> x1, local copies, waits for them, and re-layouts: 35.4 us -> 1.22 us  [body(): info = jnp.stack(ends + [offset.astype(jnp.int32)])]
    ppermute x10 -> x24, starting transfers between devices: 33.1 us -> 52.5 us  [the longest x10 30.9 us: shifted(): return lax.ppermute(block, SEQ_AXES, route)]
    slice x5 -> x1, local copies, waits for them, and re-layouts: 18.7 us -> 1.4 us  [body(): ends.append(ends[-1] + doc_lengths[i])]
    unnamed x61 -> x36, local copies, waits for them, and re-layouts: 20.7 us -> 5.49 us
  transfers between devices with their start and end apart: 11 -> 24, of which waited for: 5 -> 12; matrix products, arithmetic and copies ran while one was open for 49% -> 4% of each run, Pallas kernels for 0% -> 37%
where the time goes in v1:
time: 168 us; the launch traced here: 167 us
  Pallas kernels  61.4 us (37%)
  starting transfers between devices  52.5 us (31%)
  waiting for transfers between devices  36.5 us (22%)
  local copies, waits for them, and re-layouts  8.95 us (5%)
  other arithmetic  4.6 us (3%)
  between operations  3.48 us (2%)
    pallas_call x8, Pallas kernels, call(): pl.pallas_call(body, out_shape=tuple(outs), in_specs=specs, out_specs=tup...  61.4 us
    ppermute x10, starting transfers between devices, shifted(): return lax.ppermute(block, SEQ_AXES, route)  30.9 us
    ppermute x3, waiting for transfers between devices, over_sequence(): lax.ppermute(x, 'context', route(lambda a, b, d=d: a * 8 + (b ^ d)))  19.5 us
    ppermute x6, starting transfers between devices, across(): lax.ppermute(block, 'tensor', [(i, (i + distance) % count) for i in range...  9.96 us
    ppermute x10, waiting for transfers between devices, shifted(): return lax.ppermute(block, SEQ_AXES, route)  6.96 us
    ppermute x3, starting transfers between devices, over_sequence(): lax.ppermute(x, 'context', route(lambda a, b, d=d: a * 8 + (b ^ d)))  6.19 us
    ppermute x6, waiting for transfers between devices, across(): lax.ppermute(block, 'tensor', [(i, (i + distance) % count) for i in range...  6.15 us
    unnamed x36, local copies, waits for them, and re-layouts  5.49 us
  transfers between devices with their start and end apart: 24, of which 12 were waited for; matrix products, arithmetic and copies ran while one was open for 4% of the time, Pallas kernels for 37%

profile of v1, /device:TPU:6, one launch (start us, length us, event | category | flops | bytes accessed | tf_op | source)
XLA Modules:
  0.0 167.5 jit_solution(5004937497569072454)
XLA Ops:
  0.6 1.9 %collective-permute-start = (bf16[128,2048]{1,0:T(8,128)(2,1)}, bf16[128,2048]{1,0:T(8,128)(2,1)S(1)}, u32[]{:S(2)}, u32[]{:S(2)}) collective-permute-start(bf16[128,2048]{1,0:T(8,128)(2,1)} %k0.3), channel_id=1, source_target_pairs={{0,4},{4,8},{8,12},{12,16},{16,20},{20,24},{24,28},{28,32},{32,36}... | collective-permute-start | bytes 1572872 | tf_op jit(solution)/shard_map/ppermute | solution.py:26
  2.6 3.8 %collective-permute-start.1 = (bf16[128,2048]{1,0:T(8,128)(2,1)}, bf16[128,2048]{1,0:T(8,128)(2,1)S(1)}, u32[]{:S(2)}, u32[]{:S(2)}) collective-permute-start(bf16[128,2048]{1,0:T(8,128)(2,1)} %k0.3), channel_id=1, source_target_pairs={{0,8},{4,12},{8,16},{12,20},{16,24},{20,28},{24,32},{28,36},{32,40... | collective-permute-start | bytes 1572872 | tf_op jit(solution)/shard_map/ppermute | solution.py:26
  6.4 1.3 multiply_convert_fusion.kv
  7.7 0.0 copy-start.5
  7.8 3.6 %collective-permute-start.2 = (bf16[128,2048]{1,0:T(8,128)(2,1)S(1)}, bf16[128,2048]{1,0:T(8,128)(2,1)S(1)}, u32[]{:S(2)}, u32[]{:S(2)}) collective-permute-start(bf16[128,2048]{1,0:T(8,128)(2,1)S(1)} %multiply_convert_fusion.kv), channel_id=1, source_target_pairs={{0,4},{4,8},{8,12},{12,16},{16,20},{20,24},{24,28},{28,32},{32,36}... | collective-permute-start | bytes 1572872 | tf_op jit(solution)/shard_map/ppermute | solution.py:26
  11.4 1.4 fusion
  15.4 1.2 stack.10.info
  16.6 1.4 collective-permute-done.k1
  18.0 5.6 %collective-permute-done.1.k2 = bf16[128,2048]{1,0:T(8,128)(2,1)S(1)} collective-permute-done((bf16[128,2048]{1,0:T(8,128)(2,1)}, bf16[128,2048]{1,0:T(8,128)(2,1)S(1)}, u32[]{:S(2)}, u32[]{:S(2)}) %collective-permute-start.1) | collective-permute-done | bytes 524320 | tf_op jit(solution)/shard_map/ppermute | solution.py:26
  23.6 0.8 copy-done.1
  24.4 11.4 %shard_map.144 = (f32[16,384,128]{2,1,0:T(8,128)}, f32[128,2048]{1,0:T(8,128)}, bf16[128,2048]{1,0:T(8,128)(2,1)}, bf16[128,2048]{1,0:T(8,128)(2,1)}) custom-call(s32[5]{0:T(128)} %stack.10.info, bf16[128,2048]{1,0:T(8,128)(2,1)} %q.3, bf16[128,2048]{1,0:T(8,128)(2,1)} %k0.3, bf16[128,2048]{1,0:T(8,128)(2,1)} %copy-done, bf16[128,2048]{1,0:T(8,128)(2,1)} %copy-done.1, ...), custom_call_target="tpu_custom_call" | custom-call | flops 402653184 | bytes 7864340 | tf_op jit(solution)/shard_map/pallas_call | solution.py:38
  35.8 6.4 %collective-permute-start.10 = (bf16[128,2048]{1,0:T(8,128)(2,1)}, bf16[128,2048]{1,0:T(8,128)(2,1)S(1)}, u32[]{:S(2)}, u32[]{:S(2)}) collective-permute-start(bf16[128,2048]{1,0:T(8,128)(2,1)} %get-tuple-element.34), channel_id=1, source_target_pairs={{4,0},{8,4},{12,8},{16,12},{20,16},{24,20},{28,24},{32,28},{36,32}... | collective-permute-start | bytes 1572872 | tf_op jit(solution)/shard_map/ppermute | solution.py:26
  42.2 2.9 %collective-permute-start.11 = (bf16[128,2048]{1,0:T(8,128)(2,1)}, bf16[128,2048]{1,0:T(8,128)(2,1)S(1)}, u32[]{:S(2)}, u32[]{:S(2)}) collective-permute-start(bf16[128,2048]{1,0:T(8,128)(2,1)} %get-tuple-element.35), channel_id=1, source_target_pairs={{8,0},{12,4},{16,8},{20,12},{24,16},{28,20},{32,24},{36,28},{40,32... | collective-permute-start | bytes 1572872 | tf_op jit(solution)/shard_map/ppermute | solution.py:26
  45.2 0.1 rev.3
  45.3 0.1 pad.3.clone
  45.4 0.8 maximum_maximum_fusion.table
  46.1 0.8 copy-done.17
  46.9 9.0 %shard_map.145 = (f32[128,2048]{1,0:T(8,128)}, f32[8,128]{1,0:T(8,128)}, bf16[256,2048]{1,0:T(8,128)(2,1)}) custom-call(s32[5]{0:T(128)} %stack.10.info, bf16[128,2048]{1,0:T(8,128)(2,1)} %copy-done.17, bf16[128,2048]{1,0:T(8,128)(2,1)} %copy-done.5, bf16[128,2048]{1,0:T(8,128)(2,1)} %hyena_q.7, f32[128,256]{1,0:T(8,128)} %maximum_maximum_fusion.table), custom_call_target="tpu_custom_call" | custom-call | flops 1073741824 | bytes 3805204 | tf_op jit(solution)/shard_map/pallas_call | solution.py:38
  55.9 1.6 collective-permute-start.3
  57.5 2.9 %collective-permute-start.4 = (f32[8,128]{1,0:T(8,128)}, f32[8,128]{1,0:T(8,128)S(1)}, u32[]{:S(2)}, u32[]{:S(2)}) collective-permute-start(f32[8,128]{1,0:T(8,128)} %get-tuple-element.27.s0), channel_id=1, source_target_pairs={{0,2},{1,3},{2,0},{3,1},{4,6},{5,7},{6,4},{7,5},{8,10},{9,11},{10,... | collective-permute-start | bytes 12296 | tf_op jit(solution)/shard_map/ppermute | solution.py:31
  60.4 1.3 collective-permute-start.5
  61.7 1.1 collective-permute-done.4.s2
  62.8 1.4 collective-permute-done.5.s3
  64.2 0.6 copy-done.11
  64.8 2.8 %shard_map.146.v0 = bf16[128,2048]{1,0:T(8,128)(2,1)} custom-call(f32[128,2048]{1,0:T(8,128)} %get-tuple-element.26.signal, bf16[128,2048]{1,0:T(8,128)(2,1)} %hyena_q.7, f32[1,2048]{1,0:T(1,128)} %bitcast.3, f32[8,128]{1,0:T(8,128)} %get-tuple-element.27.s0, f32[8,128]{1,0:T(8,128)} %copy-done.9, f32[8,128]{1,0:T(8,128)} %copy-done.10, f32[8,128]{1,0:T(8,128)} %copy-done.11), custom_call_target="tpu_custom_call" | custom-call | flops 1048576 | bytes 2121728 | tf_op jit(solution)/shard_map/pallas_call | solution.py:38
  67.5 1.9 %collective-permute-start.6 = (bf16[128,2048]{1,0:T(8,128)(2,1)}, bf16[128,2048]{1,0:T(8,128)(2,1)S(1)}, u32[]{:S(2)}, u32[]{:S(2)}) collective-permute-start(bf16[128,2048]{1,0:T(8,128)(2,1)} %shard_map.146.v0), channel_id=1, source_target_pairs={{0,4},{4,8},{8,12},{12,16},{16,20},{20,24},{24,28},{28,32},{32,36}... | collective-permute-start | bytes 1572872 | tf_op jit(solution)/shard_map/ppermute | solution.py:26
  69.5 2.9 %collective-permute-start.7 = (bf16[128,2048]{1,0:T(8,128)(2,1)}, bf16[128,2048]{1,0:T(8,128)(2,1)S(1)}, u32[]{:S(2)}, u32[]{:S(2)}) collective-permute-start(bf16[128,2048]{1,0:T(8,128)(2,1)} %shard_map.146.v0), channel_id=1, source_target_pairs={{0,8},{4,12},{8,16},{12,20},{16,24},{20,28},{24,32},{28,36},{32,40... | collective-permute-start | bytes 1572872 | tf_op jit(solution)/shard_map/ppermute | solution.py:26
  72.4 0.0 copy-start.6
  72.4 0.0 copy-start.7
  72.4 0.8 copy-done.6
  73.2 0.2 copy-done.7
  73.4 3.8 %shard_map.148 = (f32[128,2048]{1,0:T(8,128)}, f32[8,128]{1,0:T(8,128)}) custom-call(f32[128,2048]{1,0:T(8,128)} %get-tuple-element.33.own, bf16[128,2048]{1,0:T(8,128)(2,1)} %copy-done.6, bf16[128,2048]{1,0:T(8,128)(2,1)} %copy-done.7, f32[128,2048]{1,0:T(8,128)} %get-tuple-element.26.signal, bf16[128,2048]{1,0:T(8,128)(2,1)} %hyena_q.7, f32[1,2048]{1,0:T(1,128)} %bitcast.4), custom_call_target="tpu_custom_call" | custom-call | flops 1572864 | bytes 4730880 | tf_op jit(solution)/shard_map/pallas_call | solution.py:38
  77.1 0.2 collective-permute-start.12
  77.3 3.8 %collective-permute-start.13 = (f32[8,128]{1,0:T(8,128)}, f32[8,128]{1,0:T(8,128)S(1)}, u32[]{:S(2)}, u32[]{:S(2)}) collective-permute-start(f32[8,128]{1,0:T(8,128)} %get-tuple-element.37.i0), channel_id=1, source_target_pairs={{0,2},{1,3},{2,0},{3,1},{4,6},{5,7},{6,4},{7,5},{8,10},{9,11},{10,... | collective-permute-start | bytes 12296 | tf_op jit(solution)/shard_map/ppermute | solution.py:31
  81.2 0.1 collective-permute-start.14
  81.3 0.9 collective-permute-done.12.i1
  82.2 0.8 collective-permute-done.13.i2
  83.0 2.0 %collective-permute-done.14.i3 = f32[8,128]{1,0:T(8,128)S(1)} collective-permute-done((f32[8,128]{1,0:T(8,128)}, f32[8,128]{1,0:T(8,128)S(1)}, u32[]{:S(2)}, u32[]{:S(2)}) %collective-permute-start.14) | collective-permute-done | bytes 4128 | tf_op jit(solution)/shard_map/ppermute | solution.py:31
  85.0 0.6 copy-done.14
  85.6 3.5 %shard_map.149 = (bf16[128,2048]{1,0:T(8,128)(2,1)}, bf16[128,2048]{1,0:T(8,128)(2,1)}) custom-call(f32[128,2048]{1,0:T(8,128)} %get-tuple-element.36.grad_values, f32[128,2048]{1,0:T(8,128)} %get-tuple-element.26.signal, bf16[128,2048]{1,0:T(8,128)(2,1)} %hyena_q.7, f32[8,128]{1,0:T(8,128)} %get-tuple-element.27.s0, f32[8,128]{1,0:T(8,128)} %copy-done.9, ...), custom_call_target="tpu_custom_call" | custom-call | flops 2097152 | bytes 3702784 | tf_op jit(solution)/shard_map/pallas_call | solution.py:38
  89.1 10.5 %shard_map.151 = f32[128,128]{1,0:T(8,128)} custom-call(s32[5]{0:T(128)} %stack.10.info, bf16[256,2048]{1,0:T(8,128)(2,1)} %get-tuple-element.42.flipped, bf16[128,2048]{1,0:T(8,128)(2,1)} %get-tuple-element.39.grad_signal), custom_call_target="tpu_custom_call" | custom-call | flops 1073741824 | bytes 1638420 | tf_op jit(solution)/shard_map/pallas_call | solution.py:38
  99.6 1.5 collective-permute-done.16
  101.0 0.8 add.53
  101.9 0.1 collective-permute-start.17
  102.0 2.6 %collective-permute-start.18 = (f32[128,128]{1,0:T(8,128)S(1)}, f32[128,128]{1,0:T(8,128)S(1)}, u32[]{:S(2)}, u32[]{:S(2)}) collective-permute-start(f32[128,128]{1,0:T(8,128)S(1)} %add.53), channel_id=1, source_target_pairs={{0,128},{8,136},{16,144},{24,152},{32,160},{40,168},{48,176},{56,1... | collective-permute-start | bytes 196616 | tf_op jit(solution)/shard_map/ppermute | solution.py:265
  104.6 2.2 %collective-permute-done.17 = f32[128,128]{1,0:T(8,128)S(1)} collective-permute-done((f32[128,128]{1,0:T(8,128)S(1)}, f32[128,128]{1,0:T(8,128)S(1)}, u32[]{:S(2)}, u32[]{:S(2)}) %collective-permute-start.17) | collective-permute-done | bytes 65568 | tf_op jit(solution)/shard_map/ppermute | solution.py:265
  106.8 3.0 %collective-permute-start.15 = (bf16[128,2048]{1,0:T(8,128)(2,1)S(1)}, bf16[128,2048]{1,0:T(8,128)(2,1)S(1)}, u32[]{:S(2)}, u32[]{:S(2)}) collective-permute-start(bf16[128,2048]{1,0:T(8,128)(2,1)S(1)} %copy-done.15), channel_id=1, source_target_pairs={{4,0},{8,4},{12,8},{16,12},{20,16},{24,20},{28,24},{32,28},{36,32}... | collective-permute-start | bytes 1572872 | tf_op jit(solution)/shard_map/ppermute | solution.py:26
  109.8 0.2 collective-permute-done.19
  110.0 2.7 %collective-permute-start.20 = (f32[128,128]{1,0:T(8,128)S(1)}, f32[128,128]{1,0:T(8,128)S(1)}, u32[]{:S(2)}, u32[]{:S(2)}) collective-permute-start(f32[128,128]{1,0:T(8,128)S(1)} %add_add_fusion.1), channel_id=1, source_target_pairs={{0,32},{8,40},{16,48},{24,56},{32,0},{40,8},{48,16},{56,24},{64,96... | collective-permute-start | bytes 196616 | tf_op jit(solution)/shard_map/ppermute | solution.py:268
  112.8 0.8 copy-done.3
  113.6 0.2 copy-done.4
  113.8 12.3 %shard_map.147 = (bf16[128,2048]{1,0:T(8,128)(2,1)}, bf16[128,2048]{1,0:T(8,128)(2,1)}, f32[128,2048]{1,0:T(8,128)}, bf16[128,2048]{1,0:T(8,128)(2,1)}, bf16[128,2048]{1,0:T(8,128)(2,1)}) custom-call(f32[16,384,128]{2,1,0:T(8,128)} %get-tuple-element.25.prob, bf16[128,2048]{1,0:T(8,128)(2,1)} %q.3, bf16[128,2048]{1,0:T(8,128)(2,1)} %k0.3, ...), custom_call_target="tpu_custom_call" | custom-call | flops 805306368 | bytes 10485760 | tf_op jit(solution)/shard_map/pallas_call | solution.py:38
  126.0 2.0 %collective-permute-start.8 = (bf16[128,2048]{1,0:T(8,128)(2,1)}, bf16[128,2048]{1,0:T(8,128)(2,1)S(1)}, u32[]{:S(2)}, u32[]{:S(2)}) collective-permute-start(bf16[128,2048]{1,0:T(8,128)(2,1)} %get-tuple-element.31), channel_id=1, source_target_pairs={{4,0},{8,4},{12,8},{16,12},{20,16},{24,20},{28,24},{32,28},{36,32}... | collective-permute-start | bytes 1572872 | tf_op jit(solution)/shard_map/ppermute | solution.py:26
  128.1 2.3 %collective-permute-start.9 = (bf16[128,2048]{1,0:T(8,128)(2,1)}, bf16[128,2048]{1,0:T(8,128)(2,1)S(1)}, u32[]{:S(2)}, u32[]{:S(2)}) collective-permute-start(bf16[128,2048]{1,0:T(8,128)(2,1)} %get-tuple-element.32), channel_id=1, source_target_pairs={{8,0},{12,4},{16,8},{20,12},{24,16},{28,20},{32,24},{36,28},{40,32... | collective-permute-start | bytes 1572872 | tf_op jit(solution)/shard_map/ppermute | solution.py:26
  130.4 1.8 %collective-permute-start.21 = (f32[128,128]{1,0:T(8,128)S(1)}, f32[128,128]{1,0:T(8,128)S(1)}, u32[]{:S(2)}, u32[]{:S(2)}) collective-permute-start(f32[128,128]{1,0:T(8,128)S(1)} %add.57), channel_id=1, source_target_pairs={{0,8},{8,0},{16,24},{24,16},{32,40},{40,32},{48,56},{56,48},{64,72... | collective-permute-start | bytes 196616 | tf_op jit(solution)/shard_map/ppermute | solution.py:270
  132.2 2.4 %collective-permute-start.22 = (f32[128,128]{1,0:T(8,128)S(1)}, f32[128,128]{1,0:T(8,128)S(1)}, u32[]{:S(2)}, u32[]{:S(2)}) collective-permute-start(f32[128,128]{1,0:T(8,128)S(1)} %add.57), channel_id=1, source_target_pairs={{0,16},{8,24},{16,0},{24,8},{32,48},{40,56},{48,32},{56,40},{64,80... | collective-permute-start | bytes 196616 | tf_op jit(solution)/shard_map/ppermute | solution.py:270
  134.5 16.2 %collective-permute-done.21 = f32[128,128]{1,0:T(8,128)S(1)} collective-permute-done((f32[128,128]{1,0:T(8,128)S(1)}, f32[128,128]{1,0:T(8,128)S(1)}, u32[]{:S(2)}, u32[]{:S(2)}) %collective-permute-start.21) | collective-permute-done | bytes 65568 | tf_op jit(solution)/shard_map/ppermute | solution.py:270
  150.7 2.1 %collective-permute-start.23 = (f32[128,128]{1,0:T(8,128)S(1)}, f32[128,128]{1,0:T(8,128)S(1)}, u32[]{:S(2)}, u32[]{:S(2)}) collective-permute-start(f32[128,128]{1,0:T(8,128)S(1)} %add.57), channel_id=1, source_target_pairs={{0,24},{8,16},{16,8},{24,0},{32,56},{40,48},{48,40},{56,32},{64,88... | collective-permute-start | bytes 196616 | tf_op jit(solution)/shard_map/ppermute | solution.py:270
  152.8 0.7 concatenate.7.table
  153.4 3.3 %collective-permute-done.23 = f32[128,128]{1,0:T(8,128)S(1)} collective-permute-done((f32[128,128]{1,0:T(8,128)S(1)}, f32[128,128]{1,0:T(8,128)S(1)}, u32[]{:S(2)}, u32[]{:S(2)}) %collective-permute-start.23) | collective-permute-done | bytes 65568 | tf_op jit(solution)/shard_map/ppermute | solution.py:270
  156.8 0.6 add_add_fusion
  157.4 0.8 copy-done.16
  158.2 8.2 %shard_map.150 = (bf16[128,2048]{1,0:T(8,128)(2,1)}, bf16[128,2048]{1,0:T(8,128)(2,1)}) custom-call(s32[5]{0:T(128)} %stack.10.info, bf16[128,2048]{1,0:T(8,128)(2,1)} %get-tuple-element.39.grad_signal, bf16[128,2048]{1,0:T(8,128)(2,1)} %copy-done.16, bf16[128,2048]{1,0:T(8,128)(2,1)} %hyena_k.1, bf16[128,2048]{1,0:T(8,128)(2,1)} %hyena_v.1, ...), custom_call_target="tpu_custom_call" | custom-call | flops 1073741824 | bytes 3276820 | tf_op jit(solution)/shard_map/pallas_call | solution.py:38
  166.5 1.0 add_convert_fusion
  (42 shorter events, 0.1 us)
Async XLA Ops:
  0.6 44.5 %copy-start.8 = (bf16[128,128]{1,0:T(8,128)(2,1)S(1)}, bf16[128,128]{1,0:T(8,128)(2,1)}, u32[]{:S(2)}) copy-start(bf16[128,128]{1,0:T(8,128)(2,1)} %param.12) | copy-start | bytes 98308
  0.6 17.4 %collective-permute-start = (bf16[128,2048]{1,0:T(8,128)(2,1)}, bf16[128,2048]{1,0:T(8,128)(2,1)S(1)}, u32[]{:S(2)}, u32[]{:S(2)}) collective-permute-start(bf16[128,2048]{1,0:T(8,128)(2,1)} %k0.3), channel_id=1, source_target_pairs={{0,4},{4,8},{8,12},{12,16},{16,20},{20,24},{24,28},{28,32},{32,36}... | collective-permute-start | bytes 1572872 | tf_op jit(solution)/shard_map/ppermute | solution.py:26
  2.6 21.0 %collective-permute-start.1 = (bf16[128,2048]{1,0:T(8,128)(2,1)}, bf16[128,2048]{1,0:T(8,128)(2,1)S(1)}, u32[]{:S(2)}, u32[]{:S(2)}) collective-permute-start(bf16[128,2048]{1,0:T(8,128)(2,1)} %k0.3), channel_id=1, source_target_pairs={{0,8},{4,12},{8,16},{12,20},{16,24},{20,28},{24,32},{28,36},{32,40... | collective-permute-start | bytes 1572872 | tf_op jit(solution)/shard_map/ppermute | solution.py:26
  7.7 38.4 %copy-start.5 = (bf16[128,2048]{1,0:T(8,128)(2,1)}, bf16[128,2048]{1,0:T(8,128)(2,1)S(1)}, u32[]{:S(2)}) copy-start(bf16[128,2048]{1,0:T(8,128)(2,1)S(1)} %multiply_convert_fusion.kv) | copy-start | bytes 1572868
  7.8 38.4 %collective-permute-start.2 = (bf16[128,2048]{1,0:T(8,128)(2,1)S(1)}, bf16[128,2048]{1,0:T(8,128)(2,1)S(1)}, u32[]{:S(2)}, u32[]{:S(2)}) collective-permute-start(bf16[128,2048]{1,0:T(8,128)(2,1)S(1)} %multiply_convert_fusion.kv), channel_id=1, source_target_pairs={{0,4},{4,8},{8,12},{12,16},{16,20},{20,24},{24,28},{28,32},{32,36}... | collective-permute-start | bytes 1572872 | tf_op jit(solution)/shard_map/ppermute | solution.py:26
  18.0 5.6 %copy-start = (bf16[128,2048]{1,0:T(8,128)(2,1)}, bf16[128,2048]{1,0:T(8,128)(2,1)S(1)}, u32[]{:S(2)}) copy-start(bf16[128,2048]{1,0:T(8,128)(2,1)S(1)} %collective-permute-done.k1) | copy-start | bytes 1572868
  23.6 0.8 copy-start.1
  35.8 36.6 %collective-permute-start.10 = (bf16[128,2048]{1,0:T(8,128)(2,1)}, bf16[128,2048]{1,0:T(8,128)(2,1)S(1)}, u32[]{:S(2)}, u32[]{:S(2)}) collective-permute-start(bf16[128,2048]{1,0:T(8,128)(2,1)} %get-tuple-element.34), channel_id=1, source_target_pairs={{4,0},{8,4},{12,8},{16,12},{20,16},{24,20},{28,24},{32,28},{36,32}... | collective-permute-start | bytes 1572872 | tf_op jit(solution)/shard_map/ppermute | solution.py:26
  42.2 30.2 %collective-permute-start.11 = (bf16[128,2048]{1,0:T(8,128)(2,1)}, bf16[128,2048]{1,0:T(8,128)(2,1)S(1)}, u32[]{:S(2)}, u32[]{:S(2)}) collective-permute-start(bf16[128,2048]{1,0:T(8,128)(2,1)} %get-tuple-element.35), channel_id=1, source_target_pairs={{8,0},{12,4},{16,8},{20,12},{24,16},{28,20},{32,24},{36,28},{40,32... | collective-permute-start | bytes 1572872 | tf_op jit(solution)/shard_map/ppermute | solution.py:26
  46.1 0.8 copy-start.17
  55.9 5.8 %collective-permute-start.3 = (f32[8,128]{1,0:T(8,128)}, f32[8,128]{1,0:T(8,128)S(1)}, u32[]{:S(2)}, u32[]{:S(2)}) collective-permute-start(f32[8,128]{1,0:T(8,128)} %get-tuple-element.27.s0), channel_id=1, source_target_pairs={{0,1},{1,2},{2,3},{3,0},{4,5},{5,6},{6,7},{7,4},{8,9},{9,10},{10,1... | collective-permute-start | bytes 12296 | tf_op jit(solution)/shard_map/ppermute | solution.py:31
  57.5 5.3 %collective-permute-start.4 = (f32[8,128]{1,0:T(8,128)}, f32[8,128]{1,0:T(8,128)S(1)}, u32[]{:S(2)}, u32[]{:S(2)}) collective-permute-start(f32[8,128]{1,0:T(8,128)} %get-tuple-element.27.s0), channel_id=1, source_target_pairs={{0,2},{1,3},{2,0},{3,1},{4,6},{5,7},{6,4},{7,5},{8,10},{9,11},{10,... | collective-permute-start | bytes 12296 | tf_op jit(solution)/shard_map/ppermute | solution.py:31
  60.4 3.8 %collective-permute-start.5 = (f32[8,128]{1,0:T(8,128)}, f32[8,128]{1,0:T(8,128)S(1)}, u32[]{:S(2)}, u32[]{:S(2)}) collective-permute-start(f32[8,128]{1,0:T(8,128)} %get-tuple-element.27.s0), channel_id=1, source_target_pairs={{0,3},{1,0},{2,1},{3,2},{4,7},{5,4},{6,5},{7,6},{8,11},{9,8},{10,9... | collective-permute-start | bytes 12296 | tf_op jit(solution)/shard_map/ppermute | solution.py:31
  61.7 2.5 %copy-start.9 = (f32[8,128]{1,0:T(8,128)}, f32[8,128]{1,0:T(8,128)S(1)}, u32[]{:S(2)}) copy-start(f32[8,128]{1,0:T(8,128)S(1)} %collective-permute-done.3.s1) | copy-start | bytes 12292
  62.8 1.4 copy-start.10
  64.2 0.6 copy-start.11
  67.5 45.2 %collective-permute-start.6 = (bf16[128,2048]{1,0:T(8,128)(2,1)}, bf16[128,2048]{1,0:T(8,128)(2,1)S(1)}, u32[]{:S(2)}, u32[]{:S(2)}) collective-permute-start(bf16[128,2048]{1,0:T(8,128)(2,1)} %shard_map.146.v0), channel_id=1, source_target_pairs={{0,4},{4,8},{8,12},{12,16},{16,20},{20,24},{24,28},{28,32},{32,36}... | collective-permute-start | bytes 1572872 | tf_op jit(solution)/shard_map/ppermute | solution.py:26
  69.5 43.3 %collective-permute-start.7 = (bf16[128,2048]{1,0:T(8,128)(2,1)}, bf16[128,2048]{1,0:T(8,128)(2,1)S(1)}, u32[]{:S(2)}, u32[]{:S(2)}) collective-permute-start(bf16[128,2048]{1,0:T(8,128)(2,1)} %shard_map.146.v0), channel_id=1, source_target_pairs={{0,8},{4,12},{8,16},{12,20},{16,24},{20,28},{24,32},{28,36},{32,40... | collective-permute-start | bytes 1572872 | tf_op jit(solution)/shard_map/ppermute | solution.py:26
  72.4 0.8 copy-start.6
  72.4 0.9 copy-start.7
  77.1 5.0 %collective-permute-start.12 = (f32[8,128]{1,0:T(8,128)}, f32[8,128]{1,0:T(8,128)S(1)}, u32[]{:S(2)}, u32[]{:S(2)}) collective-permute-start(f32[8,128]{1,0:T(8,128)} %get-tuple-element.37.i0), channel_id=1, source_target_pairs={{0,1},{1,2},{2,3},{3,0},{4,5},{5,6},{6,7},{7,4},{8,9},{9,10},{10,1... | collective-permute-start | bytes 12296 | tf_op jit(solution)/shard_map/ppermute | solution.py:31
  77.3 5.7 %collective-permute-start.13 = (f32[8,128]{1,0:T(8,128)}, f32[8,128]{1,0:T(8,128)S(1)}, u32[]{:S(2)}, u32[]{:S(2)}) collective-permute-start(f32[8,128]{1,0:T(8,128)} %get-tuple-element.37.i0), channel_id=1, source_target_pairs={{0,2},{1,3},{2,0},{3,1},{4,6},{5,7},{6,4},{7,5},{8,10},{9,11},{10,... | collective-permute-start | bytes 12296 | tf_op jit(solution)/shard_map/ppermute | solution.py:31
  81.2 3.8 %collective-permute-start.14 = (f32[8,128]{1,0:T(8,128)}, f32[8,128]{1,0:T(8,128)S(1)}, u32[]{:S(2)}, u32[]{:S(2)}) collective-permute-start(f32[8,128]{1,0:T(8,128)} %get-tuple-element.37.i0), channel_id=1, source_target_pairs={{0,3},{1,0},{2,1},{3,2},{4,7},{5,4},{6,5},{7,6},{8,11},{9,8},{10,9... | collective-permute-start | bytes 12296 | tf_op jit(solution)/shard_map/ppermute | solution.py:31
  82.2 2.8 %copy-start.12 = (f32[8,128]{1,0:T(8,128)}, f32[8,128]{1,0:T(8,128)S(1)}, u32[]{:S(2)}) copy-start(f32[8,128]{1,0:T(8,128)S(1)} %collective-permute-done.12.i1) | copy-start | bytes 12292
  83.0 2.0 %copy-start.13 = (f32[8,128]{1,0:T(8,128)}, f32[8,128]{1,0:T(8,128)S(1)}, u32[]{:S(2)}) copy-start(f32[8,128]{1,0:T(8,128)S(1)} %collective-permute-done.13.i2) | copy-start | bytes 12292
  85.0 0.6 copy-start.14
  89.1 17.7 %copy-start.15 = (bf16[128,2048]{1,0:T(8,128)(2,1)S(1)}, bf16[128,2048]{1,0:T(8,128)(2,1)}, u32[]{:S(2)}) copy-start(bf16[128,2048]{1,0:T(8,128)(2,1)} %get-tuple-element.39.grad_signal) | copy-start | bytes 1572868
  99.6 1.5 collective-permute-start.16
  101.9 4.9 %collective-permute-start.17 = (f32[128,128]{1,0:T(8,128)S(1)}, f32[128,128]{1,0:T(8,128)S(1)}, u32[]{:S(2)}, u32[]{:S(2)}) collective-permute-start(f32[128,128]{1,0:T(8,128)S(1)} %add.53), channel_id=1, source_target_pairs={{0,64},{8,72},{16,80},{24,88},{32,96},{40,104},{48,112},{56,120},{... | collective-permute-start | bytes 196616 | tf_op jit(solution)/shard_map/ppermute | solution.py:265
  102.0 7.9 %collective-permute-start.18 = (f32[128,128]{1,0:T(8,128)S(1)}, f32[128,128]{1,0:T(8,128)S(1)}, u32[]{:S(2)}, u32[]{:S(2)}) collective-permute-start(f32[128,128]{1,0:T(8,128)S(1)} %add.53), channel_id=1, source_target_pairs={{0,128},{8,136},{16,144},{24,152},{32,160},{40,168},{48,176},{56,1... | collective-permute-start | bytes 196616 | tf_op jit(solution)/shard_map/ppermute | solution.py:265
  104.6 5.5 %collective-permute-start.19 = (f32[128,128]{1,0:T(8,128)S(1)}, f32[128,128]{1,0:T(8,128)S(1)}, u32[]{:S(2)}, u32[]{:S(2)}) collective-permute-start(f32[128,128]{1,0:T(8,128)S(1)} %add.53), channel_id=1, source_target_pairs={{0,192},{8,200},{16,208},{24,216},{32,224},{40,232},{48,240},{56,2... | collective-permute-start | bytes 196616 | tf_op jit(solution)/shard_map/ppermute | solution.py:265
  106.8 50.6 %collective-permute-start.15 = (bf16[128,2048]{1,0:T(8,128)(2,1)S(1)}, bf16[128,2048]{1,0:T(8,128)(2,1)S(1)}, u32[]{:S(2)}, u32[]{:S(2)}) collective-permute-start(bf16[128,2048]{1,0:T(8,128)(2,1)S(1)} %copy-done.15), channel_id=1, source_target_pairs={{4,0},{8,4},{12,8},{16,12},{20,16},{24,20},{28,24},{32,28},{36,32}... | collective-permute-start | bytes 1572872 | tf_op jit(solution)/shard_map/ppermute | solution.py:26
  110.0 20.3 %collective-permute-start.20 = (f32[128,128]{1,0:T(8,128)S(1)}, f32[128,128]{1,0:T(8,128)S(1)}, u32[]{:S(2)}, u32[]{:S(2)}) collective-permute-start(f32[128,128]{1,0:T(8,128)S(1)} %add_add_fusion.1), channel_id=1, source_target_pairs={{0,32},{8,40},{16,48},{24,56},{32,0},{40,8},{48,16},{56,24},{64,96... | collective-permute-start | bytes 196616 | tf_op jit(solution)/shard_map/ppermute | solution.py:268
  112.8 0.8 copy-start.3
  112.8 1.0 copy-start.4
  126.0 40.4 %copy-start.2 = (f32[128,2048]{1,0:T(8,128)S(1)}, f32[128,2048]{1,0:T(8,128)}, u32[]{:S(2)}) copy-start(f32[128,2048]{1,0:T(8,128)} %get-tuple-element.30) | copy-start | bytes 3145732
  126.0 40.4 %collective-permute-start.8 = (bf16[128,2048]{1,0:T(8,128)(2,1)}, bf16[128,2048]{1,0:T(8,128)(2,1)S(1)}, u32[]{:S(2)}, u32[]{:S(2)}) collective-permute-start(bf16[128,2048]{1,0:T(8,128)(2,1)} %get-tuple-element.31), channel_id=1, source_target_pairs={{4,0},{8,4},{12,8},{16,12},{20,16},{24,20},{28,24},{32,28},{36,32}... | collective-permute-start | bytes 1572872 | tf_op jit(solution)/shard_map/ppermute | solution.py:26
  128.1 38.4 %collective-permute-start.9 = (bf16[128,2048]{1,0:T(8,128)(2,1)}, bf16[128,2048]{1,0:T(8,128)(2,1)S(1)}, u32[]{:S(2)}, u32[]{:S(2)}) collective-permute-start(bf16[128,2048]{1,0:T(8,128)(2,1)} %get-tuple-element.32), channel_id=1, source_target_pairs={{8,0},{12,4},{16,8},{20,12},{24,16},{28,20},{32,24},{36,28},{40,32... | collective-permute-start | bytes 1572872 | tf_op jit(solution)/shard_map/ppermute | solution.py:26
  130.4 20.3 %collective-permute-start.21 = (f32[128,128]{1,0:T(8,128)S(1)}, f32[128,128]{1,0:T(8,128)S(1)}, u32[]{:S(2)}, u32[]{:S(2)}) collective-permute-start(f32[128,128]{1,0:T(8,128)S(1)} %add.57), channel_id=1, source_target_pairs={{0,8},{8,0},{16,24},{24,16},{32,40},{40,32},{48,56},{56,48},{64,72... | collective-permute-start | bytes 196616 | tf_op jit(solution)/shard_map/ppermute | solution.py:270
  132.2 21.3 %collective-permute-start.22 = (f32[128,128]{1,0:T(8,128)S(1)}, f32[128,128]{1,0:T(8,128)S(1)}, u32[]{:S(2)}, u32[]{:S(2)}) collective-permute-start(f32[128,128]{1,0:T(8,128)S(1)} %add.57), channel_id=1, source_target_pairs={{0,16},{8,24},{16,0},{24,8},{32,48},{40,56},{48,32},{56,40},{64,80... | collective-permute-start | bytes 196616 | tf_op jit(solution)/shard_map/ppermute | solution.py:270
  150.7 6.1 %collective-permute-start.23 = (f32[128,128]{1,0:T(8,128)S(1)}, f32[128,128]{1,0:T(8,128)S(1)}, u32[]{:S(2)}, u32[]{:S(2)}) collective-permute-start(f32[128,128]{1,0:T(8,128)S(1)} %add.57), channel_id=1, source_target_pairs={{0,24},{8,16},{16,8},{24,0},{32,56},{40,48},{48,40},{56,32},{64,88... | collective-permute-start | bytes 196616 | tf_op jit(solution)/shard_map/ppermute | solution.py:270
  157.4 0.8 copy-start.16

commit v2 on v1

--- a/solution.py
+++ b/solution.py
@@ -1,11 +1,10 @@
-import functools
-
 import jax
 import jax.numpy as jnp
 from jax import lax
 from jax.experimental import pallas as pl
 from jax.experimental.pallas import tpu as pltpu
 from jax.sharding import PartitionSpec as P
+
 
 HEAD = 128
 D = 8192
@@ -15,6 +14,7 @@
 F32 = jnp.float32
 BF16 = jnp.bfloat16
 SEQ_AXES = ("context", "mirror")
+UNROLL = 4
 
 VMEM = pl.BlockSpec(memory_space=pltpu.VMEM)
 SMEM = pl.BlockSpec(memory_space=pltpu.SMEM)
@@ -26,12 +26,16 @@
     return lax.ppermute(block, SEQ_AXES, route)
 
 
-def across(block, distance):
+def across(block):
     count = lax.axis_size("tensor")
-    return lax.ppermute(block, "tensor", [(i, (i + distance) % count) for i in range(count)])
-
-
-def call(body, ins, outs, flops, scratch=(), exps=0):
+    others = []
+    for d in (2, 1, 3):
+        route = [(i, (i + d) % count) for i in range(count)]
+        others.append(lax.ppermute(block, "tensor", route))
+    return [block] + others
+
+
+def call(body, ins, outs, flops, room, exps=0):
     nbytes = sum(a.size * a.dtype.itemsize for a in ins)
     nbytes += sum(o.size * o.dtype.itemsize for o in outs)
     specs = [SMEM if a.dtype == jnp.int32 else VMEM for a in ins]
@@ -40,7 +44,7 @@
         out_shape=tuple(outs),
         in_specs=specs,
         out_specs=tuple(VMEM for _ in outs),
-        scratch_shapes=list(scratch),
+        compiler_params=pltpu.CompilerParams(vmem_limit_bytes=room << 20),
         cost_estimate=pl.CostEstimate(flops=flops, bytes_accessed=nbytes, transcendentals=exps),
     )(*ins)
 
@@ -49,17 +53,19 @@
     return jax.ShapeDtypeStruct(shape, dtype)
 
 
-def doc_of(info, pos):
-    doc = (pos >= info[0]).astype(jnp.int32)
+def doc_of(lengths, pos):
+    end = lengths[0]
+    doc = (pos >= end).astype(jnp.int32)
     for i in range(1, 4):
-        doc = doc + (pos >= info[i]).astype(jnp.int32)
+        end = end + lengths[i]
+        doc = doc + (pos >= end).astype(jnp.int32)
     return doc
 
 
-def conv_mask(info, first, sign=1):
-    rows = info[4] + lax.broadcasted_iota(jnp.int32, (T, 2 * T), 0)
+def conv_mask(lengths, own, first, sign=1):
+    rows = own + lax.broadcasted_iota(jnp.int32, (T, 2 * T), 0)
     cols = first + sign * lax.broadcasted_iota(jnp.int32, (T, 2 * T), 1)
-    return doc_of(info, rows) == doc_of(info, cols)
+    return doc_of(lengths, rows) == doc_of(lengths, cols)
 
 
 def column(row):
@@ -85,13 +91,13 @@
     return pl.ds(pl.multiple_of(tile * LANES, LANES), LANES)
 
 
-def conv_body(info, left, kv, hyena_q, table, signal, square, flipped):
+def conv_body(lengths, start, left, kv, hyena_q, table, signal, square, flipped):
     span = 2 * T
     turned = lax.broadcasted_iota(jnp.int32, (span, span), 0) + lax.broadcasted_iota(
         jnp.int32, (span, span), 1
     )
     turn = jnp.where(turned == span - 1, 1.0, 0.0).astype(BF16)
-    mask = conv_mask(info, info[4] - T)
+    mask = conv_mask(lengths, start[0], start[0] - T)
     tiles = kv.shape[1] // LANES
 
     def step(tile, acc):
@@ -103,7 +109,7 @@
         mix = hyena_q[:, at].astype(F32) * out
         return acc + mix * mix
 
-    acc = lax.fori_loop(0, tiles, step, jnp.zeros((T, LANES), F32))
+    acc = lax.fori_loop(0, tiles, step, jnp.zeros((T, LANES), F32), unroll=UNROLL)
     square[...] = jnp.broadcast_to(jnp.sum(jnp.transpose(acc), axis=0, keepdims=True), (8, LANES))
 
 
@@ -123,18 +129,18 @@
         values[:, at] = (mix * inv * gain[:, at]).astype(BF16)
         return 0
 
-    lax.fori_loop(0, signal.shape[1] // LANES, step, 0)
-
-
-def scores_body(info, q, k0, k1, k2, og, prob, own, part1, part2):
+    lax.fori_loop(0, signal.shape[1] // LANES, step, 0, unroll=UNROLL)
+
+
+def scores_body(lengths, start, q, k0, k1, k2, og, prob, own, part1, part2):
     span = 3 * T
-    query_pos = info[4] + lax.broadcasted_iota(jnp.int32, (span, T), 1)
-    key_pos = info[4] - 2 * T + lax.broadcasted_iota(jnp.int32, (span, T), 0)
+    query_pos = start[0] + lax.broadcasted_iota(jnp.int32, (span, T), 1)
+    key_pos = start[0] - 2 * T + lax.broadcasted_iota(jnp.int32, (span, T), 0)
     allowed = (
         (key_pos >= 0)
         & (key_pos <= query_pos)
         & (query_pos - key_pos <= 2 * T)
-        & (doc_of(info, key_pos) == doc_of(info, query_pos))
+        & (doc_of(lengths, key_pos) == doc_of(lengths, query_pos))
     )
     scale = HEAD**-0.5
 
@@ -153,7 +159,7 @@
         own[:, at] = part[2 * T :]
         return 0
 
-    lax.fori_loop(0, q.shape[1] // HEAD, step, 0)
+    lax.fori_loop(0, q.shape[1] // HEAD, step, 0, unroll=UNROLL)
 
 
 def inner_body(own, part1, part2, signal, hyena_q, gain, grad_values, inner):
@@ -164,7 +170,7 @@
         grad_values[:, at] = gv
         return acc + gv * (hyena_q[:, at].astype(F32) * signal[:, at])
 
-    acc = lax.fori_loop(0, own.shape[1] // LANES, step, jnp.zeros((T, LANES), F32))
+    acc = lax.fori_loop(0, own.shape[1] // LANES, step, jnp.zeros((T, LANES), F32), unroll=UNROLL)
     inner[...] = jnp.broadcast_to(jnp.sum(jnp.transpose(acc), axis=0, keepdims=True), (8, LANES))
 
 
@@ -185,11 +191,11 @@
         grad_signal[:, at] = (grad_mix * hq).astype(BF16)
         return 0
 
-    lax.fori_loop(0, signal.shape[1] // LANES, step, 0)
-
-
-def filter_body(info, flipped, grad_signal, out):
-    mask = conv_mask(info, info[4] + T - 1, -1)
+    lax.fori_loop(0, signal.shape[1] // LANES, step, 0, unroll=UNROLL)
+
+
+def filter_body(lengths, start, flipped, grad_signal, out):
+    mask = conv_mask(lengths, start[0], start[0] + T - 1, -1)
     lane_group = lax.broadcasted_iota(jnp.int32, (T, LANES), 1) // GROUP
     count = LANES // GROUP
 
@@ -210,11 +216,11 @@
         out[pl.ds(pl.multiple_of(tile * 8, 8), 8), :] = jnp.concatenate(rows, axis=0)
         return 0
 
-    lax.fori_loop(0, grad_signal.shape[1] // LANES, step, 0)
-
-
-def conv_back_body(info, grad_signal, right, hyena_k, hyena_v, table, grad_k, grad_v):
-    mask = conv_mask(info, info[4])
+    lax.fori_loop(0, grad_signal.shape[1] // LANES, step, 0, unroll=UNROLL)
+
+
+def conv_back_body(lengths, start, grad_signal, right, hyena_k, hyena_v, table, grad_k, grad_v):
+    mask = conv_mask(lengths, start[0], start[0])
 
     def step(tile, _):
         at = lanes_of(tile)
@@ -224,7 +230,7 @@
         grad_v[:, at] = (grad_kv * hyena_k[:, at].astype(F32)).astype(BF16)
         return 0
 
-    lax.fori_loop(0, hyena_k.shape[1] // LANES, step, 0)
+    lax.fori_loop(0, hyena_k.shape[1] // LANES, step, 0, unroll=UNROLL)
 
 
 def attend_body(
@@ -253,22 +259,19 @@
         own[:, at] = part[2 * T :]
         return 0
 
-    lax.fori_loop(0, q.shape[1] // HEAD, step, 0)
+    lax.fori_loop(0, q.shape[1] // HEAD, step, 0, unroll=UNROLL)
 
 
 def over_sequence(x):
-    def route(f):
-        return [(i, f(i // 8, i % 8)) for i in range(32)]
+    def send(x, f):
+        return lax.ppermute(x, "context", [(i, f(i // 8, i % 8)) for i in range(32)])
 
     x = x + lax.ppermute(x, "mirror", [(0, 1), (1, 0)])
-    x = x + sum(
-        lax.ppermute(x, "context", route(lambda a, b, d=d: ((a + d) % 4) * 8 + b))
-        for d in (1, 2, 3)
-    )
-    x = x + lax.ppermute(x, "context", route(lambda a, b: a * 8 + (b ^ 4)))
-    return x + sum(
-        lax.ppermute(x, "context", route(lambda a, b, d=d: a * 8 + (b ^ d))) for d in (1, 2, 3)
-    )
+    parts = [send(x, lambda a, b, d=d: ((a + d) % 4) * 8 + b) for d in (2, 1, 3)]
+    x = x + parts[0] + parts[1] + parts[2]
+    x = x + send(x, lambda a, b: a * 8 + (b ^ 4))
+    parts = [send(x, lambda a, b, d=d: a * 8 + (b ^ d)) for d in (3, 2, 1)]
+    return x + parts[0] + parts[1] + parts[2]
 
 
 def body(hyena_q, hyena_k, hyena_v, filters, norm_gain, attn_q, attn_k, out_grad, doc_lengths):
@@ -277,85 +280,80 @@
     big = (rows, channels)
     band_flops = 2 * (channels // GROUP) * T * 2 * T * LANES
     attn_flops = 2 * heads * 3 * T * T * HEAD
-    offset = lax.axis_index(SEQ_AXES) * rows
-    ends = [doc_lengths[0]]
-    for i in range(1, 4):
-        ends.append(ends[-1] + doc_lengths[i])
-    info = jnp.stack(ends + [offset.astype(jnp.int32)])
+    start = (lax.axis_index(SEQ_AXES) * rows).astype(jnp.int32).reshape(1)
+    at = (doc_lengths, start)
     gain = norm_gain[None, :]
+    wide = sds(*big)
+    half = sds(*big, dtype=BF16)
+    small = sds(8, LANES)
 
     kv = (hyena_k.astype(F32) * hyena_v.astype(F32)).astype(BF16)
     left = shifted(kv, 1)
+    k2 = shifted(attn_k, 2)
     k1 = shifted(attn_k, 1)
-    k2 = shifted(attn_k, 2)
     groups = filters.shape[0]
-    wide = filters.astype(F32)
-    back_table = jnp.concatenate([wide, jnp.zeros((groups, T), F32)], axis=1)
+    taps = filters.astype(F32)
+    back_table = jnp.concatenate([taps, jnp.zeros((groups, T), F32)], axis=1)
     fwd_table = jnp.concatenate(
-        [jnp.zeros((groups, 1), F32), wide[:, ::-1], jnp.zeros((groups, T - 1), F32)], axis=1
+        [jnp.zeros((groups, 1), F32), taps[:, ::-1], jnp.zeros((groups, T - 1), F32)], axis=1
     )
     signal, square, flipped = call(
         conv_body,
-        (info, left, kv, hyena_q, fwd_table),
-        (sds(*big), sds(8, LANES), sds(2 * rows, channels, dtype=BF16)),
+        (*at, left, kv, hyena_q, fwd_table),
+        (wide, small, sds(2 * rows, channels, dtype=BF16)),
         band_flops,
-    )
-    squares = [square] + [across(square, d) for d in (1, 2, 3)]
-    (values,) = call(
-        values_body,
-        (signal, hyena_q, gain, *squares),
-        (sds(*big, dtype=BF16),),
-        4 * rows * channels,
-    )
+        8,
+    )
+    squares = across(square)
     prob, value_own, value1, value2 = call(
         scores_body,
-        (info, attn_q, attn_k, k1, k2, out_grad),
-        (sds(heads, 3 * T, T), sds(*big), sds(*big, dtype=BF16), sds(*big, dtype=BF16)),
+        (*at, attn_q, attn_k, k1, k2, out_grad),
+        (sds(heads, 3 * T, T), wide, half, half),
         2 * attn_flops,
+        16,
         exps=heads * 3 * T * T,
     )
+    back2 = shifted(value2, -2)
+    back1 = shifted(value1, -1)
+    (values,) = call(
+        values_body, (signal, hyena_q, gain, *squares), (half,), 4 * rows * channels, 8
+    )
+    v2 = shifted(values, 2)
     v1 = shifted(values, 1)
-    v2 = shifted(values, 2)
-    back1 = shifted(value1, -1)
-    back2 = shifted(value2, -2)
     gain_grad, inner = call(
         inner_body,
         (value_own, back1, back2, signal, hyena_q, gain),
-        (sds(*big), sds(8, LANES)),
+        (wide, small),
         6 * rows * channels,
-    )
-    inners = [inner] + [across(inner, d) for d in (1, 2, 3)]
+        10,
+    )
+    inners = across(inner)
+    attn_out, grad_attn_q, key_own, key1, key2 = call(
+        attend_body,
+        (prob, attn_q, attn_k, k1, k2, values, v1, v2, out_grad),
+        (half, half, wide, half, half),
+        4 * attn_flops,
+        16,
+    )
+    from2 = shifted(key2, -2)
+    from1 = shifted(key1, -1)
     grad_hyena_q, grad_signal = call(
         signal_grad_body,
         (gain_grad, signal, hyena_q, *squares, *inners),
-        (sds(*big, dtype=BF16), sds(*big, dtype=BF16)),
+        (half, half),
         8 * rows * channels,
+        10,
     )
     right = shifted(grad_signal, -1)
-    (local,) = call(
-        filter_body, (info, flipped, grad_signal), (sds(groups, LANES),), band_flops
-    )
+    (local,) = call(filter_body, (*at, flipped, grad_signal), (sds(groups, LANES),), band_flops, 10)
     grad_filters = over_sequence(local)
-    attn_out, grad_attn_q, key_own, key1, key2 = call(
-        attend_body,
-        (prob, attn_q, attn_k, k1, k2, values, v1, v2, out_grad),
-        (
-            sds(*big, dtype=BF16),
-            sds(*big, dtype=BF16),
-            sds(*big),
-            sds(*big, dtype=BF16),
-            sds(*big, dtype=BF16),
-        ),
-        4 * attn_flops,
-    )
-    grad_attn_k = (
-        key_own + shifted(key1, -1).astype(F32) + shifted(key2, -2).astype(F32)
-    ).astype(BF16)
+    grad_attn_k = (key_own + from1.astype(F32) + from2.astype(F32)).astype(BF16)
     grad_hyena_k, grad_hyena_v = call(
         conv_back_body,
-        (info, grad_signal, right, hyena_k, hyena_v, back_table),
-        (sds(*big, dtype=BF16), sds(*big, dtype=BF16)),
+        (*at, grad_signal, right, hyena_k, hyena_v, back_table),
+        (half, half),
         band_flops,
+        10,
     )
     return (
         attn_out,
@@ -370,6 +368,7 @@
 
 def solution(mesh):
     tokens = P(SEQ_AXES, "tensor")
+
     return jax.shard_map(
         body,
         mesh=mesh,

time: 168 us -> 139 us (0.83)
  Pallas kernels: 61.4 us -> 32.5 us
  waiting for transfers between devices: 36.5 us -> 42.9 us
  local copies, waits for them, and re-layouts: 8.95 us -> 5.64 us
  between operations: 3.48 us -> 0.95 us
    pallas_call x8, Pallas kernels: 61.4 us -> 32.5 us  [call(): pl.pallas_call(body, out_shape=tuple(outs), in_specs=specs, out_specs=tup...]
    ppermute x10, waiting for transfers between devices: 6.96 us -> 11.4 us  [shifted(): return lax.ppermute(block, SEQ_AXES, route)]
    ppermute x13, waiting for transfers between devices: 28.1 us -> 30.2 us  [the longest x7 25.6 us: send(): lax.ppermute(x, 'context', [(i, f(i // 8, i % 8)) for i in range(32)])]
    unnamed x36 -> x30, local copies, waits for them, and re-layouts: 5.49 us -> 5.46 us
  transfers between devices with their start and end apart: 24 -> 24, of which waited for: 12 -> 11; matrix products, arithmetic and copies ran while one was open for 4% -> 2% of each run, Pallas kernels for 37% -> 24%
where the time goes in v2:
time: 139 us; the launch traced here: 138 us
  starting transfers between devices  52.3 us (38%)
  waiting for transfers between devices  42.9 us (31%)
  Pallas kernels  32.5 us (23%)
  local copies, waits for them, and re-layouts  5.64 us (4%)
  other arithmetic  3.9 us (3%)
    pallas_call x8, Pallas kernels, call(): pl.pallas_call(body, out_shape=tuple(outs), in_specs=specs, out_specs=tup...  32.5 us
    ppermute x10, starting transfers between devices, shifted(): return lax.ppermute(block, SEQ_AXES, route)  32.2 us
    ppermute x7, waiting for transfers between devices, send(): lax.ppermute(x, 'context', [(i, f(i // 8, i % 8)) for i in range(32)])  25.6 us
    ppermute x10, waiting for transfers between devices, shifted(): return lax.ppermute(block, SEQ_AXES, route)  11.4 us
    ppermute x6, starting transfers between devices, across(): others.append(lax.ppermute(block, 'tensor', route))  11.3 us
    ppermute x7, starting transfers between devices, send(): lax.ppermute(x, 'context', [(i, f(i // 8, i % 8)) for i in range(32)])  8.76 us
    unnamed x30, local copies, waits for them, and re-layouts  5.46 us
    ppermute x6, waiting for transfers between devices, across(): others.append(lax.ppermute(block, 'tensor', route))  4.58 us
  transfers between devices with their start and end apart: 24, of which 11 were waited for; matrix products, arithmetic and copies ran while one was open for 2% of the time, Pallas kernels for 24%

profile of v2, /device:TPU:6, one launch (start us, length us, event | category | flops | bytes accessed | tf_op | source)
XLA Modules:
  0.0 138.2 jit_solution(7029085665225398241)
XLA Ops:
  0.6 0.0 copy-start.13
  0.7 2.1 %collective-permute-start = (bf16[128,2048]{1,0:T(8,128)(2,1)}, bf16[128,2048]{1,0:T(8,128)(2,1)S(1)}, u32[]{:S(2)}, u32[]{:S(2)}) collective-permute-start(bf16[128,2048]{1,0:T(8,128)(2,1)} %k0.3), channel_id=1, source_target_pairs={{0,4},{4,8},{8,12},{12,16},{16,20},{20,24},{24,28},{28,32},{32,36}... | collective-permute-start | bytes 1572872 | tf_op jit(solution)/shard_map/ppermute | solution.py:26
  2.7 3.8 %collective-permute-start.1 = (bf16[128,2048]{1,0:T(8,128)(2,1)}, bf16[128,2048]{1,0:T(8,128)(2,1)S(1)}, u32[]{:S(2)}, u32[]{:S(2)}) collective-permute-start(bf16[128,2048]{1,0:T(8,128)(2,1)} %k0.3), channel_id=1, source_target_pairs={{0,8},{4,12},{8,16},{12,20},{16,24},{20,28},{24,32},{28,36},{32,40... | collective-permute-start | bytes 1572872 | tf_op jit(solution)/shard_map/ppermute | solution.py:26
  6.6 2.1 %multiply_convert_fusion.kv = bf16[128,2048]{1,0:T(8,128)(2,1)} fusion(bf16[128,2048]{1,0:T(8,128)(2,1)} %hyena_v.1, bf16[128,2048]{1,0:T(8,128)(2,1)} %hyena_k.1), kind=kLoop, calls=%fused_computation.1 | loop fusion | flops 1048576 | bytes 1572864 | tf_op jit(solution)/shard_map/convert_element_type | solution.py:290
  8.7 3.6 %collective-permute-start.2 = (bf16[128,2048]{1,0:T(8,128)(2,1)}, bf16[128,2048]{1,0:T(8,128)(2,1)}, u32[]{:S(2)}, u32[]{:S(2)}) collective-permute-start(bf16[128,2048]{1,0:T(8,128)(2,1)} %multiply_convert_fusion.kv), channel_id=1, source_target_pairs={{0,4},{4,8},{8,12},{12,16},{16,20},{20,24},{24,28},{28,32},{32,36}... | collective-permute-start | bytes 1572872 | tf_op jit(solution)/shard_map/ppermute | solution.py:26
  12.3 5.8 %collective-permute-done.k1 = bf16[128,2048]{1,0:T(8,128)(2,1)S(1)} collective-permute-done((bf16[128,2048]{1,0:T(8,128)(2,1)}, bf16[128,2048]{1,0:T(8,128)(2,1)S(1)}, u32[]{:S(2)}, u32[]{:S(2)}) %collective-permute-start) | collective-permute-done | bytes 524320 | tf_op jit(solution)/shard_map/ppermute | solution.py:26
  18.2 5.6 %collective-permute-done.1.k2 = bf16[128,2048]{1,0:T(8,128)(2,1)S(1)} collective-permute-done((bf16[128,2048]{1,0:T(8,128)(2,1)}, bf16[128,2048]{1,0:T(8,128)(2,1)S(1)}, u32[]{:S(2)}, u32[]{:S(2)}) %collective-permute-start.1) | collective-permute-done | bytes 524320 | tf_op jit(solution)/shard_map/ppermute | solution.py:26
  23.7 1.0 copy-done.3
  24.8 1.0 copy-done.5
  25.8 1.0 copy-done.7
  26.9 0.7 copy-done.12
  27.5 5.2 %shard_map.144 = (f32[16,384,128]{2,1,0:T(8,128)S(1)}, f32[128,2048]{1,0:T(8,128)S(1)}, bf16[128,2048]{1,0:T(8,128)(2,1)}, bf16[128,2048]{1,0:T(8,128)(2,1)}) custom-call(s32[4]{0:T(128)S(1)} %copy-done.12, s32[1]{0:T(128)} %bitcast.start, bf16[128,2048]{1,0:T(8,128)(2,1)S(1)} %copy-done.3, bf16[128,2048]{1,0:T(8,128)(2,1)S(1)} %copy-done.5, ...), custom_call_target="tpu_custom_call" | custom-call | flops 402653184 | bytes 7864340 | tf_op jit(solution)/shard_map/pallas_call | solution.py:42
  32.7 1.6 %copy-done.1 = f32[16,384,128]{2,1,0:T(8,128)} copy-done((f32[16,384,128]{2,1,0:T(8,128)}, f32[16,384,128]{2,1,0:T(8,128)S(1)}, u32[]{:S(2)}) %copy-start.1) | copy-done | bytes 3145752
  34.3 6.5 %collective-permute-start.10 = (bf16[128,2048]{1,0:T(8,128)(2,1)}, bf16[128,2048]{1,0:T(8,128)(2,1)S(1)}, u32[]{:S(2)}, u32[]{:S(2)}) collective-permute-start(bf16[128,2048]{1,0:T(8,128)(2,1)} %get-tuple-element.34), channel_id=1, source_target_pairs={{4,0},{8,4},{12,8},{16,12},{20,16},{24,20},{28,24},{32,28},{36,32}... | collective-permute-start | bytes 1572872 | tf_op jit(solution)/shard_map/ppermute | solution.py:26
  40.8 2.9 %collective-permute-start.11 = (bf16[128,2048]{1,0:T(8,128)(2,1)}, bf16[128,2048]{1,0:T(8,128)(2,1)}, u32[]{:S(2)}, u32[]{:S(2)}) collective-permute-start(bf16[128,2048]{1,0:T(8,128)(2,1)} %get-tuple-element.35), channel_id=1, source_target_pairs={{8,0},{12,4},{16,8},{20,12},{24,16},{28,20},{32,24},{36,28},{40,32... | collective-permute-start | bytes 1572872 | tf_op jit(solution)/shard_map/ppermute | solution.py:26
  43.7 0.1 rev.3
  43.8 0.1 pad.3.clone
  43.9 0.1 maximum_maximum_fusion.table
  44.0 0.0 collective-permute-done.2.left
  44.0 5.3 %shard_map.145 = (f32[128,2048]{1,0:T(8,128)S(1)}, f32[8,128]{1,0:T(8,128)S(1)}, bf16[256,2048]{1,0:T(8,128)(2,1)S(1)}) custom-call(s32[4]{0:T(128)S(1)} %copy-done.13, s32[1]{0:T(128)} %bitcast.start, bf16[128,2048]{1,0:T(8,128)(2,1)} %collective-permute-done.2.left, bf16[128,2048]{1,0:T(8,128)(2,1)} %multiply_convert_fusion.kv, ...), custom_call_target="tpu_custom_call" | custom-call | flops 1073741824 | bytes 3805204 | tf_op jit(solution)/shard_map/pallas_call | solution.py:42
  49.4 3.3 %collective-permute-start.3 = (f32[8,128]{1,0:T(8,128)S(1)}, f32[8,128]{1,0:T(8,128)S(1)}, u32[]{:S(2)}, u32[]{:S(2)}) collective-permute-start(f32[8,128]{1,0:T(8,128)S(1)} %get-tuple-element.27.s0), channel_id=1, source_target_pairs={{0,2},{1,3},{2,0},{3,1},{4,6},{5,7},{6,4},{7,5},{8,10},{9,11},{10,... | collective-permute-start | bytes 12296 | tf_op jit(solution)/shard_map/ppermute | solution.py:34
  52.6 0.7 collective-permute-start.4
  53.3 2.6 %collective-permute-start.5 = (f32[8,128]{1,0:T(8,128)S(1)}, f32[8,128]{1,0:T(8,128)S(1)}, u32[]{:S(2)}, u32[]{:S(2)}) collective-permute-start(f32[8,128]{1,0:T(8,128)S(1)} %get-tuple-element.27.s0), channel_id=1, source_target_pairs={{0,3},{1,0},{2,1},{3,2},{4,7},{5,4},{6,5},{7,6},{8,11},{9,8},{10,9... | collective-permute-start | bytes 12296 | tf_op jit(solution)/shard_map/ppermute | solution.py:34
  55.9 0.0 collective-permute-done.3.s1
  55.9 1.6 %collective-permute-done.4.s2 = f32[8,128]{1,0:T(8,128)S(1)} collective-permute-done((f32[8,128]{1,0:T(8,128)S(1)}, f32[8,128]{1,0:T(8,128)S(1)}, u32[]{:S(2)}, u32[]{:S(2)}) %collective-permute-start.4) | collective-permute-done | bytes 4128 | tf_op jit(solution)/shard_map/ppermute | solution.py:34
  57.5 0.0 collective-permute-done.5.s3
  57.5 0.5 shard_map.146.v0
  58.0 1.9 %collective-permute-start.6 = (bf16[128,2048]{1,0:T(8,128)(2,1)S(1)}, bf16[128,2048]{1,0:T(8,128)(2,1)S(1)}, u32[]{:S(2)}, u32[]{:S(2)}) collective-permute-start(bf16[128,2048]{1,0:T(8,128)(2,1)S(1)} %shard_map.146.v0), channel_id=1, source_target_pairs={{0,4},{4,8},{8,12},{12,16},{16,20},{20,24},{24,28},{28,32},{32,36}... | collective-permute-start | bytes 1572872 | tf_op jit(solution)/shard_map/ppermute | solution.py:26
  59.9 2.9 %collective-permute-start.7 = (bf16[128,2048]{1,0:T(8,128)(2,1)S(1)}, bf16[128,2048]{1,0:T(8,128)(2,1)S(1)}, u32[]{:S(2)}, u32[]{:S(2)}) collective-permute-start(bf16[128,2048]{1,0:T(8,128)(2,1)S(1)} %shard_map.146.v0), channel_id=1, source_target_pairs={{0,8},{4,12},{8,16},{12,20},{16,24},{20,28},{24,32},{28,36},{32,40... | collective-permute-start | bytes 1572872 | tf_op jit(solution)/shard_map/ppermute | solution.py:26
  62.8 0.0 collective-permute-done.10.part1
  62.8 0.0 collective-permute-done.11.part2
  62.8 1.9 %shard_map.148 = (f32[128,2048]{1,0:T(8,128)S(1)}, f32[8,128]{1,0:T(8,128)S(1)}) custom-call(f32[128,2048]{1,0:T(8,128)S(1)} %get-tuple-element.33.own, bf16[128,2048]{1,0:T(8,128)(2,1)S(1)} %collective-permute-done.10.part1, bf16[128,2048]{1,0:T(8,128)(2,1)} %collective-permute-done.11.part2, f32[128,2048]{1,0:T(8,128)S(1)} %get-tuple-element.26.signal, ...), custom_call_target="tpu_custom_call" | custom-call | flops 1572864 | bytes 4730880 | tf_op jit(solution)/shard_map/pallas_call | solution.py:42
  64.8 1.5 %collective-permute-start.12 = (f32[8,128]{1,0:T(8,128)S(1)}, f32[8,128]{1,0:T(8,128)S(1)}, u32[]{:S(2)}, u32[]{:S(2)}) collective-permute-start(f32[8,128]{1,0:T(8,128)S(1)} %get-tuple-element.37.i0), channel_id=1, source_target_pairs={{0,2},{1,3},{2,0},{3,1},{4,6},{5,7},{6,4},{7,5},{8,10},{9,11},{10,... | collective-permute-start | bytes 12296 | tf_op jit(solution)/shard_map/ppermute | solution.py:34
  66.3 2.6 %collective-permute-start.13 = (f32[8,128]{1,0:T(8,128)S(1)}, f32[8,128]{1,0:T(8,128)S(1)}, u32[]{:S(2)}, u32[]{:S(2)}) collective-permute-start(f32[8,128]{1,0:T(8,128)S(1)} %get-tuple-element.37.i0), channel_id=1, source_target_pairs={{0,1},{1,2},{2,3},{3,0},{4,5},{5,6},{6,7},{7,4},{8,9},{9,10},{10,1... | collective-permute-start | bytes 12296 | tf_op jit(solution)/shard_map/ppermute | solution.py:34
  68.9 0.6 collective-permute-start.14
  69.5 0.4 collective-permute-done.12.i1
  70.0 1.2 collective-permute-done.13.i2
  71.1 1.4 %collective-permute-done.14.i3 = f32[8,128]{1,0:T(8,128)S(1)} collective-permute-done((f32[8,128]{1,0:T(8,128)S(1)}, f32[8,128]{1,0:T(8,128)S(1)}, u32[]{:S(2)}, u32[]{:S(2)}) %collective-permute-start.14) | collective-permute-done | bytes 4128 | tf_op jit(solution)/shard_map/ppermute | solution.py:34
  72.6 1.7 %shard_map.149 = (bf16[128,2048]{1,0:T(8,128)(2,1)}, bf16[128,2048]{1,0:T(8,128)(2,1)S(1)}) custom-call(f32[128,2048]{1,0:T(8,128)S(1)} %get-tuple-element.36.grad_values, f32[128,2048]{1,0:T(8,128)S(1)} %get-tuple-element.26.signal, bf16[128,2048]{1,0:T(8,128)(2,1)S(1)} %copy-done, f32[8,128]{1,0:T(8,128)S(1)} %get-tuple-element.27.s0, ...), custom_call_target="tpu_custom_call" | custom-call | flops 2097152 | bytes 3702784 | tf_op jit(solution)/shard_map/pallas_call | solution.py:42
  74.2 6.3 %shard_map.151 = f32[128,128]{1,0:T(8,128)S(1)} custom-call(s32[4]{0:T(128)S(1)} %copy-done.13, s32[1]{0:T(128)} %bitcast.start, bf16[256,2048]{1,0:T(8,128)(2,1)S(1)} %get-tuple-element.42.flipped, bf16[128,2048]{1,0:T(8,128)(2,1)S(1)} %get-tuple-element.39.grad_signal), custom_call_target="tpu_custom_call" | custom-call | flops 1073741824 | bytes 1638420 | tf_op jit(solution)/shard_map/pallas_call | solution.py:42
  80.6 0.1 collective-permute-start.16
  80.7 1.2 collective-permute-done.16
  81.9 1.2 collective-permute-start.17
  83.1 2.1 %collective-permute-start.18 = (f32[128,128]{1,0:T(8,128)S(1)}, f32[128,128]{1,0:T(8,128)S(1)}, u32[]{:S(2)}, u32[]{:S(2)}) collective-permute-start(f32[128,128]{1,0:T(8,128)S(1)} %add.38), channel_id=1, source_target_pairs={{0,64},{8,72},{16,80},{24,88},{32,96},{40,104},{48,112},{56,120},{... | collective-permute-start | bytes 196616 | tf_op jit(solution)/shard_map/ppermute | solution.py:267
  85.2 2.6 %collective-permute-done.17 = f32[128,128]{1,0:T(8,128)S(1)} collective-permute-done((f32[128,128]{1,0:T(8,128)S(1)}, f32[128,128]{1,0:T(8,128)S(1)}, u32[]{:S(2)}, u32[]{:S(2)}) %collective-permute-start.17) | collective-permute-done | bytes 65568 | tf_op jit(solution)/shard_map/ppermute | solution.py:267
  87.8 3.7 %collective-permute-start.15 = (bf16[128,2048]{1,0:T(8,128)(2,1)S(1)}, bf16[128,2048]{1,0:T(8,128)(2,1)S(1)}, u32[]{:S(2)}, u32[]{:S(2)}) collective-permute-start(bf16[128,2048]{1,0:T(8,128)(2,1)S(1)} %get-tuple-element.39.grad_signal), channel_id=1, source_target_pairs={{4,0},{8,4},{12,8},{16,12},{20,16},{24,20},{28,24},{32,28},{36,32}... | collective-permute-start | bytes 1572872 | tf_op jit(solution)/shard_map/ppermute | solution.py:26
  91.5 0.0 collective-permute-done.18
  91.6 2.1 %collective-permute-start.20 = (f32[128,128]{1,0:T(8,128)S(1)}, f32[128,128]{1,0:T(8,128)S(1)}, u32[]{:S(2)}, u32[]{:S(2)}) collective-permute-start(f32[128,128]{1,0:T(8,128)S(1)} %add_add_fusion.1), channel_id=1, source_target_pairs={{0,32},{8,40},{16,48},{24,56},{32,0},{40,8},{48,16},{56,24},{64,96... | collective-permute-start | bytes 196616 | tf_op jit(solution)/shard_map/ppermute | solution.py:267
  93.7 0.0 collective-permute-done.6.v1
  93.7 0.0 collective-permute-done.7.v2
  93.7 0.0 copy-start.9
  93.7 0.0 copy-start.10
  93.7 6.2 %shard_map.147 = (bf16[128,2048]{1,0:T(8,128)(2,1)}, bf16[128,2048]{1,0:T(8,128)(2,1)}, f32[128,2048]{1,0:T(8,128)S(1)}, bf16[128,2048]{1,0:T(8,128)(2,1)S(1)}, bf16[128,2048]{1,0:T(8,128)(2,1)S(1)}) custom-call(f32[16,384,128]{2,1,0:T(8,128)S(1)} %copy-done.2, bf16[128,2048]{1,0:T(8,128)(2,1)S(1)} %copy-done.4, bf16[128,2048]{1,0:T(8,128)(2,1)S(1)} %copy-done.6, ...), custom_call_target="tpu_custom_call" | custom-call | flops 805306368 | bytes 10485760 | tf_op jit(solution)/shard_map/pallas_call | solution.py:42
  100.0 2.6 %collective-permute-start.8 = (bf16[128,2048]{1,0:T(8,128)(2,1)S(1)}, bf16[128,2048]{1,0:T(8,128)(2,1)S(1)}, u32[]{:S(2)}, u32[]{:S(2)}) collective-permute-start(bf16[128,2048]{1,0:T(8,128)(2,1)S(1)} %get-tuple-element.31), channel_id=1, source_target_pairs={{4,0},{8,4},{12,8},{16,12},{20,16},{24,20},{28,24},{32,28},{36,32}... | collective-permute-start | bytes 1572872 | tf_op jit(solution)/shard_map/ppermute | solution.py:26
  102.6 2.1 %collective-permute-start.9 = (bf16[128,2048]{1,0:T(8,128)(2,1)S(1)}, bf16[128,2048]{1,0:T(8,128)(2,1)S(1)}, u32[]{:S(2)}, u32[]{:S(2)}) collective-permute-start(bf16[128,2048]{1,0:T(8,128)(2,1)S(1)} %get-tuple-element.32), channel_id=1, source_target_pairs={{8,0},{12,4},{16,8},{20,12},{24,16},{28,20},{32,24},{36,28},{40,32... | collective-permute-start | bytes 1572872 | tf_op jit(solution)/shard_map/ppermute | solution.py:26
  104.8 3.0 %collective-permute-start.21 = (f32[128,128]{1,0:T(8,128)S(1)}, f32[128,128]{1,0:T(8,128)S(1)}, u32[]{:S(2)}, u32[]{:S(2)}) collective-permute-start(f32[128,128]{1,0:T(8,128)S(1)} %add.42), channel_id=1, source_target_pairs={{0,24},{8,16},{16,8},{24,0},{32,56},{40,48},{48,40},{56,32},{64,88... | collective-permute-start | bytes 196616 | tf_op jit(solution)/shard_map/ppermute | solution.py:267
  107.7 0.4 collective-permute-start.22
  108.1 18.8 %collective-permute-done.21 = f32[128,128]{1,0:T(8,128)S(1)} collective-permute-done((f32[128,128]{1,0:T(8,128)S(1)}, f32[128,128]{1,0:T(8,128)S(1)}, u32[]{:S(2)}, u32[]{:S(2)}) %collective-permute-start.21) | collective-permute-done | bytes 65568 | tf_op jit(solution)/shard_map/ppermute | solution.py:267
  126.9 0.0 collective-permute-start.23
  126.9 1.3 collective-permute-done.22
  128.2 2.9 %collective-permute-done.23 = f32[128,128]{1,0:T(8,128)S(1)} collective-permute-done((f32[128,128]{1,0:T(8,128)S(1)}, f32[128,128]{1,0:T(8,128)S(1)}, u32[]{:S(2)}, u32[]{:S(2)}) %collective-permute-start.23) | collective-permute-done | bytes 65568 | tf_op jit(solution)/shard_map/ppermute | solution.py:267
  131.2 0.6 add_add_fusion
  131.8 5.3 %shard_map.150 = (bf16[128,2048]{1,0:T(8,128)(2,1)}, bf16[128,2048]{1,0:T(8,128)(2,1)}) custom-call(s32[4]{0:T(128)S(1)} %copy-done.13, s32[1]{0:T(128)} %bitcast.start, bf16[128,2048]{1,0:T(8,128)(2,1)S(1)} %get-tuple-element.39.grad_signal, bf16[128,2048]{1,0:T(8,128)(2,1)S(1)} %collective-permute-done.15.right, bf16[128,2048]{1,0:T(8,128)(2,1)S(1)} %copy-done.10, ...), custom_call_target="tpu_custom_call" | custom-call | flops 1073741824 | bytes 3276820 | tf_op jit(solution)/shard_map/pallas_call | solution.py:42
  137.2 1.0 add_convert_fusion
  (34 shorter events, 0.1 us)
Async XLA Ops:
  0.6 43.4 %copy-start.13 = (s32[4]{0:T(128)S(1)}, s32[4]{0:T(128)}, u32[]{:S(2)}) copy-start(s32[4]{0:T(128)} %lengths.7) | copy-start | bytes 52
  0.6 43.1 %copy-start.14 = (bf16[128,128]{1,0:T(8,128)(2,1)S(1)}, bf16[128,128]{1,0:T(8,128)(2,1)}, u32[]{:S(2)}) copy-start(bf16[128,128]{1,0:T(8,128)(2,1)} %param.12) | copy-start | bytes 98308
  0.7 43.4 %copy-start = (bf16[128,2048]{1,0:T(8,128)(2,1)S(1)}, bf16[128,2048]{1,0:T(8,128)(2,1)}, u32[]{:S(2)}) copy-start(bf16[128,2048]{1,0:T(8,128)(2,1)} %hyena_q.7) | copy-start | bytes 1572868
  0.7 17.5 %collective-permute-start = (bf16[128,2048]{1,0:T(8,128)(2,1)}, bf16[128,2048]{1,0:T(8,128)(2,1)S(1)}, u32[]{:S(2)}, u32[]{:S(2)}) collective-permute-start(bf16[128,2048]{1,0:T(8,128)(2,1)} %k0.3), channel_id=1, source_target_pairs={{0,4},{4,8},{8,12},{12,16},{16,20},{20,24},{24,28},{28,32},{32,36}... | collective-permute-start | bytes 1572872 | tf_op jit(solution)/shard_map/ppermute | solution.py:26
  2.7 21.0 %collective-permute-start.1 = (bf16[128,2048]{1,0:T(8,128)(2,1)}, bf16[128,2048]{1,0:T(8,128)(2,1)S(1)}, u32[]{:S(2)}, u32[]{:S(2)}) collective-permute-start(bf16[128,2048]{1,0:T(8,128)(2,1)} %k0.3), channel_id=1, source_target_pairs={{0,8},{4,12},{8,16},{12,20},{16,24},{20,28},{24,32},{28,36},{32,40... | collective-permute-start | bytes 1572872 | tf_op jit(solution)/shard_map/ppermute | solution.py:26
  8.7 35.3 %collective-permute-start.2 = (bf16[128,2048]{1,0:T(8,128)(2,1)}, bf16[128,2048]{1,0:T(8,128)(2,1)}, u32[]{:S(2)}, u32[]{:S(2)}) collective-permute-start(bf16[128,2048]{1,0:T(8,128)(2,1)} %multiply_convert_fusion.kv), channel_id=1, source_target_pairs={{0,4},{4,8},{8,12},{12,16},{16,20},{20,24},{24,28},{28,32},{32,36}... | collective-permute-start | bytes 1572872 | tf_op jit(solution)/shard_map/ppermute | solution.py:26
  23.7 1.0 copy-start.3
  24.8 1.0 copy-start.5
  25.8 1.0 copy-start.7
  26.9 0.7 copy-start.12
  27.5 30.0 %copy-start.11 = (f32[2048]{0:T(1024)S(1)}, f32[2048]{0:T(1024)}, u32[]{:S(2)}) copy-start(f32[2048]{0:T(1024)} %param.13) | copy-start | bytes 24580
  32.7 1.6 %copy-start.1 = (f32[16,384,128]{2,1,0:T(8,128)}, f32[16,384,128]{2,1,0:T(8,128)S(1)}, u32[]{:S(2)}) copy-start(f32[16,384,128]{2,1,0:T(8,128)S(1)} %get-tuple-element.25.prob) | copy-start | bytes 9437188
  34.3 28.5 %collective-permute-start.10 = (bf16[128,2048]{1,0:T(8,128)(2,1)}, bf16[128,2048]{1,0:T(8,128)(2,1)S(1)}, u32[]{:S(2)}, u32[]{:S(2)}) collective-permute-start(bf16[128,2048]{1,0:T(8,128)(2,1)} %get-tuple-element.34), channel_id=1, source_target_pairs={{4,0},{8,4},{12,8},{16,12},{20,16},{24,20},{28,24},{32,28},{36,32}... | collective-permute-start | bytes 1572872 | tf_op jit(solution)/shard_map/ppermute | solution.py:26
  40.8 22.0 %collective-permute-start.11 = (bf16[128,2048]{1,0:T(8,128)(2,1)}, bf16[128,2048]{1,0:T(8,128)(2,1)}, u32[]{:S(2)}, u32[]{:S(2)}) collective-permute-start(bf16[128,2048]{1,0:T(8,128)(2,1)} %get-tuple-element.35), channel_id=1, source_target_pairs={{8,0},{12,4},{16,8},{20,12},{24,16},{28,20},{32,24},{36,28},{40,32... | collective-permute-start | bytes 1572872 | tf_op jit(solution)/shard_map/ppermute | solution.py:26
  49.4 6.5 %collective-permute-start.3 = (f32[8,128]{1,0:T(8,128)S(1)}, f32[8,128]{1,0:T(8,128)S(1)}, u32[]{:S(2)}, u32[]{:S(2)}) collective-permute-start(f32[8,128]{1,0:T(8,128)S(1)} %get-tuple-element.27.s0), channel_id=1, source_target_pairs={{0,2},{1,3},{2,0},{3,1},{4,6},{5,7},{6,4},{7,5},{8,10},{9,11},{10,... | collective-permute-start | bytes 12296 | tf_op jit(solution)/shard_map/ppermute | solution.py:34
  52.6 4.8 %collective-permute-start.4 = (f32[8,128]{1,0:T(8,128)S(1)}, f32[8,128]{1,0:T(8,128)S(1)}, u32[]{:S(2)}, u32[]{:S(2)}) collective-permute-start(f32[8,128]{1,0:T(8,128)S(1)} %get-tuple-element.27.s0), channel_id=1, source_target_pairs={{0,1},{1,2},{2,3},{3,0},{4,5},{5,6},{6,7},{7,4},{8,9},{9,10},{10,1... | collective-permute-start | bytes 12296 | tf_op jit(solution)/shard_map/ppermute | solution.py:34
  53.3 4.1 %collective-permute-start.5 = (f32[8,128]{1,0:T(8,128)S(1)}, f32[8,128]{1,0:T(8,128)S(1)}, u32[]{:S(2)}, u32[]{:S(2)}) collective-permute-start(f32[8,128]{1,0:T(8,128)S(1)} %get-tuple-element.27.s0), channel_id=1, source_target_pairs={{0,3},{1,0},{2,1},{3,2},{4,7},{5,4},{6,5},{7,6},{8,11},{9,8},{10,9... | collective-permute-start | bytes 12296 | tf_op jit(solution)/shard_map/ppermute | solution.py:34
  58.0 35.7 %collective-permute-start.6 = (bf16[128,2048]{1,0:T(8,128)(2,1)S(1)}, bf16[128,2048]{1,0:T(8,128)(2,1)S(1)}, u32[]{:S(2)}, u32[]{:S(2)}) collective-permute-start(bf16[128,2048]{1,0:T(8,128)(2,1)S(1)} %shard_map.146.v0), channel_id=1, source_target_pairs={{0,4},{4,8},{8,12},{12,16},{16,20},{20,24},{24,28},{28,32},{32,36}... | collective-permute-start | bytes 1572872 | tf_op jit(solution)/shard_map/ppermute | solution.py:26
  59.9 33.8 %collective-permute-start.7 = (bf16[128,2048]{1,0:T(8,128)(2,1)S(1)}, bf16[128,2048]{1,0:T(8,128)(2,1)S(1)}, u32[]{:S(2)}, u32[]{:S(2)}) collective-permute-start(bf16[128,2048]{1,0:T(8,128)(2,1)S(1)} %shard_map.146.v0), channel_id=1, source_target_pairs={{0,8},{4,12},{8,16},{12,20},{16,24},{20,28},{24,32},{28,36},{32,40... | collective-permute-start | bytes 1572872 | tf_op jit(solution)/shard_map/ppermute | solution.py:26
  64.8 5.2 %collective-permute-start.12 = (f32[8,128]{1,0:T(8,128)S(1)}, f32[8,128]{1,0:T(8,128)S(1)}, u32[]{:S(2)}, u32[]{:S(2)}) collective-permute-start(f32[8,128]{1,0:T(8,128)S(1)} %get-tuple-element.37.i0), channel_id=1, source_target_pairs={{0,2},{1,3},{2,0},{3,1},{4,6},{5,7},{6,4},{7,5},{8,10},{9,11},{10,... | collective-permute-start | bytes 12296 | tf_op jit(solution)/shard_map/ppermute | solution.py:34
  66.3 4.8 %collective-permute-start.13 = (f32[8,128]{1,0:T(8,128)S(1)}, f32[8,128]{1,0:T(8,128)S(1)}, u32[]{:S(2)}, u32[]{:S(2)}) collective-permute-start(f32[8,128]{1,0:T(8,128)S(1)} %get-tuple-element.37.i0), channel_id=1, source_target_pairs={{0,1},{1,2},{2,3},{3,0},{4,5},{5,6},{6,7},{7,4},{8,9},{9,10},{10,1... | collective-permute-start | bytes 12296 | tf_op jit(solution)/shard_map/ppermute | solution.py:34
  68.9 3.6 %collective-permute-start.14 = (f32[8,128]{1,0:T(8,128)S(1)}, f32[8,128]{1,0:T(8,128)S(1)}, u32[]{:S(2)}, u32[]{:S(2)}) collective-permute-start(f32[8,128]{1,0:T(8,128)S(1)} %get-tuple-element.37.i0), channel_id=1, source_target_pairs={{0,3},{1,0},{2,1},{3,2},{4,7},{5,4},{6,5},{7,6},{8,11},{9,8},{10,9... | collective-permute-start | bytes 12296 | tf_op jit(solution)/shard_map/ppermute | solution.py:34
  72.5 21.1 %copy-start.2 = (f32[16,384,128]{2,1,0:T(8,128)S(1)}, f32[16,384,128]{2,1,0:T(8,128)}, u32[]{:S(2)}) copy-start(f32[16,384,128]{2,1,0:T(8,128)} %copy-done.1) | copy-start | bytes 9437188
  72.5 21.1 %copy-start.4 = (bf16[128,2048]{1,0:T(8,128)(2,1)S(1)}, bf16[128,2048]{1,0:T(8,128)(2,1)}, u32[]{:S(2)}) copy-start(bf16[128,2048]{1,0:T(8,128)(2,1)} %q.3) | copy-start | bytes 1572868
  72.5 21.1 %copy-start.6 = (bf16[128,2048]{1,0:T(8,128)(2,1)S(1)}, bf16[128,2048]{1,0:T(8,128)(2,1)}, u32[]{:S(2)}) copy-start(bf16[128,2048]{1,0:T(8,128)(2,1)} %k0.3) | copy-start | bytes 1572868
  72.5 21.1 %copy-start.8 = (bf16[128,2048]{1,0:T(8,128)(2,1)S(1)}, bf16[128,2048]{1,0:T(8,128)(2,1)}, u32[]{:S(2)}) copy-start(bf16[128,2048]{1,0:T(8,128)(2,1)} %og.3) | copy-start | bytes 1572868
  80.6 1.3 collective-permute-start.16
  81.9 5.9 %collective-permute-start.17 = (f32[128,128]{1,0:T(8,128)S(1)}, f32[128,128]{1,0:T(8,128)S(1)}, u32[]{:S(2)}, u32[]{:S(2)}) collective-permute-start(f32[128,128]{1,0:T(8,128)S(1)} %add.38), channel_id=1, source_target_pairs={{0,128},{8,136},{16,144},{24,152},{32,160},{40,168},{48,176},{56,1... | collective-permute-start | bytes 196616 | tf_op jit(solution)/shard_map/ppermute | solution.py:267
  83.1 8.4 %collective-permute-start.18 = (f32[128,128]{1,0:T(8,128)S(1)}, f32[128,128]{1,0:T(8,128)S(1)}, u32[]{:S(2)}, u32[]{:S(2)}) collective-permute-start(f32[128,128]{1,0:T(8,128)S(1)} %add.38), channel_id=1, source_target_pairs={{0,64},{8,72},{16,80},{24,88},{32,96},{40,104},{48,112},{56,120},{... | collective-permute-start | bytes 196616 | tf_op jit(solution)/shard_map/ppermute | solution.py:267
  85.2 6.3 %collective-permute-start.19 = (f32[128,128]{1,0:T(8,128)S(1)}, f32[128,128]{1,0:T(8,128)S(1)}, u32[]{:S(2)}, u32[]{:S(2)}) collective-permute-start(f32[128,128]{1,0:T(8,128)S(1)} %add.38), channel_id=1, source_target_pairs={{0,192},{8,200},{16,208},{24,216},{32,224},{40,232},{48,240},{56,2... | collective-permute-start | bytes 196616 | tf_op jit(solution)/shard_map/ppermute | solution.py:267
  87.8 44.0 %collective-permute-start.15 = (bf16[128,2048]{1,0:T(8,128)(2,1)S(1)}, bf16[128,2048]{1,0:T(8,128)(2,1)S(1)}, u32[]{:S(2)}, u32[]{:S(2)}) collective-permute-start(bf16[128,2048]{1,0:T(8,128)(2,1)S(1)} %get-tuple-element.39.grad_signal), channel_id=1, source_target_pairs={{4,0},{8,4},{12,8},{16,12},{20,16},{24,20},{28,24},{32,28},{36,32}... | collective-permute-start | bytes 1572872 | tf_op jit(solution)/shard_map/ppermute | solution.py:26
  91.6 13.1 %collective-permute-start.20 = (f32[128,128]{1,0:T(8,128)S(1)}, f32[128,128]{1,0:T(8,128)S(1)}, u32[]{:S(2)}, u32[]{:S(2)}) collective-permute-start(f32[128,128]{1,0:T(8,128)S(1)} %add_add_fusion.1), channel_id=1, source_target_pairs={{0,32},{8,40},{16,48},{24,56},{32,0},{40,8},{48,16},{56,24},{64,96... | collective-permute-start | bytes 196616 | tf_op jit(solution)/shard_map/ppermute | solution.py:267
  93.7 38.1 %copy-start.9 = (bf16[128,2048]{1,0:T(8,128)(2,1)S(1)}, bf16[128,2048]{1,0:T(8,128)(2,1)}, u32[]{:S(2)}) copy-start(bf16[128,2048]{1,0:T(8,128)(2,1)} %hyena_v.1) | copy-start | bytes 1572868
  93.7 38.1 %copy-start.10 = (bf16[128,2048]{1,0:T(8,128)(2,1)S(1)}, bf16[128,2048]{1,0:T(8,128)(2,1)}, u32[]{:S(2)}) copy-start(bf16[128,2048]{1,0:T(8,128)(2,1)} %hyena_k.1) | copy-start | bytes 1572868
  100.0 37.2 %collective-permute-start.8 = (bf16[128,2048]{1,0:T(8,128)(2,1)S(1)}, bf16[128,2048]{1,0:T(8,128)(2,1)S(1)}, u32[]{:S(2)}, u32[]{:S(2)}) collective-permute-start(bf16[128,2048]{1,0:T(8,128)(2,1)S(1)} %get-tuple-element.31), channel_id=1, source_target_pairs={{4,0},{8,4},{12,8},{16,12},{20,16},{24,20},{28,24},{32,28},{36,32}... | collective-permute-start | bytes 1572872 | tf_op jit(solution)/shard_map/ppermute | solution.py:26
  102.6 34.6 %collective-permute-start.9 = (bf16[128,2048]{1,0:T(8,128)(2,1)S(1)}, bf16[128,2048]{1,0:T(8,128)(2,1)S(1)}, u32[]{:S(2)}, u32[]{:S(2)}) collective-permute-start(bf16[128,2048]{1,0:T(8,128)(2,1)S(1)} %get-tuple-element.32), channel_id=1, source_target_pairs={{8,0},{12,4},{16,8},{20,12},{24,16},{28,20},{32,24},{36,28},{40,32... | collective-permute-start | bytes 1572872 | tf_op jit(solution)/shard_map/ppermute | solution.py:26
  104.8 22.2 %collective-permute-start.21 = (f32[128,128]{1,0:T(8,128)S(1)}, f32[128,128]{1,0:T(8,128)S(1)}, u32[]{:S(2)}, u32[]{:S(2)}) collective-permute-start(f32[128,128]{1,0:T(8,128)S(1)} %add.42), channel_id=1, source_target_pairs={{0,24},{8,16},{16,8},{24,0},{32,56},{40,48},{48,40},{56,32},{64,88... | collective-permute-start | bytes 196616 | tf_op jit(solution)/shard_map/ppermute | solution.py:267
  107.7 20.5 %collective-permute-start.22 = (f32[128,128]{1,0:T(8,128)S(1)}, f32[128,128]{1,0:T(8,128)S(1)}, u32[]{:S(2)}, u32[]{:S(2)}) collective-permute-start(f32[128,128]{1,0:T(8,128)S(1)} %add.42), channel_id=1, source_target_pairs={{0,16},{8,24},{16,0},{24,8},{32,48},{40,56},{48,32},{56,40},{64,80... | collective-permute-start | bytes 196616 | tf_op jit(solution)/shard_map/ppermute | solution.py:267
  126.9 4.3 %collective-permute-start.23 = (f32[128,128]{1,0:T(8,128)S(1)}, f32[128,128]{1,0:T(8,128)S(1)}, u32[]{:S(2)}, u32[]{:S(2)}) collective-permute-start(f32[128,128]{1,0:T(8,128)S(1)} %add.42), channel_id=1, source_target_pairs={{0,8},{8,0},{16,24},{24,16},{32,40},{40,32},{48,56},{56,48},{64,72... | collective-permute-start | bytes 196616 | tf_op jit(solution)/shard_map/ppermute | solution.py:267

commit v3 on v2

--- a/solution.py
+++ b/solution.py
@@ -22,7 +22,7 @@
 
 def shifted(block, distance):
     count = lax.axis_size(SEQ_AXES)
-    route = [(i - distance, i) for i in range(count) if 0 <= i - distance < count]
+    route = [(i, (i + distance) % count) for i in range(count)]
     return lax.ppermute(block, SEQ_AXES, route)
 
 
@@ -62,22 +62,33 @@
     return doc
 
 
-def conv_mask(lengths, own, first, sign=1):
-    rows = own + lax.broadcasted_iota(jnp.int32, (T, 2 * T), 0)
-    cols = first + sign * lax.broadcasted_iota(jnp.int32, (T, 2 * T), 1)
-    return doc_of(lengths, rows) == doc_of(lengths, cols)
+def same_doc(lengths, own, cols):
+    rows = own + lax.broadcasted_iota(jnp.int32, (T, T), 0)
+    return (doc_of(lengths, rows) == doc_of(lengths, cols)) & (cols >= 0)
+
+
+def half_masks(lengths, own, first):
+    t = lax.broadcasted_iota(jnp.int32, (T, T), 0)
+    l = lax.broadcasted_iota(jnp.int32, (T, T), 1)
+    low, high = (l > t, l <= t) if first != 0 else (l >= t, l < t)
+    masks = []
+    for half, base in ((low, own + first), (high, own + first + T)):
+        keep = half & same_doc(lengths, own, base + l)
+        masks.append(jnp.where(keep, 1.0, 0.0).astype(BF16))
+    return masks
 
 
 def column(row):
     return jnp.transpose(jnp.broadcast_to(row, (T, LANES)))
 
 
-def banded_matmul(table_ref, mask, window, tile):
+def banded_matmul(table_ref, masks, window, tile):
     bands = []
     for g in range(LANES // GROUP):
         row = table_ref[pl.ds(tile * 8 + g, 1), :]
-        band = pltpu.roll(jnp.broadcast_to(row, (T, 2 * T)), 0, 1, stride=1, stride_axis=0)
-        bands.append(jnp.where(mask, band, 0.0).astype(BF16))
+        turned = pltpu.roll(jnp.broadcast_to(row, (T, T)), 0, 1, stride=1, stride_axis=0)
+        turned = turned.astype(BF16)
+        bands.append(jnp.concatenate([turned * masks[0], turned * masks[1]], axis=1))
     stacked = jnp.concatenate(bands, axis=0)
     full = jnp.dot(stacked, window, preferred_element_type=F32)
     lane_group = lax.broadcasted_iota(jnp.int32, (T, LANES), 1) // GROUP
@@ -97,7 +108,7 @@
         jnp.int32, (span, span), 1
     )
     turn = jnp.where(turned == span - 1, 1.0, 0.0).astype(BF16)
-    mask = conv_mask(lengths, start[0], start[0] - T)
+    mask = half_masks(lengths, start[0], -T)
     tiles = kv.shape[1] // LANES
 
     def step(tile, acc):
@@ -132,7 +143,7 @@
     lax.fori_loop(0, signal.shape[1] // LANES, step, 0, unroll=UNROLL)
 
 
-def scores_body(lengths, start, q, k0, k1, k2, og, prob, own, part1, part2):
+def scores_body(lengths, start, q, k0, k1, k2, og, prob, own, lse):
     span = 3 * T
     query_pos = start[0] + lax.broadcasted_iota(jnp.int32, (span, T), 1)
     key_pos = start[0] - 2 * T + lax.broadcasted_iota(jnp.int32, (span, T), 0)
@@ -151,26 +162,41 @@
         s = jnp.where(allowed, s * scale, -1e30)
         top = jnp.max(s, axis=0, keepdims=True)
         e = jnp.exp(s - top)
-        p = e * (1.0 / jnp.sum(e, axis=0, keepdims=True))
+        total = jnp.sum(e, axis=0, keepdims=True)
+        p = e * (1.0 / total)
         prob[h] = p
-        part = jnp.dot(p.astype(BF16), og[:, at], preferred_element_type=F32)
-        part2[:, at] = part[:T].astype(BF16)
-        part1[:, at] = part[T : 2 * T].astype(BF16)
-        own[:, at] = part[2 * T :]
+        lse[pl.ds(h, 1), :] = top + jnp.log(total)
+        own[:, at] = jnp.dot(p[2 * T :].astype(BF16), og[:, at], preferred_element_type=F32)
         return 0
 
     lax.fori_loop(0, q.shape[1] // HEAD, step, 0, unroll=UNROLL)
 
 
-def inner_body(own, part1, part2, signal, hyena_q, gain, grad_values, inner):
-    def step(tile, acc):
-        at = lanes_of(tile)
-        gv = own[:, at] + part1[:, at].astype(F32) + part2[:, at].astype(F32)
+def later_body(
+    lengths, start, k0, q1, q2, og1, og2, lse1, lse2, own, signal, hyena_q, gain, prob, grad_values, inner
+):
+    span = 2 * T
+    query_pos = start[0] + T + lax.broadcasted_iota(jnp.int32, (T, span), 1)
+    key_pos = start[0] + lax.broadcasted_iota(jnp.int32, (T, span), 0)
+    allowed = (query_pos - key_pos <= 2 * T) & (
+        doc_of(lengths, key_pos) == doc_of(lengths, query_pos)
+    )
+    scale = HEAD**-0.5
+
+    def step(h, acc):
+        at = lanes_of(h)
+        queries = jnp.concatenate([q1[:, at], q2[:, at]], axis=0)
+        grads = jnp.concatenate([og1[:, at], og2[:, at]], axis=0)
+        row = jnp.concatenate([lse1[pl.ds(h, 1), :], lse2[pl.ds(h, 1), :]], axis=1)
+        s = lax.dot_general(k0[:, at], queries, (((1,), (1,)), ((), ())), preferred_element_type=F32)
+        p = jnp.exp(jnp.where(allowed, s * scale - row, -1e30))
+        prob[h] = p
+        gv = own[:, at] + jnp.dot(p.astype(BF16), grads, preferred_element_type=F32)
         gv = gv * gain[:, at]
         grad_values[:, at] = gv
         return acc + gv * (hyena_q[:, at].astype(F32) * signal[:, at])
 
-    acc = lax.fori_loop(0, own.shape[1] // LANES, step, jnp.zeros((T, LANES), F32), unroll=UNROLL)
+    acc = lax.fori_loop(0, own.shape[1] // HEAD, step, jnp.zeros((T, LANES), F32), unroll=UNROLL)
     inner[...] = jnp.broadcast_to(jnp.sum(jnp.transpose(acc), axis=0, keepdims=True), (8, LANES))
 
 
@@ -195,7 +221,10 @@
 
 
 def filter_body(lengths, start, flipped, grad_signal, out):
-    mask = conv_mask(lengths, start[0], start[0] + T - 1, -1)
+    t = lax.broadcasted_iota(jnp.int32, (T, T), 0)
+    l = lax.broadcasted_iota(jnp.int32, (T, T), 1)
+    own = l >= T - 1 - t
+    mask = same_doc(lengths, start[0], start[0] - 1 - l + jnp.where(own, T, 0))
     lane_group = lax.broadcasted_iota(jnp.int32, (T, LANES), 1) // GROUP
     count = LANES // GROUP
 
@@ -210,9 +239,10 @@
         )
         rows = []
         for g in range(count):
-            corr = jnp.where(mask, full[g * T : (g + 1) * T], 0.0)
-            aligned = pltpu.roll(corr, T + 1, 1, stride=1, stride_axis=0)
-            rows.append(jnp.sum(aligned[:, :LANES], axis=0, keepdims=True))
+            corr = full[g * T : (g + 1) * T]
+            corr = jnp.where(mask, jnp.where(own, corr[:, :T], corr[:, T:]), 0.0)
+            aligned = pltpu.roll(corr, 1, 1, stride=1, stride_axis=0)
+            rows.append(jnp.sum(aligned, axis=0, keepdims=True))
         out[pl.ds(pl.multiple_of(tile * 8, 8), 8), :] = jnp.concatenate(rows, axis=0)
         return 0
 
@@ -220,7 +250,7 @@
 
 
 def conv_back_body(lengths, start, grad_signal, right, hyena_k, hyena_v, table, grad_k, grad_v):
-    mask = conv_mask(lengths, start[0], start[0])
+    mask = half_masks(lengths, start[0], 0)
 
     def step(tile, _):
         at = lanes_of(tile)
@@ -234,7 +264,7 @@
 
 
 def attend_body(
-    prob, q, k0, k1, k2, v0, v1, v2, og, attn_out, grad_q, own, part1, part2
+    prob, q, k0, k1, k2, v0, v1, v2, og, attn_out, grad_q, own, delta_rows
 ):
     scale = HEAD**-0.5
     over_keys = (((0,), (0,)), ((), ()))
@@ -246,6 +276,7 @@
         p = prob[h]
         gp = lax.dot_general(vals, og[:, at], (((1,), (1,)), ((), ())), preferred_element_type=F32)
         delta = jnp.sum(p * gp, axis=0, keepdims=True)
+        delta_rows[pl.ds(h, 1), :] = delta
         gs = (p * (gp - delta) * scale).astype(BF16)
         attn_out[:, at] = lax.dot_general(
             p.astype(BF16), vals, over_keys, preferred_element_type=F32
@@ -253,13 +284,27 @@
         grad_q[:, at] = lax.dot_general(
             gs, keys, over_keys, preferred_element_type=F32
         ).astype(BF16)
-        part = jnp.dot(gs, q[:, at], preferred_element_type=F32)
-        part2[:, at] = part[:T].astype(BF16)
-        part1[:, at] = part[T : 2 * T].astype(BF16)
-        own[:, at] = part[2 * T :]
+        own[:, at] = jnp.dot(gs[2 * T :], q[:, at], preferred_element_type=F32)
         return 0
 
     lax.fori_loop(0, q.shape[1] // HEAD, step, 0, unroll=UNROLL)
+
+
+def keys_body(prob, v0, q1, q2, og1, og2, delta1, delta2, own, grad_k):
+    scale = HEAD**-0.5
+
+    def step(h, _):
+        at = lanes_of(h)
+        queries = jnp.concatenate([q1[:, at], q2[:, at]], axis=0)
+        grads = jnp.concatenate([og1[:, at], og2[:, at]], axis=0)
+        delta = jnp.concatenate([delta1[pl.ds(h, 1), :], delta2[pl.ds(h, 1), :]], axis=1)
+        gp = lax.dot_general(v0[:, at], grads, (((1,), (1,)), ((), ())), preferred_element_type=F32)
+        gs = (prob[h] * (gp - delta) * scale).astype(BF16)
+        part = jnp.dot(gs, queries, preferred_element_type=F32)
+        grad_k[:, at] = (own[:, at] + part).astype(BF16)
+        return 0
+
+    lax.fori_loop(0, v0.shape[1] // HEAD, step, 0, unroll=UNROLL)
 
 
 def over_sequence(x):
@@ -289,54 +334,57 @@
 
     kv = (hyena_k.astype(F32) * hyena_v.astype(F32)).astype(BF16)
     left = shifted(kv, 1)
+    og2 = shifted(out_grad, -2)
+    q2 = shifted(attn_q, -2)
+    og1 = shifted(out_grad, -1)
+    q1 = shifted(attn_q, -1)
     k2 = shifted(attn_k, 2)
     k1 = shifted(attn_k, 1)
     groups = filters.shape[0]
     taps = filters.astype(F32)
-    back_table = jnp.concatenate([taps, jnp.zeros((groups, T), F32)], axis=1)
-    fwd_table = jnp.concatenate(
-        [jnp.zeros((groups, 1), F32), taps[:, ::-1], jnp.zeros((groups, T - 1), F32)], axis=1
-    )
+    fwd_taps = jnp.concatenate([taps[:, :1], taps[:, :0:-1]], axis=1)
     signal, square, flipped = call(
         conv_body,
-        (*at, left, kv, hyena_q, fwd_table),
+        (*at, left, kv, hyena_q, fwd_taps),
         (wide, small, sds(2 * rows, channels, dtype=BF16)),
         band_flops,
         8,
     )
     squares = across(square)
-    prob, value_own, value1, value2 = call(
+    stat = sds(heads, T)
+    prob, value_own, lse = call(
         scores_body,
         (*at, attn_q, attn_k, k1, k2, out_grad),
-        (sds(heads, 3 * T, T), wide, half, half),
-        2 * attn_flops,
+        (sds(heads, 3 * T, T), wide, stat),
+        4 * attn_flops // 3,
         16,
         exps=heads * 3 * T * T,
     )
-    back2 = shifted(value2, -2)
-    back1 = shifted(value1, -1)
+    lse2 = shifted(lse, -2)
+    lse1 = shifted(lse, -1)
     (values,) = call(
         values_body, (signal, hyena_q, gain, *squares), (half,), 4 * rows * channels, 8
     )
     v2 = shifted(values, 2)
     v1 = shifted(values, 1)
-    gain_grad, inner = call(
-        inner_body,
-        (value_own, back1, back2, signal, hyena_q, gain),
-        (wide, small),
-        6 * rows * channels,
-        10,
+    prob_later, gain_grad, inner = call(
+        later_body,
+        (*at, attn_k, q1, q2, og1, og2, lse1, lse2, value_own, signal, hyena_q, gain),
+        (sds(heads, T, 2 * T), wide, small),
+        4 * attn_flops // 3,
+        14,
+        exps=heads * 2 * T * T,
     )
     inners = across(inner)
-    attn_out, grad_attn_q, key_own, key1, key2 = call(
+    attn_out, grad_attn_q, key_own, delta = call(
         attend_body,
         (prob, attn_q, attn_k, k1, k2, values, v1, v2, out_grad),
-        (half, half, wide, half, half),
-        4 * attn_flops,
+        (half, half, wide, stat),
+        10 * attn_flops // 3,
         16,
     )
-    from2 = shifted(key2, -2)
-    from1 = shifted(key1, -1)
+    delta2 = shifted(delta, -2)
+    delta1 = shifted(delta, -1)
     grad_hyena_q, grad_signal = call(
         signal_grad_body,
         (gain_grad, signal, hyena_q, *squares, *inners),
@@ -347,10 +395,16 @@
     right = shifted(grad_signal, -1)
     (local,) = call(filter_body, (*at, flipped, grad_signal), (sds(groups, LANES),), band_flops, 10)
     grad_filters = over_sequence(local)
-    grad_attn_k = (key_own + from1.astype(F32) + from2.astype(F32)).astype(BF16)
+    (grad_attn_k,) = call(
+        keys_body,
+        (prob_later, values, q1, q2, og1, og2, delta1, delta2, key_own),
+        (half,),
+        4 * attn_flops // 3,
+        12,
+    )
     grad_hyena_k, grad_hyena_v = call(
         conv_back_body,
-        (*at, grad_signal, right, hyena_k, hyena_v, back_table),
+        (*at, grad_signal, right, hyena_k, hyena_v, taps),
         (half, half),
         band_flops,
         10,

time: 139 us -> 124 us (0.89)
  the two profiles are of different devices: /device:TPU:6 before, /device:TPU:1 now
where the time goes in v3:
time: 124 us
  starting transfers between devices  47.1 us (38%)
  Pallas kernels  34.3 us (28%)
  waiting for transfers between devices  33.3 us (27%)
  local copies, waits for them, and re-layouts  5.49 us (4%)
  other arithmetic  2.9 us (2%)
    pallas_call x9, Pallas kernels, call(): pl.pallas_call(body, out_shape=tuple(outs), in_specs=specs, out_specs=tup...  34.3 us
    ppermute x14, starting transfers between devices, shifted(): return lax.ppermute(block, SEQ_AXES, route)  25.6 us
    ppermute x7, waiting for transfers between devices, send(): lax.ppermute(x, 'context', [(i, f(i // 8, i % 8)) for i in range(32)])  22.3 us
    ppermute x7, starting transfers between devices, send(): lax.ppermute(x, 'context', [(i, f(i // 8, i % 8)) for i in range(32)])  9.43 us
    ppermute x14, waiting for transfers between devices, shifted(): return lax.ppermute(block, SEQ_AXES, route)  8.81 us
    ppermute x6, starting transfers between devices, across(): others.append(lax.ppermute(block, 'tensor', route))  8.71 us
    unnamed x26, local copies, waits for them, and re-layouts  3.82 us
    ppermute x1, starting transfers between devices, over_sequence(): x = x + lax.ppermute(x, 'mirror', [(0, 1), (1, 0)])  3.38 us
  transfers between devices with their start and end apart: 28, of which 8 were waited for; matrix products, arithmetic and copies ran while one was open for 4% of the time, Pallas kernels for 20%

profile of v3, /device:TPU:1, one launch (start us, length us, event | category | flops | bytes accessed | tf_op | source)
XLA Modules:
  0.0 124.0 jit_solution(7568147257539068215)
XLA Ops:
  0.6 3.1 %collective-permute-start = (bf16[128,2048]{1,0:T(8,128)(2,1)}, bf16[128,2048]{1,0:T(8,128)(2,1)S(1)}, u32[]{:S(2)}, u32[]{:S(2)}) collective-permute-start(bf16[128,2048]{1,0:T(8,128)(2,1)} %k0.5), channel_id=1, source_target_pairs={{0,4},{4,8},{8,12},{12,16},{16,20},{20,24},{24,28},{28,32},{32,36}... | collective-permute-start | bytes 1572872 | tf_op jit(solution)/shard_map/ppermute | solution.py:26
  3.7 1.6 %collective-permute-start.1 = (bf16[128,2048]{1,0:T(8,128)(2,1)}, bf16[128,2048]{1,0:T(8,128)(2,1)S(1)}, u32[]{:S(2)}, u32[]{:S(2)}) collective-permute-start(bf16[128,2048]{1,0:T(8,128)(2,1)} %k0.5), channel_id=1, source_target_pairs={{0,8},{4,12},{8,16},{12,20},{16,24},{20,28},{24,32},{28,36},{32,40... | collective-permute-start | bytes 1572872 | tf_op jit(solution)/shard_map/ppermute | solution.py:26
  5.4 2.1 %multiply_convert_fusion.kv = bf16[128,2048]{1,0:T(8,128)(2,1)} fusion(bf16[128,2048]{1,0:T(8,128)(2,1)} %hyena_v.1, bf16[128,2048]{1,0:T(8,128)(2,1)} %hyena_k.1), kind=kLoop, calls=%fused_computation | loop fusion | flops 1048576 | bytes 1572864 | tf_op jit(solution)/shard_map/convert_element_type | solution.py:335
  7.5 0.4 collective-permute-start.2
  7.9 0.1 collective-permute-start.8
  8.0 4.2 %collective-permute-start.9 = (bf16[128,2048]{1,0:T(8,128)(2,1)}, bf16[128,2048]{1,0:T(8,128)(2,1)S(1)}, u32[]{:S(2)}, u32[]{:S(2)}) collective-permute-start(bf16[128,2048]{1,0:T(8,128)(2,1)} %q.3), channel_id=1, source_target_pairs={{0,248},{4,252},{8,0},{12,4},{16,8},{20,12},{24,16},{28,20},{32,24... | collective-permute-start | bytes 1572872 | tf_op jit(solution)/shard_map/ppermute | solution.py:26
  12.2 2.9 %collective-permute-done.k1 = bf16[128,2048]{1,0:T(8,128)(2,1)S(1)} collective-permute-done((bf16[128,2048]{1,0:T(8,128)(2,1)}, bf16[128,2048]{1,0:T(8,128)(2,1)S(1)}, u32[]{:S(2)}, u32[]{:S(2)}) %collective-permute-start) | collective-permute-done | bytes 524320 | tf_op jit(solution)/shard_map/ppermute | solution.py:26
  15.1 6.3 %collective-permute-start.10 = (bf16[128,2048]{1,0:T(8,128)(2,1)}, bf16[128,2048]{1,0:T(8,128)(2,1)S(1)}, u32[]{:S(2)}, u32[]{:S(2)}) collective-permute-start(bf16[128,2048]{1,0:T(8,128)(2,1)} %og.3), channel_id=1, source_target_pairs={{0,252},{4,0},{8,4},{12,8},{16,12},{20,16},{24,20},{28,24},{32,28}... | collective-permute-start | bytes 1572872 | tf_op jit(solution)/shard_map/ppermute | solution.py:26
  21.4 5.9 %collective-permute-done.1.k2 = bf16[128,2048]{1,0:T(8,128)(2,1)S(1)} collective-permute-done((bf16[128,2048]{1,0:T(8,128)(2,1)}, bf16[128,2048]{1,0:T(8,128)(2,1)S(1)}, u32[]{:S(2)}, u32[]{:S(2)}) %collective-permute-start.1) | collective-permute-done | bytes 524320 | tf_op jit(solution)/shard_map/ppermute | solution.py:26
  27.3 2.3 %collective-permute-start.11 = (bf16[128,2048]{1,0:T(8,128)(2,1)}, bf16[128,2048]{1,0:T(8,128)(2,1)}, u32[]{:S(2)}, u32[]{:S(2)}) collective-permute-start(bf16[128,2048]{1,0:T(8,128)(2,1)} %og.3), channel_id=1, source_target_pairs={{0,248},{4,252},{8,0},{12,4},{16,8},{20,12},{24,16},{28,20},{32,24... | collective-permute-start | bytes 1572872 | tf_op jit(solution)/shard_map/ppermute | solution.py:26
  29.6 0.8 slice.9
  30.5 0.8 slice.8
  31.2 0.1 rev.3
  31.3 0.1 pad_maximum_fusion.table
  31.4 0.0 copy-start
  31.4 1.0 copy-done
  32.5 1.0 copy-done.3
  33.5 1.0 copy-done.5
  34.5 0.7 copy-done.10
  35.2 5.0 %shard_map.144 = (f32[16,384,128]{2,1,0:T(8,128)S(1)}, f32[128,2048]{1,0:T(8,128)S(1)}, f32[16,128]{1,0:T(8,128)S(1)}) custom-call(s32[4]{0:T(128)S(1)} %copy-done.10, s32[1]{0:T(128)} %bitcast.start, bf16[128,2048]{1,0:T(8,128)(2,1)S(1)} %copy-done.3, bf16[128,2048]{1,0:T(8,128)(2,1)S(1)} %copy-done, bf16[128,2048]{1,0:T(8,128)(2,1)S(1)} %collective-permute-done.k1, ...), custom_call_target="tpu_custom_call" | custom-call | flops 268435456 | bytes 6823956 | tf_op jit(solution)/shard_map/pallas_call | solution.py:42
  40.2 0.1 collective-permute-start.12
  40.3 0.0 collective-permute-done.8.q1
  40.3 0.8 collective-permute-start.13
  41.1 4.9 %shard_map.145 = (f32[128,2048]{1,0:T(8,128)S(1)}, f32[8,128]{1,0:T(8,128)S(1)}, bf16[256,2048]{1,0:T(8,128)(2,1)S(1)}) custom-call(s32[4]{0:T(128)S(1)} %copy-done.10, s32[1]{0:T(128)} %bitcast.start, bf16[128,2048]{1,0:T(8,128)(2,1)} %collective-permute-done.2.left, bf16[128,2048]{1,0:T(8,128)(2,1)} %multiply_convert_fusion.kv, ...), custom_call_target="tpu_custom_call" | custom-call | flops 1073741824 | bytes 3739668 | tf_op jit(solution)/shard_map/pallas_call | solution.py:42
  46.1 3.0 %collective-permute-start.3 = (f32[8,128]{1,0:T(8,128)S(1)}, f32[8,128]{1,0:T(8,128)S(1)}, u32[]{:S(2)}, u32[]{:S(2)}) collective-permute-start(f32[8,128]{1,0:T(8,128)S(1)} %get-tuple-element.26.s0), channel_id=1, source_target_pairs={{0,2},{1,3},{2,0},{3,1},{4,6},{5,7},{6,4},{7,5},{8,10},{9,11},{10,... | collective-permute-start | bytes 12296 | tf_op jit(solution)/shard_map/ppermute | solution.py:34
  49.1 0.0 collective-permute-done.10.og1
  49.1 0.4 collective-permute-start.4
  49.5 0.0 collective-permute-done.11.og2
  49.5 2.3 %collective-permute-start.5 = (f32[8,128]{1,0:T(8,128)S(1)}, f32[8,128]{1,0:T(8,128)S(1)}, u32[]{:S(2)}, u32[]{:S(2)}) collective-permute-start(f32[8,128]{1,0:T(8,128)S(1)} %get-tuple-element.26.s0), channel_id=1, source_target_pairs={{0,3},{1,0},{2,1},{3,2},{4,7},{5,4},{6,5},{7,6},{8,11},{9,8},{10,9... | collective-permute-start | bytes 12296 | tf_op jit(solution)/shard_map/ppermute | solution.py:34
  51.8 3.4 %shard_map.148 = (f32[16,128,256]{2,1,0:T(8,128)S(1)}, f32[128,2048]{1,0:T(8,128)S(1)}, f32[8,128]{1,0:T(8,128)S(1)}) custom-call(s32[4]{0:T(128)S(1)} %copy-done.10, s32[1]{0:T(128)} %bitcast.start, bf16[128,2048]{1,0:T(8,128)(2,1)S(1)} %copy-done.1, bf16[128,2048]{1,0:T(8,128)(2,1)S(1)} %collective-permute-done.8.q1, ...), custom_call_target="tpu_custom_call" | custom-call | flops 268435456 | bytes 8417300 | tf_op jit(solution)/shard_map/pallas_call | solution.py:42
  55.2 0.3 collective-permute-start.16
  55.4 0.6 collective-permute-start.17
  56.0 2.2 %collective-permute-start.18 = (f32[8,128]{1,0:T(8,128)S(1)}, f32[8,128]{1,0:T(8,128)S(1)}, u32[]{:S(2)}, u32[]{:S(2)}) collective-permute-start(f32[8,128]{1,0:T(8,128)S(1)} %get-tuple-element.35.i0), channel_id=1, source_target_pairs={{0,3},{1,0},{2,1},{3,2},{4,7},{5,4},{6,5},{7,6},{8,11},{9,8},{10,9... | collective-permute-start | bytes 12296 | tf_op jit(solution)/shard_map/ppermute | solution.py:34
  58.2 0.0 collective-permute-done.4.s2
  58.2 0.0 collective-permute-done.5.s3
  58.2 1.2 collective-permute-done.16.i1
  59.4 0.0 collective-permute-done.17.i2
  59.4 0.0 collective-permute-done.18.i3
  59.4 1.7 %shard_map.150 = (bf16[128,2048]{1,0:T(8,128)(2,1)}, bf16[128,2048]{1,0:T(8,128)(2,1)S(1)}) custom-call(f32[128,2048]{1,0:T(8,128)S(1)} %get-tuple-element.34.grad_values, f32[128,2048]{1,0:T(8,128)S(1)} %get-tuple-element.25.signal, bf16[128,2048]{1,0:T(8,128)(2,1)S(1)} %copy-done.2, f32[8,128]{1,0:T(8,128)S(1)} %get-tuple-element.26.s0, ...), custom_call_target="tpu_custom_call" | custom-call | flops 2097152 | bytes 3702784 | tf_op jit(solution)/shard_map/pallas_call | solution.py:42
  61.1 3.9 %shard_map.152 = f32[128,128]{1,0:T(8,128)S(1)} custom-call(s32[4]{0:T(128)S(1)} %copy-done.10, s32[1]{0:T(128)} %bitcast.start, bf16[256,2048]{1,0:T(8,128)(2,1)S(1)} %get-tuple-element.40.flipped, bf16[128,2048]{1,0:T(8,128)(2,1)S(1)} %get-tuple-element.37.grad_signal), custom_call_target="tpu_custom_call" | custom-call | flops 1073741824 | bytes 1638420 | tf_op jit(solution)/shard_map/pallas_call | solution.py:42
  65.0 3.4 %collective-permute-start.20 = (f32[128,128]{1,0:T(8,128)S(1)}, f32[128,128]{1,0:T(8,128)S(1)}, u32[]{:S(2)}, u32[]{:S(2)}) collective-permute-start(f32[128,128]{1,0:T(8,128)S(1)} %shard_map.152), channel_id=1, source_target_pairs={{0,4},{4,0},{1,5},{5,1},{2,6},{6,2},{3,7},{7,3},{8,12},{12,8},{9,1... | collective-permute-start | bytes 196616 | tf_op jit(solution)/shard_map/ppermute | solution.py:314
  68.4 0.9 collective-permute-done.20
  69.3 0.6 collective-permute-start.23
  69.9 0.9 collective-permute-start.22
  70.9 0.5 collective-permute-start.21
  71.4 0.5 shard_map.146.v0
  71.9 1.9 %collective-permute-start.6 = (bf16[128,2048]{1,0:T(8,128)(2,1)S(1)}, bf16[128,2048]{1,0:T(8,128)(2,1)S(1)}, u32[]{:S(2)}, u32[]{:S(2)}) collective-permute-start(bf16[128,2048]{1,0:T(8,128)(2,1)S(1)} %shard_map.146.v0), channel_id=1, source_target_pairs={{0,4},{4,8},{8,12},{12,16},{16,20},{20,24},{24,28},{28,32},{32,36}... | collective-permute-start | bytes 1572872 | tf_op jit(solution)/shard_map/ppermute | solution.py:26
  73.8 0.7 collective-permute-start.7
  74.5 1.1 collective-permute-done.21
  75.6 1.8 %collective-permute-start.24 = (f32[128,128]{1,0:T(8,128)S(1)}, f32[128,128]{1,0:T(8,128)S(1)}, u32[]{:S(2)}, u32[]{:S(2)}) collective-permute-start(f32[128,128]{1,0:T(8,128)S(1)} %add_add_fusion.1), channel_id=1, source_target_pairs={{0,32},{8,40},{16,48},{24,56},{32,0},{40,8},{48,16},{56,24},{64,96... | collective-permute-start | bytes 196616 | tf_op jit(solution)/shard_map/ppermute | solution.py:312
  77.4 18.7 %collective-permute-done.24 = f32[128,128]{1,0:T(8,128)S(1)} collective-permute-done((f32[128,128]{1,0:T(8,128)S(1)}, f32[128,128]{1,0:T(8,128)S(1)}, u32[]{:S(2)}, u32[]{:S(2)}) %collective-permute-start.24) | collective-permute-done | bytes 65568 | tf_op jit(solution)/shard_map/ppermute | solution.py:312
  96.1 0.1 collective-permute-start.27
  96.2 2.9 %collective-permute-start.26 = (f32[128,128]{1,0:T(8,128)S(1)}, f32[128,128]{1,0:T(8,128)S(1)}, u32[]{:S(2)}, u32[]{:S(2)}) collective-permute-start(f32[128,128]{1,0:T(8,128)S(1)} %add.32), channel_id=1, source_target_pairs={{0,16},{8,24},{16,0},{24,8},{32,48},{40,56},{48,32},{56,40},{64,80... | collective-permute-start | bytes 196616 | tf_op jit(solution)/shard_map/ppermute | solution.py:312
  99.1 0.2 collective-permute-done.27
  99.3 2.6 %collective-permute-start.25 = (f32[128,128]{1,0:T(8,128)S(1)}, f32[128,128]{1,0:T(8,128)S(1)}, u32[]{:S(2)}, u32[]{:S(2)}) collective-permute-start(f32[128,128]{1,0:T(8,128)S(1)} %add.32), channel_id=1, source_target_pairs={{0,24},{8,16},{16,8},{24,0},{32,56},{40,48},{48,40},{56,32},{64,88... | collective-permute-start | bytes 196616 | tf_op jit(solution)/shard_map/ppermute | solution.py:312
  101.8 2.4 %collective-permute-done.25 = f32[128,128]{1,0:T(8,128)S(1)} collective-permute-done((f32[128,128]{1,0:T(8,128)S(1)}, f32[128,128]{1,0:T(8,128)S(1)}, u32[]{:S(2)}, u32[]{:S(2)}) %collective-permute-start.25) | collective-permute-done | bytes 65568 | tf_op jit(solution)/shard_map/ppermute | solution.py:312
  104.3 0.6 add_add_fusion
  104.9 0.0 copy-start.7
  105.0 0.0 copy-start.8
  105.0 0.0 copy-start.11
  105.0 6.1 %shard_map.147 = (bf16[128,2048]{1,0:T(8,128)(2,1)}, bf16[128,2048]{1,0:T(8,128)(2,1)}, f32[128,2048]{1,0:T(8,128)S(1)}, f32[16,128]{1,0:T(8,128)S(1)}) custom-call(f32[16,384,128]{2,1,0:T(8,128)S(1)} %get-tuple-element.24.prob, bf16[128,2048]{1,0:T(8,128)(2,1)S(1)} %copy-done.4, bf16[128,2048]{1,0:T(8,128)(2,1)S(1)} %copy-done.1, ...), custom_call_target="tpu_custom_call" | custom-call | flops 671088640 | bytes 9445376 | tf_op jit(solution)/shard_map/pallas_call | solution.py:42
  111.1 4.0 %collective-permute-start.15 = (f32[16,128]{1,0:T(8,128)S(1)}, f32[16,128]{1,0:T(8,128)S(1)}, u32[]{:S(2)}, u32[]{:S(2)}) collective-permute-start(f32[16,128]{1,0:T(8,128)S(1)} %get-tuple-element.32), channel_id=1, source_target_pairs={{0,248},{4,252},{8,0},{12,4},{16,8},{20,12},{24,16},{28,20},{32,24... | collective-permute-start | bytes 24584 | tf_op jit(solution)/shard_map/ppermute | solution.py:26
  115.1 4.8 %shard_map.151 = (bf16[128,2048]{1,0:T(8,128)(2,1)}, bf16[128,2048]{1,0:T(8,128)(2,1)}) custom-call(s32[4]{0:T(128)S(1)} %copy-done.11, s32[1]{0:T(128)} %bitcast.start, bf16[128,2048]{1,0:T(8,128)(2,1)S(1)} %get-tuple-element.37.grad_signal, bf16[128,2048]{1,0:T(8,128)(2,1)S(1)} %collective-permute-done.19.right, bf16[128,2048]{1,0:T(8,128)(2,1)S(1)} %copy-done.8, ...), custom_call_target="tpu_custom_call" | custom-call | flops 1073741824 | bytes 3211284 | tf_op jit(solution)/shard_map/pallas_call | solution.py:42
  120.0 4.0 %shard_map.149 = bf16[128,2048]{1,0:T(8,128)(2,1)} custom-call(f32[16,128,256]{2,1,0:T(8,128)S(1)} %get-tuple-element.31.prob, bf16[128,2048]{1,0:T(8,128)(2,1)S(1)} %shard_map.146.v0, bf16[128,2048]{1,0:T(8,128)(2,1)S(1)} %collective-permute-done.8.q1, bf16[128,2048]{1,0:T(8,128)(2,1)S(1)} %collective-permute-done.9.q2, ...), custom_call_target="tpu_custom_call" | custom-call | flops 268435456 | bytes 6307840 | tf_op jit(solution)/shard_map/pallas_call | solution.py:42
  (37 shorter events, 0.1 us)
Async XLA Ops:
  0.6 40.5 %copy-start.2 = (bf16[128,2048]{1,0:T(8,128)(2,1)S(1)}, bf16[128,2048]{1,0:T(8,128)(2,1)}, u32[]{:S(2)}) copy-start(bf16[128,2048]{1,0:T(8,128)(2,1)} %hyena_q.7) | copy-start | bytes 1572868
  0.6 14.5 %collective-permute-start = (bf16[128,2048]{1,0:T(8,128)(2,1)}, bf16[128,2048]{1,0:T(8,128)(2,1)S(1)}, u32[]{:S(2)}, u32[]{:S(2)}) collective-permute-start(bf16[128,2048]{1,0:T(8,128)(2,1)} %k0.5), channel_id=1, source_target_pairs={{0,4},{4,8},{8,12},{12,16},{16,20},{20,24},{24,28},{28,32},{32,36}... | collective-permute-start | bytes 1572872 | tf_op jit(solution)/shard_map/ppermute | solution.py:26
  3.7 23.6 %collective-permute-start.1 = (bf16[128,2048]{1,0:T(8,128)(2,1)}, bf16[128,2048]{1,0:T(8,128)(2,1)S(1)}, u32[]{:S(2)}, u32[]{:S(2)}) collective-permute-start(bf16[128,2048]{1,0:T(8,128)(2,1)} %k0.5), channel_id=1, source_target_pairs={{0,8},{4,12},{8,16},{12,20},{16,24},{20,28},{24,32},{28,36},{32,40... | collective-permute-start | bytes 1572872 | tf_op jit(solution)/shard_map/ppermute | solution.py:26
  7.5 32.7 %collective-permute-start.2 = (bf16[128,2048]{1,0:T(8,128)(2,1)}, bf16[128,2048]{1,0:T(8,128)(2,1)}, u32[]{:S(2)}, u32[]{:S(2)}) collective-permute-start(bf16[128,2048]{1,0:T(8,128)(2,1)} %multiply_convert_fusion.kv), channel_id=1, source_target_pairs={{0,4},{4,8},{8,12},{12,16},{16,20},{20,24},{24,28},{28,32},{32,36}... | collective-permute-start | bytes 1572872 | tf_op jit(solution)/shard_map/ppermute | solution.py:26
  7.9 32.4 %collective-permute-start.8 = (bf16[128,2048]{1,0:T(8,128)(2,1)}, bf16[128,2048]{1,0:T(8,128)(2,1)S(1)}, u32[]{:S(2)}, u32[]{:S(2)}) collective-permute-start(bf16[128,2048]{1,0:T(8,128)(2,1)} %q.3), channel_id=1, source_target_pairs={{0,252},{4,0},{8,4},{12,8},{16,12},{20,16},{24,20},{28,24},{32,28}... | collective-permute-start | bytes 1572872 | tf_op jit(solution)/shard_map/ppermute | solution.py:26
  8.0 38.0 %collective-permute-start.9 = (bf16[128,2048]{1,0:T(8,128)(2,1)}, bf16[128,2048]{1,0:T(8,128)(2,1)S(1)}, u32[]{:S(2)}, u32[]{:S(2)}) collective-permute-start(bf16[128,2048]{1,0:T(8,128)(2,1)} %q.3), channel_id=1, source_target_pairs={{0,248},{4,252},{8,0},{12,4},{16,8},{20,12},{24,16},{28,20},{32,24... | collective-permute-start | bytes 1572872 | tf_op jit(solution)/shard_map/ppermute | solution.py:26
  15.1 33.9 %collective-permute-start.10 = (bf16[128,2048]{1,0:T(8,128)(2,1)}, bf16[128,2048]{1,0:T(8,128)(2,1)S(1)}, u32[]{:S(2)}, u32[]{:S(2)}) collective-permute-start(bf16[128,2048]{1,0:T(8,128)(2,1)} %og.3), channel_id=1, source_target_pairs={{0,252},{4,0},{8,4},{12,8},{16,12},{20,16},{24,20},{28,24},{32,28}... | collective-permute-start | bytes 1572872 | tf_op jit(solution)/shard_map/ppermute | solution.py:26
  27.3 22.1 %collective-permute-start.11 = (bf16[128,2048]{1,0:T(8,128)(2,1)}, bf16[128,2048]{1,0:T(8,128)(2,1)}, u32[]{:S(2)}, u32[]{:S(2)}) collective-permute-start(bf16[128,2048]{1,0:T(8,128)(2,1)} %og.3), channel_id=1, source_target_pairs={{0,248},{4,252},{8,0},{12,4},{16,8},{20,12},{24,16},{28,20},{32,24... | collective-permute-start | bytes 1572872 | tf_op jit(solution)/shard_map/ppermute | solution.py:26
  31.4 1.0 copy-start
  32.5 1.0 copy-start.3
  33.5 1.0 copy-start.5
  34.5 0.7 copy-start.10
  35.2 16.5 %copy-start.1 = (bf16[128,2048]{1,0:T(8,128)(2,1)S(1)}, bf16[128,2048]{1,0:T(8,128)(2,1)}, u32[]{:S(2)}) copy-start(bf16[128,2048]{1,0:T(8,128)(2,1)} %k0.5) | copy-start | bytes 1572868
  35.2 16.6 %copy-start.9 = (f32[2048]{0:T(1024)S(1)}, f32[2048]{0:T(1024)}, u32[]{:S(2)}) copy-start(f32[2048]{0:T(1024)} %param.13) | copy-start | bytes 24580
  40.2 11.5 %collective-permute-start.12 = (f32[16,128]{1,0:T(8,128)S(1)}, f32[16,128]{1,0:T(8,128)S(1)}, u32[]{:S(2)}, u32[]{:S(2)}) collective-permute-start(f32[16,128]{1,0:T(8,128)S(1)} %get-tuple-element.29), channel_id=1, source_target_pairs={{0,252},{4,0},{8,4},{12,8},{16,12},{20,16},{24,20},{28,24},{32,28}... | collective-permute-start | bytes 24584 | tf_op jit(solution)/shard_map/ppermute | solution.py:26
  40.3 11.4 %collective-permute-start.13 = (f32[16,128]{1,0:T(8,128)S(1)}, f32[16,128]{1,0:T(8,128)S(1)}, u32[]{:S(2)}, u32[]{:S(2)}) collective-permute-start(f32[16,128]{1,0:T(8,128)S(1)} %get-tuple-element.29), channel_id=1, source_target_pairs={{0,248},{4,252},{8,0},{12,4},{16,8},{20,12},{24,16},{28,20},{32,24... | collective-permute-start | bytes 24584 | tf_op jit(solution)/shard_map/ppermute | solution.py:26
  46.1 10.0 %collective-permute-start.3 = (f32[8,128]{1,0:T(8,128)S(1)}, f32[8,128]{1,0:T(8,128)S(1)}, u32[]{:S(2)}, u32[]{:S(2)}) collective-permute-start(f32[8,128]{1,0:T(8,128)S(1)} %get-tuple-element.26.s0), channel_id=1, source_target_pairs={{0,2},{1,3},{2,0},{3,1},{4,6},{5,7},{6,4},{7,5},{8,10},{9,11},{10,... | collective-permute-start | bytes 12296 | tf_op jit(solution)/shard_map/ppermute | solution.py:34
  49.1 9.1 %collective-permute-start.4 = (f32[8,128]{1,0:T(8,128)S(1)}, f32[8,128]{1,0:T(8,128)S(1)}, u32[]{:S(2)}, u32[]{:S(2)}) collective-permute-start(f32[8,128]{1,0:T(8,128)S(1)} %get-tuple-element.26.s0), channel_id=1, source_target_pairs={{0,1},{1,2},{2,3},{3,0},{4,5},{5,6},{6,7},{7,4},{8,9},{9,10},{10,1... | collective-permute-start | bytes 12296 | tf_op jit(solution)/shard_map/ppermute | solution.py:34
  49.5 8.7 %collective-permute-start.5 = (f32[8,128]{1,0:T(8,128)S(1)}, f32[8,128]{1,0:T(8,128)S(1)}, u32[]{:S(2)}, u32[]{:S(2)}) collective-permute-start(f32[8,128]{1,0:T(8,128)S(1)} %get-tuple-element.26.s0), channel_id=1, source_target_pairs={{0,3},{1,0},{2,1},{3,2},{4,7},{5,4},{6,5},{7,6},{8,11},{9,8},{10,9... | collective-permute-start | bytes 12296 | tf_op jit(solution)/shard_map/ppermute | solution.py:34
  55.2 4.2 %collective-permute-start.16 = (f32[8,128]{1,0:T(8,128)S(1)}, f32[8,128]{1,0:T(8,128)S(1)}, u32[]{:S(2)}, u32[]{:S(2)}) collective-permute-start(f32[8,128]{1,0:T(8,128)S(1)} %get-tuple-element.35.i0), channel_id=1, source_target_pairs={{0,2},{1,3},{2,0},{3,1},{4,6},{5,7},{6,4},{7,5},{8,10},{9,11},{10,... | collective-permute-start | bytes 12296 | tf_op jit(solution)/shard_map/ppermute | solution.py:34
  55.4 4.0 %collective-permute-start.17 = (f32[8,128]{1,0:T(8,128)S(1)}, f32[8,128]{1,0:T(8,128)S(1)}, u32[]{:S(2)}, u32[]{:S(2)}) collective-permute-start(f32[8,128]{1,0:T(8,128)S(1)} %get-tuple-element.35.i0), channel_id=1, source_target_pairs={{0,1},{1,2},{2,3},{3,0},{4,5},{5,6},{6,7},{7,4},{8,9},{9,10},{10,1... | collective-permute-start | bytes 12296 | tf_op jit(solution)/shard_map/ppermute | solution.py:34
  56.0 3.4 %collective-permute-start.18 = (f32[8,128]{1,0:T(8,128)S(1)}, f32[8,128]{1,0:T(8,128)S(1)}, u32[]{:S(2)}, u32[]{:S(2)}) collective-permute-start(f32[8,128]{1,0:T(8,128)S(1)} %get-tuple-element.35.i0), channel_id=1, source_target_pairs={{0,3},{1,0},{2,1},{3,2},{4,7},{5,4},{6,5},{7,6},{8,11},{9,8},{10,9... | collective-permute-start | bytes 12296 | tf_op jit(solution)/shard_map/ppermute | solution.py:34
  61.1 40.7 %copy-start.12 = (bf16[128,128]{1,0:T(8,128)(2,1)S(1)}, bf16[128,128]{1,0:T(8,128)(2,1)}, u32[]{:S(2)}) copy-start(bf16[128,128]{1,0:T(8,128)(2,1)} %param.12) | copy-start | bytes 98308
  61.1 43.8 %copy-start.4 = (bf16[128,2048]{1,0:T(8,128)(2,1)S(1)}, bf16[128,2048]{1,0:T(8,128)(2,1)}, u32[]{:S(2)}) copy-start(bf16[128,2048]{1,0:T(8,128)(2,1)} %q.3) | copy-start | bytes 1572868
  61.1 43.8 %copy-start.6 = (bf16[128,2048]{1,0:T(8,128)(2,1)S(1)}, bf16[128,2048]{1,0:T(8,128)(2,1)}, u32[]{:S(2)}) copy-start(bf16[128,2048]{1,0:T(8,128)(2,1)} %og.3) | copy-start | bytes 1572868
  65.0 4.3 %collective-permute-start.20 = (f32[128,128]{1,0:T(8,128)S(1)}, f32[128,128]{1,0:T(8,128)S(1)}, u32[]{:S(2)}, u32[]{:S(2)}) collective-permute-start(f32[128,128]{1,0:T(8,128)S(1)} %shard_map.152), channel_id=1, source_target_pairs={{0,4},{4,0},{1,5},{5,1},{2,6},{6,2},{3,7},{7,3},{8,12},{12,8},{9,1... | collective-permute-start | bytes 196616 | tf_op jit(solution)/shard_map/ppermute | solution.py:314
  69.3 5.2 %collective-permute-start.23 = (f32[128,128]{1,0:T(8,128)S(1)}, f32[128,128]{1,0:T(8,128)S(1)}, u32[]{:S(2)}, u32[]{:S(2)}) collective-permute-start(f32[128,128]{1,0:T(8,128)S(1)} %add.28), channel_id=1, source_target_pairs={{0,192},{8,200},{16,208},{24,216},{32,224},{40,232},{48,240},{56,2... | collective-permute-start | bytes 196616 | tf_op jit(solution)/shard_map/ppermute | solution.py:312
  69.9 4.6 %collective-permute-start.22 = (f32[128,128]{1,0:T(8,128)S(1)}, f32[128,128]{1,0:T(8,128)S(1)}, u32[]{:S(2)}, u32[]{:S(2)}) collective-permute-start(f32[128,128]{1,0:T(8,128)S(1)} %add.28), channel_id=1, source_target_pairs={{0,64},{8,72},{16,80},{24,88},{32,96},{40,104},{48,112},{56,120},{... | collective-permute-start | bytes 196616 | tf_op jit(solution)/shard_map/ppermute | solution.py:312
  70.9 4.7 %collective-permute-start.21 = (f32[128,128]{1,0:T(8,128)S(1)}, f32[128,128]{1,0:T(8,128)S(1)}, u32[]{:S(2)}, u32[]{:S(2)}) collective-permute-start(f32[128,128]{1,0:T(8,128)S(1)} %add.28), channel_id=1, source_target_pairs={{0,128},{8,136},{16,144},{24,152},{32,160},{40,168},{48,176},{56,1... | collective-permute-start | bytes 196616 | tf_op jit(solution)/shard_map/ppermute | solution.py:312
  71.9 33.1 %collective-permute-start.6 = (bf16[128,2048]{1,0:T(8,128)(2,1)S(1)}, bf16[128,2048]{1,0:T(8,128)(2,1)S(1)}, u32[]{:S(2)}, u32[]{:S(2)}) collective-permute-start(bf16[128,2048]{1,0:T(8,128)(2,1)S(1)} %shard_map.146.v0), channel_id=1, source_target_pairs={{0,4},{4,8},{8,12},{12,16},{16,20},{20,24},{24,28},{28,32},{32,36}... | collective-permute-start | bytes 1572872 | tf_op jit(solution)/shard_map/ppermute | solution.py:26
  73.8 31.2 %collective-permute-start.7 = (bf16[128,2048]{1,0:T(8,128)(2,1)S(1)}, bf16[128,2048]{1,0:T(8,128)(2,1)S(1)}, u32[]{:S(2)}, u32[]{:S(2)}) collective-permute-start(bf16[128,2048]{1,0:T(8,128)(2,1)S(1)} %shard_map.146.v0), channel_id=1, source_target_pairs={{0,8},{4,12},{8,16},{12,20},{16,24},{20,28},{24,32},{28,36},{32,40... | collective-permute-start | bytes 1572872 | tf_op jit(solution)/shard_map/ppermute | solution.py:26
  74.5 40.6 %collective-permute-start.19 = (bf16[128,2048]{1,0:T(8,128)(2,1)S(1)}, bf16[128,2048]{1,0:T(8,128)(2,1)S(1)}, u32[]{:S(2)}, u32[]{:S(2)}) collective-permute-start(bf16[128,2048]{1,0:T(8,128)(2,1)S(1)} %get-tuple-element.37.grad_signal), channel_id=1, source_target_pairs={{0,252},{4,0},{8,4},{12,8},{16,12},{20,16},{24,20},{28,24},{32,28}... | collective-permute-start | bytes 1572872 | tf_op jit(solution)/shard_map/ppermute | solution.py:26
  75.6 20.4 %collective-permute-start.24 = (f32[128,128]{1,0:T(8,128)S(1)}, f32[128,128]{1,0:T(8,128)S(1)}, u32[]{:S(2)}, u32[]{:S(2)}) collective-permute-start(f32[128,128]{1,0:T(8,128)S(1)} %add_add_fusion.1), channel_id=1, source_target_pairs={{0,32},{8,40},{16,48},{24,56},{32,0},{40,8},{48,16},{56,24},{64,96... | collective-permute-start | bytes 196616 | tf_op jit(solution)/shard_map/ppermute | solution.py:312
  96.1 3.2 %collective-permute-start.27 = (f32[128,128]{1,0:T(8,128)S(1)}, f32[128,128]{1,0:T(8,128)S(1)}, u32[]{:S(2)}, u32[]{:S(2)}) collective-permute-start(f32[128,128]{1,0:T(8,128)S(1)} %add.32), channel_id=1, source_target_pairs={{0,8},{8,0},{16,24},{24,16},{32,40},{40,32},{48,56},{56,48},{64,72... | collective-permute-start | bytes 196616 | tf_op jit(solution)/shard_map/ppermute | solution.py:312
  96.2 5.7 %collective-permute-start.26 = (f32[128,128]{1,0:T(8,128)S(1)}, f32[128,128]{1,0:T(8,128)S(1)}, u32[]{:S(2)}, u32[]{:S(2)}) collective-permute-start(f32[128,128]{1,0:T(8,128)S(1)} %add.32), channel_id=1, source_target_pairs={{0,16},{8,24},{16,0},{24,8},{32,48},{40,56},{48,32},{56,40},{64,80... | collective-permute-start | bytes 196616 | tf_op jit(solution)/shard_map/ppermute | solution.py:312
  99.3 5.0 %collective-permute-start.25 = (f32[128,128]{1,0:T(8,128)S(1)}, f32[128,128]{1,0:T(8,128)S(1)}, u32[]{:S(2)}, u32[]{:S(2)}) collective-permute-start(f32[128,128]{1,0:T(8,128)S(1)} %add.32), channel_id=1, source_target_pairs={{0,24},{8,16},{16,8},{24,0},{32,56},{40,48},{48,40},{56,32},{64,88... | collective-permute-start | bytes 196616 | tf_op jit(solution)/shard_map/ppermute | solution.py:312
  104.9 10.2 %copy-start.7 = (bf16[128,2048]{1,0:T(8,128)(2,1)S(1)}, bf16[128,2048]{1,0:T(8,128)(2,1)}, u32[]{:S(2)}) copy-start(bf16[128,2048]{1,0:T(8,128)(2,1)} %hyena_v.1) | copy-start | bytes 1572868
  105.0 10.1 %copy-start.8 = (bf16[128,2048]{1,0:T(8,128)(2,1)S(1)}, bf16[128,2048]{1,0:T(8,128)(2,1)}, u32[]{:S(2)}) copy-start(bf16[128,2048]{1,0:T(8,128)(2,1)} %hyena_k.1) | copy-start | bytes 1572868
  105.0 10.1 %copy-start.11 = (s32[4]{0:T(128)S(1)}, s32[4]{0:T(128)}, u32[]{:S(2)}) copy-start(s32[4]{0:T(128)} %lengths.9) | copy-start | bytes 52
  111.1 8.9 %collective-permute-start.14 = (f32[16,128]{1,0:T(8,128)S(1)}, f32[16,128]{1,0:T(8,128)S(1)}, u32[]{:S(2)}, u32[]{:S(2)}) collective-permute-start(f32[16,128]{1,0:T(8,128)S(1)} %get-tuple-element.32), channel_id=1, source_target_pairs={{0,252},{4,0},{8,4},{12,8},{16,12},{20,16},{24,20},{28,24},{32,28}... | collective-permute-start | bytes 24584 | tf_op jit(solution)/shard_map/ppermute | solution.py:26
  111.1 8.9 %collective-permute-start.15 = (f32[16,128]{1,0:T(8,128)S(1)}, f32[16,128]{1,0:T(8,128)S(1)}, u32[]{:S(2)}, u32[]{:S(2)}) collective-permute-start(f32[16,128]{1,0:T(8,128)S(1)} %get-tuple-element.32), channel_id=1, source_target_pairs={{0,248},{4,252},{8,0},{12,4},{16,8},{20,12},{24,16},{28,20},{32,24... | collective-permute-start | bytes 24584 | tf_op jit(solution)/shard_map/ppermute | solution.py:26

commit v4 on v3

--- a/solution.py
+++ b/solution.py
@@ -246,7 +246,7 @@
         out[pl.ds(pl.multiple_of(tile * 8, 8), 8), :] = jnp.concatenate(rows, axis=0)
         return 0
 
-    lax.fori_loop(0, grad_signal.shape[1] // LANES, step, 0, unroll=UNROLL)
+    lax.fori_loop(0, grad_signal.shape[1] // LANES, step, 0, unroll=2 * UNROLL)
 
 
 def conv_back_body(lengths, start, grad_signal, right, hyena_k, hyena_v, table, grad_k, grad_v):
@@ -263,9 +263,24 @@
     lax.fori_loop(0, hyena_k.shape[1] // LANES, step, 0, unroll=UNROLL)
 
 
-def attend_body(
-    prob, q, k0, k1, k2, v0, v1, v2, og, attn_out, grad_q, own, delta_rows
-):
+def delta_body(prob, q, v0, v1, v2, og, own, delta_rows):
+    scale = HEAD**-0.5
+
+    def step(h, _):
+        at = lanes_of(h)
+        vals = jnp.concatenate([v2[:, at], v1[:, at], v0[:, at]], axis=0)
+        p = prob[h]
+        gp = lax.dot_general(vals, og[:, at], (((1,), (1,)), ((), ())), preferred_element_type=F32)
+        delta = jnp.sum(p * gp, axis=0, keepdims=True)
+        delta_rows[pl.ds(h, 1), :] = delta
+        gs = (p[2 * T :] * (gp[2 * T :] - delta) * scale).astype(BF16)
+        own[:, at] = jnp.dot(gs, q[:, at], preferred_element_type=F32)
+        return 0
+
+    lax.fori_loop(0, q.shape[1] // HEAD, step, 0, unroll=UNROLL)
+
+
+def out_body(prob, k0, k1, k2, v0, v1, v2, og, delta_rows, attn_out, grad_q):
     scale = HEAD**-0.5
     over_keys = (((0,), (0,)), ((), ()))
 
@@ -275,19 +290,16 @@
         vals = jnp.concatenate([v2[:, at], v1[:, at], v0[:, at]], axis=0)
         p = prob[h]
         gp = lax.dot_general(vals, og[:, at], (((1,), (1,)), ((), ())), preferred_element_type=F32)
-        delta = jnp.sum(p * gp, axis=0, keepdims=True)
-        delta_rows[pl.ds(h, 1), :] = delta
-        gs = (p * (gp - delta) * scale).astype(BF16)
+        gs = (p * (gp - delta_rows[pl.ds(h, 1), :]) * scale).astype(BF16)
         attn_out[:, at] = lax.dot_general(
             p.astype(BF16), vals, over_keys, preferred_element_type=F32
         ).astype(BF16)
         grad_q[:, at] = lax.dot_general(
             gs, keys, over_keys, preferred_element_type=F32
         ).astype(BF16)
-        own[:, at] = jnp.dot(gs[2 * T :], q[:, at], preferred_element_type=F32)
-        return 0
-
-    lax.fori_loop(0, q.shape[1] // HEAD, step, 0, unroll=UNROLL)
+        return 0
+
+    lax.fori_loop(0, k0.shape[1] // HEAD, step, 0, unroll=2 * UNROLL)
 
 
 def keys_body(prob, v0, q1, q2, og1, og2, delta1, delta2, own, grad_k):
@@ -376,12 +388,8 @@
         exps=heads * 2 * T * T,
     )
     inners = across(inner)
-    attn_out, grad_attn_q, key_own, delta = call(
-        attend_body,
-        (prob, attn_q, attn_k, k1, k2, values, v1, v2, out_grad),
-        (half, half, wide, stat),
-        10 * attn_flops // 3,
-        16,
+    key_own, delta = call(
+        delta_body, (prob, attn_q, values, v1, v2, out_grad), (wide, stat), 4 * attn_flops // 3, 12
     )
     delta2 = shifted(delta, -2)
     delta1 = shifted(delta, -1)
@@ -409,6 +417,13 @@
         band_flops,
         10,
     )
+    attn_out, grad_attn_q = call(
+        out_body,
+        (prob, attn_k, k1, k2, values, v1, v2, out_grad, delta),
+        (half, half),
+        3 * attn_flops,
+        14,
+    )
     return (
         attn_out,
         grad_attn_q,

time: 124 us -> 125 us (level)
  the two profiles are of different devices: /device:TPU:1 before, /device:TPU:6 now
where the time goes in v4:
time: 125 us; the launch traced here: 124 us
  starting transfers between devices  52.1 us (42%)
  Pallas kernels  34.3 us (27%)
  waiting for transfers between devices  26.4 us (21%)
  local copies, waits for them, and re-layouts  7.32 us (6%)
  other arithmetic  2.9 us (2%)
    pallas_call x10, Pallas kernels, call(): pl.pallas_call(body, out_shape=tuple(outs), in_specs=specs, out_specs=tup...  34.3 us
    ppermute x14, starting transfers between devices, shifted(): return lax.ppermute(block, SEQ_AXES, route)  30.3 us
    ppermute x7, waiting for transfers between devices, send(): lax.ppermute(x, 'context', [(i, f(i // 8, i % 8)) for i in range(32)])  14.3 us
    ppermute x7, starting transfers between devices, send(): lax.ppermute(x, 'context', [(i, f(i // 8, i % 8)) for i in range(32)])  11.6 us
    ppermute x6, starting transfers between devices, across(): others.append(lax.ppermute(block, 'tensor', route))  10.1 us
    ppermute x14, waiting for transfers between devices, shifted(): return lax.ppermute(block, SEQ_AXES, route)  9.13 us
    unnamed x30, local copies, waits for them, and re-layouts  5.65 us
  transfers between devices with their start and end apart: 28, of which 7 were waited for; matrix products, arithmetic and copies ran while one was open for 4% of the time, Pallas kernels for 21%

profile of v4, /device:TPU:6, one launch (start us, length us, event | category | flops | bytes accessed | tf_op | source)
XLA Modules:
  0.0 123.9 jit_solution(10401055463164629681)
XLA Ops:
  0.6 0.1 collective-permute-start
  0.7 2.0 %collective-permute-start.1 = (bf16[128,2048]{1,0:T(8,128)(2,1)}, bf16[128,2048]{1,0:T(8,128)(2,1)S(1)}, u32[]{:S(2)}, u32[]{:S(2)}) collective-permute-start(bf16[128,2048]{1,0:T(8,128)(2,1)} %k0.5), channel_id=1, source_target_pairs={{0,8},{4,12},{8,16},{12,20},{16,24},{20,28},{24,32},{28,36},{32,40... | collective-permute-start | bytes 1572872 | tf_op jit(solution)/shard_map/ppermute | solution.py:26
  2.7 2.1 %multiply_convert_fusion.kv = bf16[128,2048]{1,0:T(8,128)(2,1)} fusion(bf16[128,2048]{1,0:T(8,128)(2,1)} %hyena_v.1, bf16[128,2048]{1,0:T(8,128)(2,1)} %hyena_k.1), kind=kLoop, calls=%fused_computation | loop fusion | flops 1048576 | bytes 1572864 | tf_op jit(solution)/shard_map/convert_element_type | solution.py:347
  4.8 1.7 %collective-permute-start.2 = (bf16[128,2048]{1,0:T(8,128)(2,1)}, bf16[128,2048]{1,0:T(8,128)(2,1)}, u32[]{:S(2)}, u32[]{:S(2)}) collective-permute-start(bf16[128,2048]{1,0:T(8,128)(2,1)} %multiply_convert_fusion.kv), channel_id=1, source_target_pairs={{0,4},{4,8},{8,12},{12,16},{16,20},{20,24},{24,28},{28,32},{32,36}... | collective-permute-start | bytes 1572872 | tf_op jit(solution)/shard_map/ppermute | solution.py:26
  6.5 2.2 %collective-permute-start.8 = (bf16[128,2048]{1,0:T(8,128)(2,1)}, bf16[128,2048]{1,0:T(8,128)(2,1)S(1)}, u32[]{:S(2)}, u32[]{:S(2)}) collective-permute-start(bf16[128,2048]{1,0:T(8,128)(2,1)} %q.3), channel_id=1, source_target_pairs={{0,252},{4,0},{8,4},{12,8},{16,12},{20,16},{24,20},{28,24},{32,28}... | collective-permute-start | bytes 1572872 | tf_op jit(solution)/shard_map/ppermute | solution.py:26
  8.7 2.1 %collective-permute-start.9 = (bf16[128,2048]{1,0:T(8,128)(2,1)}, bf16[128,2048]{1,0:T(8,128)(2,1)S(1)}, u32[]{:S(2)}, u32[]{:S(2)}) collective-permute-start(bf16[128,2048]{1,0:T(8,128)(2,1)} %q.3), channel_id=1, source_target_pairs={{0,248},{4,252},{8,0},{12,4},{16,8},{20,12},{24,16},{28,20},{32,24... | collective-permute-start | bytes 1572872 | tf_op jit(solution)/shard_map/ppermute | solution.py:26
  10.8 7.2 %collective-permute-done.k1 = bf16[128,2048]{1,0:T(8,128)(2,1)S(1)} collective-permute-done((bf16[128,2048]{1,0:T(8,128)(2,1)}, bf16[128,2048]{1,0:T(8,128)(2,1)S(1)}, u32[]{:S(2)}, u32[]{:S(2)}) %collective-permute-start) | collective-permute-done | bytes 524320 | tf_op jit(solution)/shard_map/ppermute | solution.py:26
  18.0 0.0 collective-permute-start.10
  18.0 1.9 %collective-permute-done.1.k2 = bf16[128,2048]{1,0:T(8,128)(2,1)S(1)} collective-permute-done((bf16[128,2048]{1,0:T(8,128)(2,1)}, bf16[128,2048]{1,0:T(8,128)(2,1)S(1)}, u32[]{:S(2)}, u32[]{:S(2)}) %collective-permute-start.1) | collective-permute-done | bytes 524320 | tf_op jit(solution)/shard_map/ppermute | solution.py:26
  19.9 0.8 copy-done.7
  20.7 2.0 %collective-permute-start.11 = (bf16[128,2048]{1,0:T(8,128)(2,1)}, bf16[128,2048]{1,0:T(8,128)(2,1)S(1)}, u32[]{:S(2)}, u32[]{:S(2)}) collective-permute-start(bf16[128,2048]{1,0:T(8,128)(2,1)} %og.5), channel_id=1, source_target_pairs={{0,248},{4,252},{8,0},{12,4},{16,8},{20,12},{24,16},{28,20},{32,24... | collective-permute-start | bytes 1572872 | tf_op jit(solution)/shard_map/ppermute | solution.py:26
  22.7 0.8 slice.9
  23.6 0.8 slice.8
  24.3 0.1 rev.3
  24.4 0.1 pad_maximum_fusion.table
  24.5 0.0 copy-start.1
  24.5 1.0 copy-done.1
  25.6 1.0 copy-done.3
  26.6 1.0 copy-done.5
  27.6 1.0 copy-done.8
  28.7 0.7 copy-done.13
  29.3 5.0 %shard_map.144 = (f32[16,384,128]{2,1,0:T(8,128)S(1)}, f32[128,2048]{1,0:T(8,128)S(1)}, f32[16,128]{1,0:T(8,128)S(1)}) custom-call(s32[4]{0:T(128)S(1)} %copy-done.13, s32[1]{0:T(128)} %bitcast.start, bf16[128,2048]{1,0:T(8,128)(2,1)S(1)} %copy-done.5, bf16[128,2048]{1,0:T(8,128)(2,1)S(1)} %copy-done.1, bf16[128,2048]{1,0:T(8,128)(2,1)S(1)} %collective-permute-done.k1, ...), custom_call_target="tpu_custom_call" | custom-call | flops 268435456 | bytes 6823956 | tf_op jit(solution)/shard_map/pallas_call | solution.py:42
  34.3 0.0 collective-permute-done.2.left
  34.3 5.5 %collective-permute-start.12 = (f32[16,128]{1,0:T(8,128)S(1)}, f32[16,128]{1,0:T(8,128)S(1)}, u32[]{:S(2)}, u32[]{:S(2)}) collective-permute-start(f32[16,128]{1,0:T(8,128)S(1)} %get-tuple-element.30), channel_id=1, source_target_pairs={{0,252},{4,0},{8,4},{12,8},{16,12},{20,16},{24,20},{28,24},{32,28}... | collective-permute-start | bytes 24584 | tf_op jit(solution)/shard_map/ppermute | solution.py:26
  39.8 1.0 collective-permute-start.13
  40.8 4.9 %shard_map.145 = (f32[128,2048]{1,0:T(8,128)S(1)}, f32[8,128]{1,0:T(8,128)S(1)}, bf16[256,2048]{1,0:T(8,128)(2,1)S(1)}) custom-call(s32[4]{0:T(128)S(1)} %copy-done.13, s32[1]{0:T(128)} %bitcast.start, bf16[128,2048]{1,0:T(8,128)(2,1)} %collective-permute-done.2.left, bf16[128,2048]{1,0:T(8,128)(2,1)} %multiply_convert_fusion.kv, ...), custom_call_target="tpu_custom_call" | custom-call | flops 1073741824 | bytes 3739668 | tf_op jit(solution)/shard_map/pallas_call | solution.py:42
  45.8 3.3 %collective-permute-start.3 = (f32[8,128]{1,0:T(8,128)S(1)}, f32[8,128]{1,0:T(8,128)S(1)}, u32[]{:S(2)}, u32[]{:S(2)}) collective-permute-start(f32[8,128]{1,0:T(8,128)S(1)} %get-tuple-element.26.s0), channel_id=1, source_target_pairs={{0,2},{1,3},{2,0},{3,1},{4,6},{5,7},{6,4},{7,5},{8,10},{9,11},{10,... | collective-permute-start | bytes 12296 | tf_op jit(solution)/shard_map/ppermute | solution.py:34
  49.1 0.7 collective-permute-start.4
  49.7 2.6 %collective-permute-start.5 = (f32[8,128]{1,0:T(8,128)S(1)}, f32[8,128]{1,0:T(8,128)S(1)}, u32[]{:S(2)}, u32[]{:S(2)}) collective-permute-start(f32[8,128]{1,0:T(8,128)S(1)} %get-tuple-element.26.s0), channel_id=1, source_target_pairs={{0,3},{1,0},{2,1},{3,2},{4,7},{5,4},{6,5},{7,6},{8,11},{9,8},{10,9... | collective-permute-start | bytes 12296 | tf_op jit(solution)/shard_map/ppermute | solution.py:34
  52.3 0.0 collective-permute-done.13.lse2
  52.3 2.9 %shard_map.149 = (f32[16,128,256]{2,1,0:T(8,128)S(1)}, f32[128,2048]{1,0:T(8,128)S(1)}, f32[8,128]{1,0:T(8,128)S(1)}) custom-call(s32[4]{0:T(128)S(1)} %copy-done.13, s32[1]{0:T(128)} %bitcast.start, bf16[128,2048]{1,0:T(8,128)(2,1)S(1)} %copy-done.2, bf16[128,2048]{1,0:T(8,128)(2,1)S(1)} %collective-permute-done.8.q1, ...), custom_call_target="tpu_custom_call" | custom-call | flops 268435456 | bytes 8417300 | tf_op jit(solution)/shard_map/pallas_call | solution.py:42
  55.2 0.3 collective-permute-start.16
  55.5 0.9 collective-permute-start.17
  56.4 2.5 %collective-permute-start.18 = (f32[8,128]{1,0:T(8,128)S(1)}, f32[8,128]{1,0:T(8,128)S(1)}, u32[]{:S(2)}, u32[]{:S(2)}) collective-permute-start(f32[8,128]{1,0:T(8,128)S(1)} %get-tuple-element.35.i0), channel_id=1, source_target_pairs={{0,3},{1,0},{2,1},{3,2},{4,7},{5,4},{6,5},{7,6},{8,11},{9,8},{10,9... | collective-permute-start | bytes 12296 | tf_op jit(solution)/shard_map/ppermute | solution.py:34
  58.8 0.0 collective-permute-done.4.s2
  58.8 1.8 %collective-permute-done.16.i1 = f32[8,128]{1,0:T(8,128)S(1)} collective-permute-done((f32[8,128]{1,0:T(8,128)S(1)}, f32[8,128]{1,0:T(8,128)S(1)}, u32[]{:S(2)}, u32[]{:S(2)}) %collective-permute-start.16) | collective-permute-done | bytes 4128 | tf_op jit(solution)/shard_map/ppermute | solution.py:34
  60.6 1.7 %shard_map.151 = (bf16[128,2048]{1,0:T(8,128)(2,1)}, bf16[128,2048]{1,0:T(8,128)(2,1)S(1)}) custom-call(f32[128,2048]{1,0:T(8,128)S(1)} %get-tuple-element.34.grad_values, f32[128,2048]{1,0:T(8,128)S(1)} %get-tuple-element.25.signal, bf16[128,2048]{1,0:T(8,128)(2,1)S(1)} %copy-done, f32[8,128]{1,0:T(8,128)S(1)} %get-tuple-element.26.s0, ...), custom_call_target="tpu_custom_call" | custom-call | flops 2097152 | bytes 3702784 | tf_op jit(solution)/shard_map/pallas_call | solution.py:42
  62.3 3.4 %shard_map.153 = f32[128,128]{1,0:T(8,128)S(1)} custom-call(s32[4]{0:T(128)S(1)} %copy-done.13, s32[1]{0:T(128)} %bitcast.start, bf16[256,2048]{1,0:T(8,128)(2,1)S(1)} %get-tuple-element.40.flipped, bf16[128,2048]{1,0:T(8,128)(2,1)S(1)} %get-tuple-element.37.grad_signal), custom_call_target="tpu_custom_call" | custom-call | flops 1073741824 | bytes 1638420 | tf_op jit(solution)/shard_map/pallas_call | solution.py:42
  65.7 0.1 collective-permute-start.20
  65.8 1.2 %collective-permute-done.20 = f32[128,128]{1,0:T(8,128)S(1)} collective-permute-done((f32[128,128]{1,0:T(8,128)S(1)}, f32[128,128]{1,0:T(8,128)S(1)}, u32[]{:S(2)}, u32[]{:S(2)}) %collective-permute-start.20) | collective-permute-done | bytes 65568 | tf_op jit(solution)/shard_map/ppermute | solution.py:326
  67.0 0.6 collective-permute-start.23
  67.6 2.7 %collective-permute-start.22 = (f32[128,128]{1,0:T(8,128)S(1)}, f32[128,128]{1,0:T(8,128)S(1)}, u32[]{:S(2)}, u32[]{:S(2)}) collective-permute-start(f32[128,128]{1,0:T(8,128)S(1)} %add.28), channel_id=1, source_target_pairs={{0,64},{8,72},{16,80},{24,88},{32,96},{40,104},{48,112},{56,120},{... | collective-permute-start | bytes 196616 | tf_op jit(solution)/shard_map/ppermute | solution.py:324
  70.3 0.6 collective-permute-start.21
  71.0 0.5 shard_map.146.v0
  71.5 0.1 collective-permute-start.6
  71.6 1.1 collective-permute-start.7
  72.7 3.5 %collective-permute-start.19 = (bf16[128,2048]{1,0:T(8,128)(2,1)S(1)}, bf16[128,2048]{1,0:T(8,128)(2,1)S(1)}, u32[]{:S(2)}, u32[]{:S(2)}) collective-permute-start(bf16[128,2048]{1,0:T(8,128)(2,1)S(1)} %get-tuple-element.37.grad_signal), channel_id=1, source_target_pairs={{0,252},{4,0},{8,4},{12,8},{16,12},{20,16},{24,20},{28,24},{32,28}... | collective-permute-start | bytes 1572872 | tf_op jit(solution)/shard_map/ppermute | solution.py:26
  76.2 0.2 collective-permute-start.24
  76.4 11.2 %collective-permute-done.24 = f32[128,128]{1,0:T(8,128)S(1)} collective-permute-done((f32[128,128]{1,0:T(8,128)S(1)}, f32[128,128]{1,0:T(8,128)S(1)}, u32[]{:S(2)}, u32[]{:S(2)}) %collective-permute-start.24) | collective-permute-done | bytes 65568 | tf_op jit(solution)/shard_map/ppermute | solution.py:324
  87.7 0.0 copy-start.9
  87.7 0.1 collective-permute-start.27
  87.8 4.0 %collective-permute-start.26 = (f32[128,128]{1,0:T(8,128)S(1)}, f32[128,128]{1,0:T(8,128)S(1)}, u32[]{:S(2)}, u32[]{:S(2)}) collective-permute-start(f32[128,128]{1,0:T(8,128)S(1)} %add.32), channel_id=1, source_target_pairs={{0,16},{8,24},{16,0},{24,8},{32,48},{40,56},{48,32},{56,40},{64,80... | collective-permute-start | bytes 196616 | tf_op jit(solution)/shard_map/ppermute | solution.py:324
  91.8 0.3 collective-permute-done.27
  92.0 3.3 %collective-permute-start.25 = (f32[128,128]{1,0:T(8,128)S(1)}, f32[128,128]{1,0:T(8,128)S(1)}, u32[]{:S(2)}, u32[]{:S(2)}) collective-permute-start(f32[128,128]{1,0:T(8,128)S(1)} %add.32), channel_id=1, source_target_pairs={{0,24},{8,16},{16,8},{24,0},{32,56},{40,48},{48,40},{56,32},{64,88... | collective-permute-start | bytes 196616 | tf_op jit(solution)/shard_map/ppermute | solution.py:324
  95.4 2.8 %collective-permute-done.25 = f32[128,128]{1,0:T(8,128)S(1)} collective-permute-done((f32[128,128]{1,0:T(8,128)S(1)}, f32[128,128]{1,0:T(8,128)S(1)}, u32[]{:S(2)}, u32[]{:S(2)}) %collective-permute-start.25) | collective-permute-done | bytes 65568 | tf_op jit(solution)/shard_map/ppermute | solution.py:324
  98.2 0.6 add_add_fusion
  98.8 3.3 %shard_map.147 = (f32[128,2048]{1,0:T(8,128)S(1)}, f32[16,128]{1,0:T(8,128)S(1)}) custom-call(f32[16,384,128]{2,1,0:T(8,128)S(1)} %get-tuple-element.24.prob, bf16[128,2048]{1,0:T(8,128)(2,1)S(1)} %copy-done.6, bf16[128,2048]{1,0:T(8,128)(2,1)S(1)} %shard_map.146.v0, bf16[128,2048]{1,0:T(8,128)(2,1)S(1)} %collective-permute-done.6.v1, ...), custom_call_target="tpu_custom_call" | custom-call | flops 268435456 | bytes 6823936 | tf_op jit(solution)/shard_map/pallas_call | solution.py:42
  102.2 0.0 copy-start.10
  102.2 0.0 copy-start.11
  102.2 9.1 %collective-permute-start.14 = (f32[16,128]{1,0:T(8,128)S(1)}, f32[16,128]{1,0:T(8,128)S(1)}, u32[]{:S(2)}, u32[]{:S(2)}) collective-permute-start(f32[16,128]{1,0:T(8,128)S(1)} %get-tuple-element.27.delta_rows), channel_id=1, source_target_pairs={{0,252},{4,0},{8,4},{12,8},{16,12},{20,16},{24,20},{28,24},{32,28}... | collective-permute-start | bytes 24584 | tf_op jit(solution)/shard_map/ppermute | solution.py:26
  111.3 0.0 collective-permute-start.15
  111.3 4.9 %shard_map.148 = (bf16[128,2048]{1,0:T(8,128)(2,1)}, bf16[128,2048]{1,0:T(8,128)(2,1)}) custom-call(f32[16,384,128]{2,1,0:T(8,128)S(1)} %get-tuple-element.24.prob, bf16[128,2048]{1,0:T(8,128)(2,1)S(1)} %copy-done.2, bf16[128,2048]{1,0:T(8,128)(2,1)S(1)} %collective-permute-done.k1, bf16[128,2048]{1,0:T(8,128)(2,1)S(1)} %copy-done.9, ...), custom_call_target="tpu_custom_call" | custom-call | flops 603979776 | bytes 7872512 | tf_op jit(solution)/shard_map/pallas_call | solution.py:42
  116.2 4.8 %shard_map.152 = (bf16[128,2048]{1,0:T(8,128)(2,1)}, bf16[128,2048]{1,0:T(8,128)(2,1)}) custom-call(s32[4]{0:T(128)S(1)} %copy-done.13, s32[1]{0:T(128)} %bitcast.start, bf16[128,2048]{1,0:T(8,128)(2,1)S(1)} %get-tuple-element.37.grad_signal, bf16[128,2048]{1,0:T(8,128)(2,1)S(1)} %collective-permute-done.19.right, bf16[128,2048]{1,0:T(8,128)(2,1)S(1)} %copy-done.11, ...), custom_call_target="tpu_custom_call" | custom-call | flops 1073741824 | bytes 3211284 | tf_op jit(solution)/shard_map/pallas_call | solution.py:42
  121.0 3.0 %shard_map.150 = bf16[128,2048]{1,0:T(8,128)(2,1)} custom-call(f32[16,128,256]{2,1,0:T(8,128)S(1)} %get-tuple-element.32.prob, bf16[128,2048]{1,0:T(8,128)(2,1)S(1)} %shard_map.146.v0, bf16[128,2048]{1,0:T(8,128)(2,1)S(1)} %collective-permute-done.8.q1, bf16[128,2048]{1,0:T(8,128)(2,1)S(1)} %collective-permute-done.9.q2, ...), custom_call_target="tpu_custom_call" | custom-call | flops 268435456 | bytes 6307840 | tf_op jit(solution)/shard_map/pallas_call | solution.py:42
  (42 shorter events, 0.1 us)
Async XLA Ops:
  0.6 40.2 %copy-start = (bf16[128,2048]{1,0:T(8,128)(2,1)S(1)}, bf16[128,2048]{1,0:T(8,128)(2,1)}, u32[]{:S(2)}) copy-start(bf16[128,2048]{1,0:T(8,128)(2,1)} %hyena_q.7) | copy-start | bytes 1572868
  0.6 17.4 %collective-permute-start = (bf16[128,2048]{1,0:T(8,128)(2,1)}, bf16[128,2048]{1,0:T(8,128)(2,1)S(1)}, u32[]{:S(2)}, u32[]{:S(2)}) collective-permute-start(bf16[128,2048]{1,0:T(8,128)(2,1)} %k0.5), channel_id=1, source_target_pairs={{0,4},{4,8},{8,12},{12,16},{16,20},{20,24},{24,28},{28,32},{32,36}... | collective-permute-start | bytes 1572872 | tf_op jit(solution)/shard_map/ppermute | solution.py:26
  0.7 19.2 %collective-permute-start.1 = (bf16[128,2048]{1,0:T(8,128)(2,1)}, bf16[128,2048]{1,0:T(8,128)(2,1)S(1)}, u32[]{:S(2)}, u32[]{:S(2)}) collective-permute-start(bf16[128,2048]{1,0:T(8,128)(2,1)} %k0.5), channel_id=1, source_target_pairs={{0,8},{4,12},{8,16},{12,20},{16,24},{20,28},{24,32},{28,36},{32,40... | collective-permute-start | bytes 1572872 | tf_op jit(solution)/shard_map/ppermute | solution.py:26
  4.8 29.5 %collective-permute-start.2 = (bf16[128,2048]{1,0:T(8,128)(2,1)}, bf16[128,2048]{1,0:T(8,128)(2,1)}, u32[]{:S(2)}, u32[]{:S(2)}) collective-permute-start(bf16[128,2048]{1,0:T(8,128)(2,1)} %multiply_convert_fusion.kv), channel_id=1, source_target_pairs={{0,4},{4,8},{8,12},{12,16},{16,20},{20,24},{24,28},{28,32},{32,36}... | collective-permute-start | bytes 1572872 | tf_op jit(solution)/shard_map/ppermute | solution.py:26
  6.5 33.3 %collective-permute-start.8 = (bf16[128,2048]{1,0:T(8,128)(2,1)}, bf16[128,2048]{1,0:T(8,128)(2,1)S(1)}, u32[]{:S(2)}, u32[]{:S(2)}) collective-permute-start(bf16[128,2048]{1,0:T(8,128)(2,1)} %q.3), channel_id=1, source_target_pairs={{0,252},{4,0},{8,4},{12,8},{16,12},{20,16},{24,20},{28,24},{32,28}... | collective-permute-start | bytes 1572872 | tf_op jit(solution)/shard_map/ppermute | solution.py:26
  8.7 37.1 %collective-permute-start.9 = (bf16[128,2048]{1,0:T(8,128)(2,1)}, bf16[128,2048]{1,0:T(8,128)(2,1)S(1)}, u32[]{:S(2)}, u32[]{:S(2)}) collective-permute-start(bf16[128,2048]{1,0:T(8,128)(2,1)} %q.3), channel_id=1, source_target_pairs={{0,248},{4,252},{8,0},{12,4},{16,8},{20,12},{24,16},{28,20},{32,24... | collective-permute-start | bytes 1572872 | tf_op jit(solution)/shard_map/ppermute | solution.py:26
  18.0 31.0 %collective-permute-start.10 = (bf16[128,2048]{1,0:T(8,128)(2,1)}, bf16[128,2048]{1,0:T(8,128)(2,1)S(1)}, u32[]{:S(2)}, u32[]{:S(2)}) collective-permute-start(bf16[128,2048]{1,0:T(8,128)(2,1)} %og.5), channel_id=1, source_target_pairs={{0,252},{4,0},{8,4},{12,8},{16,12},{20,16},{24,20},{28,24},{32,28}... | collective-permute-start | bytes 1572872 | tf_op jit(solution)/shard_map/ppermute | solution.py:26
  19.9 0.8 copy-start.7
  20.7 29.0 %collective-permute-start.11 = (bf16[128,2048]{1,0:T(8,128)(2,1)}, bf16[128,2048]{1,0:T(8,128)(2,1)S(1)}, u32[]{:S(2)}, u32[]{:S(2)}) collective-permute-start(bf16[128,2048]{1,0:T(8,128)(2,1)} %og.5), channel_id=1, source_target_pairs={{0,248},{4,252},{8,0},{12,4},{16,8},{20,12},{24,16},{28,20},{32,24... | collective-permute-start | bytes 1572872 | tf_op jit(solution)/shard_map/ppermute | solution.py:26
  24.5 1.0 copy-start.1
  25.6 1.0 copy-start.3
  26.6 1.0 copy-start.5
  27.6 1.0 copy-start.8
  28.7 0.7 copy-start.13
  29.3 23.0 %copy-start.2 = (bf16[128,2048]{1,0:T(8,128)(2,1)S(1)}, bf16[128,2048]{1,0:T(8,128)(2,1)}, u32[]{:S(2)}) copy-start(bf16[128,2048]{1,0:T(8,128)(2,1)} %k0.5) | copy-start | bytes 1572868
  29.3 23.0 %copy-start.12 = (f32[2048]{0:T(1024)S(1)}, f32[2048]{0:T(1024)}, u32[]{:S(2)}) copy-start(f32[2048]{0:T(1024)} %param.13) | copy-start | bytes 24580
  34.3 18.0 %collective-permute-start.12 = (f32[16,128]{1,0:T(8,128)S(1)}, f32[16,128]{1,0:T(8,128)S(1)}, u32[]{:S(2)}, u32[]{:S(2)}) collective-permute-start(f32[16,128]{1,0:T(8,128)S(1)} %get-tuple-element.30), channel_id=1, source_target_pairs={{0,252},{4,0},{8,4},{12,8},{16,12},{20,16},{24,20},{28,24},{32,28}... | collective-permute-start | bytes 24584 | tf_op jit(solution)/shard_map/ppermute | solution.py:26
  39.8 12.5 %collective-permute-start.13 = (f32[16,128]{1,0:T(8,128)S(1)}, f32[16,128]{1,0:T(8,128)S(1)}, u32[]{:S(2)}, u32[]{:S(2)}) collective-permute-start(f32[16,128]{1,0:T(8,128)S(1)} %get-tuple-element.30), channel_id=1, source_target_pairs={{0,248},{4,252},{8,0},{12,4},{16,8},{20,12},{24,16},{28,20},{32,24... | collective-permute-start | bytes 24584 | tf_op jit(solution)/shard_map/ppermute | solution.py:26
  45.8 10.6 %collective-permute-start.3 = (f32[8,128]{1,0:T(8,128)S(1)}, f32[8,128]{1,0:T(8,128)S(1)}, u32[]{:S(2)}, u32[]{:S(2)}) collective-permute-start(f32[8,128]{1,0:T(8,128)S(1)} %get-tuple-element.26.s0), channel_id=1, source_target_pairs={{0,2},{1,3},{2,0},{3,1},{4,6},{5,7},{6,4},{7,5},{8,10},{9,11},{10,... | collective-permute-start | bytes 12296 | tf_op jit(solution)/shard_map/ppermute | solution.py:34
  49.1 9.8 %collective-permute-start.4 = (f32[8,128]{1,0:T(8,128)S(1)}, f32[8,128]{1,0:T(8,128)S(1)}, u32[]{:S(2)}, u32[]{:S(2)}) collective-permute-start(f32[8,128]{1,0:T(8,128)S(1)} %get-tuple-element.26.s0), channel_id=1, source_target_pairs={{0,1},{1,2},{2,3},{3,0},{4,5},{5,6},{6,7},{7,4},{8,9},{9,10},{10,1... | collective-permute-start | bytes 12296 | tf_op jit(solution)/shard_map/ppermute | solution.py:34
  49.7 9.1 %collective-permute-start.5 = (f32[8,128]{1,0:T(8,128)S(1)}, f32[8,128]{1,0:T(8,128)S(1)}, u32[]{:S(2)}, u32[]{:S(2)}) collective-permute-start(f32[8,128]{1,0:T(8,128)S(1)} %get-tuple-element.26.s0), channel_id=1, source_target_pairs={{0,3},{1,0},{2,1},{3,2},{4,7},{5,4},{6,5},{7,6},{8,11},{9,8},{10,9... | collective-permute-start | bytes 12296 | tf_op jit(solution)/shard_map/ppermute | solution.py:34
  55.2 5.4 %collective-permute-start.16 = (f32[8,128]{1,0:T(8,128)S(1)}, f32[8,128]{1,0:T(8,128)S(1)}, u32[]{:S(2)}, u32[]{:S(2)}) collective-permute-start(f32[8,128]{1,0:T(8,128)S(1)} %get-tuple-element.35.i0), channel_id=1, source_target_pairs={{0,2},{1,3},{2,0},{3,1},{4,6},{5,7},{6,4},{7,5},{8,10},{9,11},{10,... | collective-permute-start | bytes 12296 | tf_op jit(solution)/shard_map/ppermute | solution.py:34
  55.5 5.1 %collective-permute-start.17 = (f32[8,128]{1,0:T(8,128)S(1)}, f32[8,128]{1,0:T(8,128)S(1)}, u32[]{:S(2)}, u32[]{:S(2)}) collective-permute-start(f32[8,128]{1,0:T(8,128)S(1)} %get-tuple-element.35.i0), channel_id=1, source_target_pairs={{0,1},{1,2},{2,3},{3,0},{4,5},{5,6},{6,7},{7,4},{8,9},{9,10},{10,1... | collective-permute-start | bytes 12296 | tf_op jit(solution)/shard_map/ppermute | solution.py:34
  56.4 4.2 %collective-permute-start.18 = (f32[8,128]{1,0:T(8,128)S(1)}, f32[8,128]{1,0:T(8,128)S(1)}, u32[]{:S(2)}, u32[]{:S(2)}) collective-permute-start(f32[8,128]{1,0:T(8,128)S(1)} %get-tuple-element.35.i0), channel_id=1, source_target_pairs={{0,3},{1,0},{2,1},{3,2},{4,7},{5,4},{6,5},{7,6},{8,11},{9,8},{10,9... | collective-permute-start | bytes 12296 | tf_op jit(solution)/shard_map/ppermute | solution.py:34
  62.3 33.1 %copy-start.14 = (bf16[128,128]{1,0:T(8,128)(2,1)S(1)}, bf16[128,128]{1,0:T(8,128)(2,1)}, u32[]{:S(2)}) copy-start(bf16[128,128]{1,0:T(8,128)(2,1)} %param.12) | copy-start | bytes 98308
  62.3 36.5 %copy-start.4 = (bf16[128,2048]{1,0:T(8,128)(2,1)S(1)}, bf16[128,2048]{1,0:T(8,128)(2,1)}, u32[]{:S(2)}) copy-start(bf16[128,2048]{1,0:T(8,128)(2,1)} %og.5) | copy-start | bytes 1572868
  62.3 36.5 %copy-start.6 = (bf16[128,2048]{1,0:T(8,128)(2,1)S(1)}, bf16[128,2048]{1,0:T(8,128)(2,1)}, u32[]{:S(2)}) copy-start(bf16[128,2048]{1,0:T(8,128)(2,1)} %q.3) | copy-start | bytes 1572868
  65.7 1.3 %collective-permute-start.20 = (f32[128,128]{1,0:T(8,128)S(1)}, f32[128,128]{1,0:T(8,128)S(1)}, u32[]{:S(2)}, u32[]{:S(2)}) collective-permute-start(f32[128,128]{1,0:T(8,128)S(1)} %shard_map.153), channel_id=1, source_target_pairs={{0,4},{4,0},{1,5},{5,1},{2,6},{6,2},{3,7},{7,3},{8,12},{12,8},{9,1... | collective-permute-start | bytes 196616 | tf_op jit(solution)/shard_map/ppermute | solution.py:326
  67.0 5.6 %collective-permute-start.23 = (f32[128,128]{1,0:T(8,128)S(1)}, f32[128,128]{1,0:T(8,128)S(1)}, u32[]{:S(2)}, u32[]{:S(2)}) collective-permute-start(f32[128,128]{1,0:T(8,128)S(1)} %add.28), channel_id=1, source_target_pairs={{0,192},{8,200},{16,208},{24,216},{32,224},{40,232},{48,240},{56,2... | collective-permute-start | bytes 196616 | tf_op jit(solution)/shard_map/ppermute | solution.py:324
  67.6 8.5 %collective-permute-start.22 = (f32[128,128]{1,0:T(8,128)S(1)}, f32[128,128]{1,0:T(8,128)S(1)}, u32[]{:S(2)}, u32[]{:S(2)}) collective-permute-start(f32[128,128]{1,0:T(8,128)S(1)} %add.28), channel_id=1, source_target_pairs={{0,64},{8,72},{16,80},{24,88},{32,96},{40,104},{48,112},{56,120},{... | collective-permute-start | bytes 196616 | tf_op jit(solution)/shard_map/ppermute | solution.py:324
  70.3 5.8 %collective-permute-start.21 = (f32[128,128]{1,0:T(8,128)S(1)}, f32[128,128]{1,0:T(8,128)S(1)}, u32[]{:S(2)}, u32[]{:S(2)}) collective-permute-start(f32[128,128]{1,0:T(8,128)S(1)} %add.28), channel_id=1, source_target_pairs={{0,128},{8,136},{16,144},{24,152},{32,160},{40,168},{48,176},{56,1... | collective-permute-start | bytes 196616 | tf_op jit(solution)/shard_map/ppermute | solution.py:324
  71.5 27.4 %collective-permute-start.6 = (bf16[128,2048]{1,0:T(8,128)(2,1)S(1)}, bf16[128,2048]{1,0:T(8,128)(2,1)S(1)}, u32[]{:S(2)}, u32[]{:S(2)}) collective-permute-start(bf16[128,2048]{1,0:T(8,128)(2,1)S(1)} %shard_map.146.v0), channel_id=1, source_target_pairs={{0,4},{4,8},{8,12},{12,16},{16,20},{20,24},{24,28},{28,32},{32,36}... | collective-permute-start | bytes 1572872 | tf_op jit(solution)/shard_map/ppermute | solution.py:26
  71.6 27.3 %collective-permute-start.7 = (bf16[128,2048]{1,0:T(8,128)(2,1)S(1)}, bf16[128,2048]{1,0:T(8,128)(2,1)S(1)}, u32[]{:S(2)}, u32[]{:S(2)}) collective-permute-start(bf16[128,2048]{1,0:T(8,128)(2,1)S(1)} %shard_map.146.v0), channel_id=1, source_target_pairs={{0,8},{4,12},{8,16},{12,20},{16,24},{20,28},{24,32},{28,36},{32,40... | collective-permute-start | bytes 1572872 | tf_op jit(solution)/shard_map/ppermute | solution.py:26
  72.7 43.5 %collective-permute-start.19 = (bf16[128,2048]{1,0:T(8,128)(2,1)S(1)}, bf16[128,2048]{1,0:T(8,128)(2,1)S(1)}, u32[]{:S(2)}, u32[]{:S(2)}) collective-permute-start(bf16[128,2048]{1,0:T(8,128)(2,1)S(1)} %get-tuple-element.37.grad_signal), channel_id=1, source_target_pairs={{0,252},{4,0},{8,4},{12,8},{16,12},{20,16},{24,20},{28,24},{32,28}... | collective-permute-start | bytes 1572872 | tf_op jit(solution)/shard_map/ppermute | solution.py:26
  76.2 11.5 %collective-permute-start.24 = (f32[128,128]{1,0:T(8,128)S(1)}, f32[128,128]{1,0:T(8,128)S(1)}, u32[]{:S(2)}, u32[]{:S(2)}) collective-permute-start(f32[128,128]{1,0:T(8,128)S(1)} %add_add_fusion.1), channel_id=1, source_target_pairs={{0,32},{8,40},{16,48},{24,56},{32,0},{40,8},{48,16},{56,24},{64,96... | collective-permute-start | bytes 196616 | tf_op jit(solution)/shard_map/ppermute | solution.py:324
  87.7 23.6 %copy-start.9 = (bf16[128,2048]{1,0:T(8,128)(2,1)S(1)}, bf16[128,2048]{1,0:T(8,128)(2,1)}, u32[]{:S(2)}) copy-start(bf16[128,2048]{1,0:T(8,128)(2,1)} %copy-done.7) | copy-start | bytes 1572868
  87.7 4.4 %collective-permute-start.27 = (f32[128,128]{1,0:T(8,128)S(1)}, f32[128,128]{1,0:T(8,128)S(1)}, u32[]{:S(2)}, u32[]{:S(2)}) collective-permute-start(f32[128,128]{1,0:T(8,128)S(1)} %add.32), channel_id=1, source_target_pairs={{0,8},{8,0},{16,24},{24,16},{32,40},{40,32},{48,56},{56,48},{64,72... | collective-permute-start | bytes 196616 | tf_op jit(solution)/shard_map/ppermute | solution.py:324
  87.8 7.6 %collective-permute-start.26 = (f32[128,128]{1,0:T(8,128)S(1)}, f32[128,128]{1,0:T(8,128)S(1)}, u32[]{:S(2)}, u32[]{:S(2)}) collective-permute-start(f32[128,128]{1,0:T(8,128)S(1)} %add.32), channel_id=1, source_target_pairs={{0,16},{8,24},{16,0},{24,8},{32,48},{40,56},{48,32},{56,40},{64,80... | collective-permute-start | bytes 196616 | tf_op jit(solution)/shard_map/ppermute | solution.py:324
  92.0 6.1 %collective-permute-start.25 = (f32[128,128]{1,0:T(8,128)S(1)}, f32[128,128]{1,0:T(8,128)S(1)}, u32[]{:S(2)}, u32[]{:S(2)}) collective-permute-start(f32[128,128]{1,0:T(8,128)S(1)} %add.32), channel_id=1, source_target_pairs={{0,24},{8,16},{16,8},{24,0},{32,56},{40,48},{48,40},{56,32},{64,88... | collective-permute-start | bytes 196616 | tf_op jit(solution)/shard_map/ppermute | solution.py:324
  102.2 14.0 %copy-start.10 = (bf16[128,2048]{1,0:T(8,128)(2,1)S(1)}, bf16[128,2048]{1,0:T(8,128)(2,1)}, u32[]{:S(2)}) copy-start(bf16[128,2048]{1,0:T(8,128)(2,1)} %hyena_v.1) | copy-start | bytes 1572868
  102.2 14.0 %copy-start.11 = (bf16[128,2048]{1,0:T(8,128)(2,1)S(1)}, bf16[128,2048]{1,0:T(8,128)(2,1)}, u32[]{:S(2)}) copy-start(bf16[128,2048]{1,0:T(8,128)(2,1)} %hyena_k.1) | copy-start | bytes 1572868
  102.2 18.8 %collective-permute-start.14 = (f32[16,128]{1,0:T(8,128)S(1)}, f32[16,128]{1,0:T(8,128)S(1)}, u32[]{:S(2)}, u32[]{:S(2)}) collective-permute-start(f32[16,128]{1,0:T(8,128)S(1)} %get-tuple-element.27.delta_rows), channel_id=1, source_target_pairs={{0,252},{4,0},{8,4},{12,8},{16,12},{20,16},{24,20},{28,24},{32,28}... | collective-permute-start | bytes 24584 | tf_op jit(solution)/shard_map/ppermute | solution.py:26
  111.3 9.7 %collective-permute-start.15 = (f32[16,128]{1,0:T(8,128)S(1)}, f32[16,128]{1,0:T(8,128)S(1)}, u32[]{:S(2)}, u32[]{:S(2)}) collective-permute-start(f32[16,128]{1,0:T(8,128)S(1)} %get-tuple-element.27.delta_rows), channel_id=1, source_target_pairs={{0,248},{4,252},{8,0},{12,4},{16,8},{20,12},{24,16},{28,20},{32,24... | collective-permute-start | bytes 24584 | tf_op jit(solution)/shard_map/ppermute | solution.py:26

commit v5 on v4

--- a/solution.py
+++ b/solution.py
@@ -169,7 +169,7 @@
         own[:, at] = jnp.dot(p[2 * T :].astype(BF16), og[:, at], preferred_element_type=F32)
         return 0
 
-    lax.fori_loop(0, q.shape[1] // HEAD, step, 0, unroll=UNROLL)
+    lax.fori_loop(0, q.shape[1] // HEAD, step, 0, unroll=2 * UNROLL)
 
 
 def later_body(
@@ -196,7 +196,7 @@
         grad_values[:, at] = gv
         return acc + gv * (hyena_q[:, at].astype(F32) * signal[:, at])
 
-    acc = lax.fori_loop(0, own.shape[1] // HEAD, step, jnp.zeros((T, LANES), F32), unroll=UNROLL)
+    acc = lax.fori_loop(0, own.shape[1] // HEAD, step, jnp.zeros((T, LANES), F32), unroll=2 * UNROLL)
     inner[...] = jnp.broadcast_to(jnp.sum(jnp.transpose(acc), axis=0, keepdims=True), (8, LANES))
 
 
@@ -260,7 +260,7 @@
         grad_v[:, at] = (grad_kv * hyena_k[:, at].astype(F32)).astype(BF16)
         return 0
 
-    lax.fori_loop(0, hyena_k.shape[1] // LANES, step, 0, unroll=UNROLL)
+    lax.fori_loop(0, hyena_k.shape[1] // LANES, step, 0, unroll=2 * UNROLL)
 
 
 def delta_body(prob, q, v0, v1, v2, og, own, delta_rows):
@@ -277,7 +277,7 @@
         own[:, at] = jnp.dot(gs, q[:, at], preferred_element_type=F32)
         return 0
 
-    lax.fori_loop(0, q.shape[1] // HEAD, step, 0, unroll=UNROLL)
+    lax.fori_loop(0, q.shape[1] // HEAD, step, 0, unroll=2 * UNROLL)
 
 
 def out_body(prob, k0, k1, k2, v0, v1, v2, og, delta_rows, attn_out, grad_q):

time: 125 us -> 123 us (0.984)
  Pallas kernels: 34.3 us -> 32.1 us
    pallas_call x10, Pallas kernels: 34.3 us -> 32.1 us  [call(): pl.pallas_call(body, out_shape=tuple(outs), in_specs=specs, out_specs=tup...]
  transfers between devices with their start and end apart: 28 -> 28, of which waited for: 7 -> 7; matrix products, arithmetic and copies ran while one was open for 4% -> 4% of each run, Pallas kernels for 21% -> 20%
where the time goes in v5:
time: 123 us; the launch traced here: 122 us
  starting transfers between devices  52.5 us (43%)
  Pallas kernels  32.1 us (26%)
  waiting for transfers between devices  25.9 us (21%)
  local copies, waits for them, and re-layouts  7.32 us (6%)
  other arithmetic  2.9 us (2%)
    pallas_call x10, Pallas kernels, call(): pl.pallas_call(body, out_shape=tuple(outs), in_specs=specs, out_specs=tup...  32.1 us
    ppermute x14, starting transfers between devices, shifted(): return lax.ppermute(block, SEQ_AXES, route)  30.3 us
    ppermute x7, waiting for transfers between devices, send(): lax.ppermute(x, 'context', [(i, f(i // 8, i % 8)) for i in range(32)])  13.7 us
    ppermute x7, starting transfers between devices, send(): lax.ppermute(x, 'context', [(i, f(i // 8, i % 8)) for i in range(32)])  12.2 us
    ppermute x6, starting transfers between devices, across(): others.append(lax.ppermute(block, 'tensor', route))  9.93 us
    ppermute x14, waiting for transfers between devices, shifted(): return lax.ppermute(block, SEQ_AXES, route)  9.13 us
    unnamed x30, local copies, waits for them, and re-layouts  5.65 us
  transfers between devices with their start and end apart: 28, of which 7 were waited for; matrix products, arithmetic and copies ran while one was open for 4% of the time, Pallas kernels for 20%

profile of v5, /device:TPU:6, one launch (start us, length us, event | category | flops | bytes accessed | tf_op | source)
XLA Modules:
  0.0 121.5 jit_solution(3987670791354851581)
XLA Ops:
  0.6 0.1 collective-permute-start
  0.7 2.0 %collective-permute-start.1 = (bf16[128,2048]{1,0:T(8,128)(2,1)}, bf16[128,2048]{1,0:T(8,128)(2,1)S(1)}, u32[]{:S(2)}, u32[]{:S(2)}) collective-permute-start(bf16[128,2048]{1,0:T(8,128)(2,1)} %k0.5), channel_id=1, source_target_pairs={{0,8},{4,12},{8,16},{12,20},{16,24},{20,28},{24,32},{28,36},{32,40... | collective-permute-start | bytes 1572872 | tf_op jit(solution)/shard_map/ppermute | solution.py:26
  2.7 2.1 %multiply_convert_fusion.kv = bf16[128,2048]{1,0:T(8,128)(2,1)} fusion(bf16[128,2048]{1,0:T(8,128)(2,1)} %hyena_v.1, bf16[128,2048]{1,0:T(8,128)(2,1)} %hyena_k.1), kind=kLoop, calls=%fused_computation | loop fusion | flops 1048576 | bytes 1572864 | tf_op jit(solution)/shard_map/convert_element_type | solution.py:347
  4.8 1.7 %collective-permute-start.2 = (bf16[128,2048]{1,0:T(8,128)(2,1)}, bf16[128,2048]{1,0:T(8,128)(2,1)}, u32[]{:S(2)}, u32[]{:S(2)}) collective-permute-start(bf16[128,2048]{1,0:T(8,128)(2,1)} %multiply_convert_fusion.kv), channel_id=1, source_target_pairs={{0,4},{4,8},{8,12},{12,16},{16,20},{20,24},{24,28},{28,32},{32,36}... | collective-permute-start | bytes 1572872 | tf_op jit(solution)/shard_map/ppermute | solution.py:26
  6.5 2.2 %collective-permute-start.8 = (bf16[128,2048]{1,0:T(8,128)(2,1)}, bf16[128,2048]{1,0:T(8,128)(2,1)S(1)}, u32[]{:S(2)}, u32[]{:S(2)}) collective-permute-start(bf16[128,2048]{1,0:T(8,128)(2,1)} %q.3), channel_id=1, source_target_pairs={{0,252},{4,0},{8,4},{12,8},{16,12},{20,16},{24,20},{28,24},{32,28}... | collective-permute-start | bytes 1572872 | tf_op jit(solution)/shard_map/ppermute | solution.py:26
  8.7 2.1 %collective-permute-start.9 = (bf16[128,2048]{1,0:T(8,128)(2,1)}, bf16[128,2048]{1,0:T(8,128)(2,1)S(1)}, u32[]{:S(2)}, u32[]{:S(2)}) collective-permute-start(bf16[128,2048]{1,0:T(8,128)(2,1)} %q.3), channel_id=1, source_target_pairs={{0,248},{4,252},{8,0},{12,4},{16,8},{20,12},{24,16},{28,20},{32,24... | collective-permute-start | bytes 1572872 | tf_op jit(solution)/shard_map/ppermute | solution.py:26
  10.8 7.2 %collective-permute-done.k1 = bf16[128,2048]{1,0:T(8,128)(2,1)S(1)} collective-permute-done((bf16[128,2048]{1,0:T(8,128)(2,1)}, bf16[128,2048]{1,0:T(8,128)(2,1)S(1)}, u32[]{:S(2)}, u32[]{:S(2)}) %collective-permute-start) | collective-permute-done | bytes 524320 | tf_op jit(solution)/shard_map/ppermute | solution.py:26
  18.0 0.0 collective-permute-start.10
  18.0 1.9 %collective-permute-done.1.k2 = bf16[128,2048]{1,0:T(8,128)(2,1)S(1)} collective-permute-done((bf16[128,2048]{1,0:T(8,128)(2,1)}, bf16[128,2048]{1,0:T(8,128)(2,1)S(1)}, u32[]{:S(2)}, u32[]{:S(2)}) %collective-permute-start.1) | collective-permute-done | bytes 524320 | tf_op jit(solution)/shard_map/ppermute | solution.py:26
  19.9 0.8 copy-done.7
  20.7 2.0 %collective-permute-start.11 = (bf16[128,2048]{1,0:T(8,128)(2,1)}, bf16[128,2048]{1,0:T(8,128)(2,1)S(1)}, u32[]{:S(2)}, u32[]{:S(2)}) collective-permute-start(bf16[128,2048]{1,0:T(8,128)(2,1)} %og.5), channel_id=1, source_target_pairs={{0,248},{4,252},{8,0},{12,4},{16,8},{20,12},{24,16},{28,20},{32,24... | collective-permute-start | bytes 1572872 | tf_op jit(solution)/shard_map/ppermute | solution.py:26
  22.7 0.8 slice.9
  23.6 0.8 slice.8
  24.3 0.1 rev.3
  24.4 0.1 pad_maximum_fusion.table
  24.5 0.0 copy-start.1
  24.5 1.0 copy-done.1
  25.6 1.0 copy-done.3
  26.6 1.0 copy-done.5
  27.6 1.0 copy-done.8
  28.7 0.7 copy-done.13
  29.3 4.3 %shard_map.144 = (f32[16,384,128]{2,1,0:T(8,128)S(1)}, f32[128,2048]{1,0:T(8,128)S(1)}, f32[16,128]{1,0:T(8,128)S(1)}) custom-call(s32[4]{0:T(128)S(1)} %copy-done.13, s32[1]{0:T(128)} %bitcast.start, bf16[128,2048]{1,0:T(8,128)(2,1)S(1)} %copy-done.5, bf16[128,2048]{1,0:T(8,128)(2,1)S(1)} %copy-done.1, bf16[128,2048]{1,0:T(8,128)(2,1)S(1)} %collective-permute-done.k1, ...), custom_call_target="tpu_custom_call" | custom-call | flops 268435456 | bytes 6823956 | tf_op jit(solution)/shard_map/pallas_call | solution.py:42
  33.6 5.5 %collective-permute-start.12 = (f32[16,128]{1,0:T(8,128)S(1)}, f32[16,128]{1,0:T(8,128)S(1)}, u32[]{:S(2)}, u32[]{:S(2)}) collective-permute-start(f32[16,128]{1,0:T(8,128)S(1)} %get-tuple-element.30), channel_id=1, source_target_pairs={{0,252},{4,0},{8,4},{12,8},{16,12},{20,16},{24,20},{28,24},{32,28}... | collective-permute-start | bytes 24584 | tf_op jit(solution)/shard_map/ppermute | solution.py:26
  39.1 0.0 collective-permute-done.8.q1
  39.1 1.0 collective-permute-start.13
  40.1 4.9 %shard_map.145 = (f32[128,2048]{1,0:T(8,128)S(1)}, f32[8,128]{1,0:T(8,128)S(1)}, bf16[256,2048]{1,0:T(8,128)(2,1)S(1)}) custom-call(s32[4]{0:T(128)S(1)} %copy-done.13, s32[1]{0:T(128)} %bitcast.start, bf16[128,2048]{1,0:T(8,128)(2,1)} %collective-permute-done.2.left, bf16[128,2048]{1,0:T(8,128)(2,1)} %multiply_convert_fusion.kv, ...), custom_call_target="tpu_custom_call" | custom-call | flops 1073741824 | bytes 3739668 | tf_op jit(solution)/shard_map/pallas_call | solution.py:42
  45.1 0.0 collective-permute-done.9.q2
  45.1 3.3 %collective-permute-start.3 = (f32[8,128]{1,0:T(8,128)S(1)}, f32[8,128]{1,0:T(8,128)S(1)}, u32[]{:S(2)}, u32[]{:S(2)}) collective-permute-start(f32[8,128]{1,0:T(8,128)S(1)} %get-tuple-element.26.s0), channel_id=1, source_target_pairs={{0,2},{1,3},{2,0},{3,1},{4,6},{5,7},{6,4},{7,5},{8,10},{9,11},{10,... | collective-permute-start | bytes 12296 | tf_op jit(solution)/shard_map/ppermute | solution.py:34
  48.4 0.0 collective-permute-done.10.og1
  48.4 0.7 collective-permute-start.4
  49.0 0.0 collective-permute-done.11.og2
  49.0 2.6 %collective-permute-start.5 = (f32[8,128]{1,0:T(8,128)S(1)}, f32[8,128]{1,0:T(8,128)S(1)}, u32[]{:S(2)}, u32[]{:S(2)}) collective-permute-start(f32[8,128]{1,0:T(8,128)S(1)} %get-tuple-element.26.s0), channel_id=1, source_target_pairs={{0,3},{1,0},{2,1},{3,2},{4,7},{5,4},{6,5},{7,6},{8,11},{9,8},{10,9... | collective-permute-start | bytes 12296 | tf_op jit(solution)/shard_map/ppermute | solution.py:34
  51.6 2.3 %shard_map.149 = (f32[16,128,256]{2,1,0:T(8,128)S(1)}, f32[128,2048]{1,0:T(8,128)S(1)}, f32[8,128]{1,0:T(8,128)S(1)}) custom-call(s32[4]{0:T(128)S(1)} %copy-done.13, s32[1]{0:T(128)} %bitcast.start, bf16[128,2048]{1,0:T(8,128)(2,1)S(1)} %copy-done.2, bf16[128,2048]{1,0:T(8,128)(2,1)S(1)} %collective-permute-done.8.q1, ...), custom_call_target="tpu_custom_call" | custom-call | flops 268435456 | bytes 8417300 | tf_op jit(solution)/shard_map/pallas_call | solution.py:42
  53.9 0.1 collective-permute-start.16
  54.0 0.9 collective-permute-start.17
  54.9 2.5 %collective-permute-start.18 = (f32[8,128]{1,0:T(8,128)S(1)}, f32[8,128]{1,0:T(8,128)S(1)}, u32[]{:S(2)}, u32[]{:S(2)}) collective-permute-start(f32[8,128]{1,0:T(8,128)S(1)} %get-tuple-element.35.i0), channel_id=1, source_target_pairs={{0,3},{1,0},{2,1},{3,2},{4,7},{5,4},{6,5},{7,6},{8,11},{9,8},{10,9... | collective-permute-start | bytes 12296 | tf_op jit(solution)/shard_map/ppermute | solution.py:34
  57.4 1.8 %collective-permute-done.16.i1 = f32[8,128]{1,0:T(8,128)S(1)} collective-permute-done((f32[8,128]{1,0:T(8,128)S(1)}, f32[8,128]{1,0:T(8,128)S(1)}, u32[]{:S(2)}, u32[]{:S(2)}) %collective-permute-start.16) | collective-permute-done | bytes 4128 | tf_op jit(solution)/shard_map/ppermute | solution.py:34
  59.2 1.7 %shard_map.151 = (bf16[128,2048]{1,0:T(8,128)(2,1)}, bf16[128,2048]{1,0:T(8,128)(2,1)S(1)}) custom-call(f32[128,2048]{1,0:T(8,128)S(1)} %get-tuple-element.34.grad_values, f32[128,2048]{1,0:T(8,128)S(1)} %get-tuple-element.25.signal, bf16[128,2048]{1,0:T(8,128)(2,1)S(1)} %copy-done, f32[8,128]{1,0:T(8,128)S(1)} %get-tuple-element.26.s0, ...), custom_call_target="tpu_custom_call" | custom-call | flops 2097152 | bytes 3702784 | tf_op jit(solution)/shard_map/pallas_call | solution.py:42
  60.8 3.4 %shard_map.153 = f32[128,128]{1,0:T(8,128)S(1)} custom-call(s32[4]{0:T(128)S(1)} %copy-done.13, s32[1]{0:T(128)} %bitcast.start, bf16[256,2048]{1,0:T(8,128)(2,1)S(1)} %get-tuple-element.40.flipped, bf16[128,2048]{1,0:T(8,128)(2,1)S(1)} %get-tuple-element.37.grad_signal), custom_call_target="tpu_custom_call" | custom-call | flops 1073741824 | bytes 1638420 | tf_op jit(solution)/shard_map/pallas_call | solution.py:42
  64.2 0.1 collective-permute-start.20
  64.3 1.2 %collective-permute-done.20 = f32[128,128]{1,0:T(8,128)S(1)} collective-permute-done((f32[128,128]{1,0:T(8,128)S(1)}, f32[128,128]{1,0:T(8,128)S(1)}, u32[]{:S(2)}, u32[]{:S(2)}) %collective-permute-start.20) | collective-permute-done | bytes 65568 | tf_op jit(solution)/shard_map/ppermute | solution.py:326
  65.6 0.6 collective-permute-start.23
  66.2 2.7 %collective-permute-start.22 = (f32[128,128]{1,0:T(8,128)S(1)}, f32[128,128]{1,0:T(8,128)S(1)}, u32[]{:S(2)}, u32[]{:S(2)}) collective-permute-start(f32[128,128]{1,0:T(8,128)S(1)} %add.28), channel_id=1, source_target_pairs={{0,64},{8,72},{16,80},{24,88},{32,96},{40,104},{48,112},{56,120},{... | collective-permute-start | bytes 196616 | tf_op jit(solution)/shard_map/ppermute | solution.py:324
  68.9 0.6 collective-permute-start.21
  69.5 0.5 shard_map.146.v0
  70.0 0.1 collective-permute-start.6
  70.1 1.1 collective-permute-start.7
  71.2 3.5 %collective-permute-start.19 = (bf16[128,2048]{1,0:T(8,128)(2,1)S(1)}, bf16[128,2048]{1,0:T(8,128)(2,1)S(1)}, u32[]{:S(2)}, u32[]{:S(2)}) collective-permute-start(bf16[128,2048]{1,0:T(8,128)(2,1)S(1)} %get-tuple-element.37.grad_signal), channel_id=1, source_target_pairs={{0,252},{4,0},{8,4},{12,8},{16,12},{20,16},{24,20},{28,24},{32,28}... | collective-permute-start | bytes 1572872 | tf_op jit(solution)/shard_map/ppermute | solution.py:26
  74.7 0.8 collective-permute-start.24
  75.5 10.7 %collective-permute-done.24 = f32[128,128]{1,0:T(8,128)S(1)} collective-permute-done((f32[128,128]{1,0:T(8,128)S(1)}, f32[128,128]{1,0:T(8,128)S(1)}, u32[]{:S(2)}, u32[]{:S(2)}) %collective-permute-start.24) | collective-permute-done | bytes 65568 | tf_op jit(solution)/shard_map/ppermute | solution.py:324
  86.2 0.0 copy-start.9
  86.2 0.1 collective-permute-start.27
  86.3 4.0 %collective-permute-start.26 = (f32[128,128]{1,0:T(8,128)S(1)}, f32[128,128]{1,0:T(8,128)S(1)}, u32[]{:S(2)}, u32[]{:S(2)}) collective-permute-start(f32[128,128]{1,0:T(8,128)S(1)} %add.32), channel_id=1, source_target_pairs={{0,16},{8,24},{16,0},{24,8},{32,48},{40,56},{48,32},{56,40},{64,80... | collective-permute-start | bytes 196616 | tf_op jit(solution)/shard_map/ppermute | solution.py:324
  90.3 0.3 collective-permute-done.27
  90.6 3.3 %collective-permute-start.25 = (f32[128,128]{1,0:T(8,128)S(1)}, f32[128,128]{1,0:T(8,128)S(1)}, u32[]{:S(2)}, u32[]{:S(2)}) collective-permute-start(f32[128,128]{1,0:T(8,128)S(1)} %add.32), channel_id=1, source_target_pairs={{0,24},{8,16},{16,8},{24,0},{32,56},{40,48},{48,40},{56,32},{64,88... | collective-permute-start | bytes 196616 | tf_op jit(solution)/shard_map/ppermute | solution.py:324
  94.0 2.8 %collective-permute-done.25 = f32[128,128]{1,0:T(8,128)S(1)} collective-permute-done((f32[128,128]{1,0:T(8,128)S(1)}, f32[128,128]{1,0:T(8,128)S(1)}, u32[]{:S(2)}, u32[]{:S(2)}) %collective-permute-start.25) | collective-permute-done | bytes 65568 | tf_op jit(solution)/shard_map/ppermute | solution.py:324
  96.7 0.6 add_add_fusion
  97.4 2.7 %shard_map.147 = (f32[128,2048]{1,0:T(8,128)S(1)}, f32[16,128]{1,0:T(8,128)S(1)}) custom-call(f32[16,384,128]{2,1,0:T(8,128)S(1)} %get-tuple-element.24.prob, bf16[128,2048]{1,0:T(8,128)(2,1)S(1)} %copy-done.6, bf16[128,2048]{1,0:T(8,128)(2,1)S(1)} %shard_map.146.v0, bf16[128,2048]{1,0:T(8,128)(2,1)S(1)} %collective-permute-done.6.v1, ...), custom_call_target="tpu_custom_call" | custom-call | flops 268435456 | bytes 6823936 | tf_op jit(solution)/shard_map/pallas_call | solution.py:42
  100.1 0.0 copy-start.10
  100.2 0.0 copy-start.11
  100.2 9.1 %collective-permute-start.14 = (f32[16,128]{1,0:T(8,128)S(1)}, f32[16,128]{1,0:T(8,128)S(1)}, u32[]{:S(2)}, u32[]{:S(2)}) collective-permute-start(f32[16,128]{1,0:T(8,128)S(1)} %get-tuple-element.27.delta_rows), channel_id=1, source_target_pairs={{0,252},{4,0},{8,4},{12,8},{16,12},{20,16},{24,20},{28,24},{32,28}... | collective-permute-start | bytes 24584 | tf_op jit(solution)/shard_map/ppermute | solution.py:26
  109.3 4.9 %shard_map.148 = (bf16[128,2048]{1,0:T(8,128)(2,1)}, bf16[128,2048]{1,0:T(8,128)(2,1)}) custom-call(f32[16,384,128]{2,1,0:T(8,128)S(1)} %get-tuple-element.24.prob, bf16[128,2048]{1,0:T(8,128)(2,1)S(1)} %copy-done.2, bf16[128,2048]{1,0:T(8,128)(2,1)S(1)} %collective-permute-done.k1, bf16[128,2048]{1,0:T(8,128)(2,1)S(1)} %copy-done.9, ...), custom_call_target="tpu_custom_call" | custom-call | flops 603979776 | bytes 7872512 | tf_op jit(solution)/shard_map/pallas_call | solution.py:42
  114.1 4.4 %shard_map.152 = (bf16[128,2048]{1,0:T(8,128)(2,1)}, bf16[128,2048]{1,0:T(8,128)(2,1)}) custom-call(s32[4]{0:T(128)S(1)} %copy-done.13, s32[1]{0:T(128)} %bitcast.start, bf16[128,2048]{1,0:T(8,128)(2,1)S(1)} %get-tuple-element.37.grad_signal, bf16[128,2048]{1,0:T(8,128)(2,1)S(1)} %collective-permute-done.19.right, bf16[128,2048]{1,0:T(8,128)(2,1)S(1)} %copy-done.11, ...), custom_call_target="tpu_custom_call" | custom-call | flops 1073741824 | bytes 3211284 | tf_op jit(solution)/shard_map/pallas_call | solution.py:42
  118.6 3.0 %shard_map.150 = bf16[128,2048]{1,0:T(8,128)(2,1)} custom-call(f32[16,128,256]{2,1,0:T(8,128)S(1)} %get-tuple-element.32.prob, bf16[128,2048]{1,0:T(8,128)(2,1)S(1)} %shard_map.146.v0, bf16[128,2048]{1,0:T(8,128)(2,1)S(1)} %collective-permute-done.8.q1, bf16[128,2048]{1,0:T(8,128)(2,1)S(1)} %collective-permute-done.9.q2, ...), custom_call_target="tpu_custom_call" | custom-call | flops 268435456 | bytes 6307840 | tf_op jit(solution)/shard_map/pallas_call | solution.py:42
  (42 shorter events, 0.1 us)
Async XLA Ops:
  0.6 39.5 %copy-start = (bf16[128,2048]{1,0:T(8,128)(2,1)S(1)}, bf16[128,2048]{1,0:T(8,128)(2,1)}, u32[]{:S(2)}) copy-start(bf16[128,2048]{1,0:T(8,128)(2,1)} %hyena_q.7) | copy-start | bytes 1572868
  0.6 17.4 %collective-permute-start = (bf16[128,2048]{1,0:T(8,128)(2,1)}, bf16[128,2048]{1,0:T(8,128)(2,1)S(1)}, u32[]{:S(2)}, u32[]{:S(2)}) collective-permute-start(bf16[128,2048]{1,0:T(8,128)(2,1)} %k0.5), channel_id=1, source_target_pairs={{0,4},{4,8},{8,12},{12,16},{16,20},{20,24},{24,28},{28,32},{32,36}... | collective-permute-start | bytes 1572872 | tf_op jit(solution)/shard_map/ppermute | solution.py:26
  0.7 19.2 %collective-permute-start.1 = (bf16[128,2048]{1,0:T(8,128)(2,1)}, bf16[128,2048]{1,0:T(8,128)(2,1)S(1)}, u32[]{:S(2)}, u32[]{:S(2)}) collective-permute-start(bf16[128,2048]{1,0:T(8,128)(2,1)} %k0.5), channel_id=1, source_target_pairs={{0,8},{4,12},{8,16},{12,20},{16,24},{20,28},{24,32},{28,36},{32,40... | collective-permute-start | bytes 1572872 | tf_op jit(solution)/shard_map/ppermute | solution.py:26
  4.8 28.8 %collective-permute-start.2 = (bf16[128,2048]{1,0:T(8,128)(2,1)}, bf16[128,2048]{1,0:T(8,128)(2,1)}, u32[]{:S(2)}, u32[]{:S(2)}) collective-permute-start(bf16[128,2048]{1,0:T(8,128)(2,1)} %multiply_convert_fusion.kv), channel_id=1, source_target_pairs={{0,4},{4,8},{8,12},{12,16},{16,20},{20,24},{24,28},{28,32},{32,36}... | collective-permute-start | bytes 1572872 | tf_op jit(solution)/shard_map/ppermute | solution.py:26
  6.5 32.6 %collective-permute-start.8 = (bf16[128,2048]{1,0:T(8,128)(2,1)}, bf16[128,2048]{1,0:T(8,128)(2,1)S(1)}, u32[]{:S(2)}, u32[]{:S(2)}) collective-permute-start(bf16[128,2048]{1,0:T(8,128)(2,1)} %q.3), channel_id=1, source_target_pairs={{0,252},{4,0},{8,4},{12,8},{16,12},{20,16},{24,20},{28,24},{32,28}... | collective-permute-start | bytes 1572872 | tf_op jit(solution)/shard_map/ppermute | solution.py:26
  8.7 36.4 %collective-permute-start.9 = (bf16[128,2048]{1,0:T(8,128)(2,1)}, bf16[128,2048]{1,0:T(8,128)(2,1)S(1)}, u32[]{:S(2)}, u32[]{:S(2)}) collective-permute-start(bf16[128,2048]{1,0:T(8,128)(2,1)} %q.3), channel_id=1, source_target_pairs={{0,248},{4,252},{8,0},{12,4},{16,8},{20,12},{24,16},{28,20},{32,24... | collective-permute-start | bytes 1572872 | tf_op jit(solution)/shard_map/ppermute | solution.py:26
  18.0 30.3 %collective-permute-start.10 = (bf16[128,2048]{1,0:T(8,128)(2,1)}, bf16[128,2048]{1,0:T(8,128)(2,1)S(1)}, u32[]{:S(2)}, u32[]{:S(2)}) collective-permute-start(bf16[128,2048]{1,0:T(8,128)(2,1)} %og.5), channel_id=1, source_target_pairs={{0,252},{4,0},{8,4},{12,8},{16,12},{20,16},{24,20},{28,24},{32,28}... | collective-permute-start | bytes 1572872 | tf_op jit(solution)/shard_map/ppermute | solution.py:26
  19.9 0.8 copy-start.7
  20.7 28.3 %collective-permute-start.11 = (bf16[128,2048]{1,0:T(8,128)(2,1)}, bf16[128,2048]{1,0:T(8,128)(2,1)S(1)}, u32[]{:S(2)}, u32[]{:S(2)}) collective-permute-start(bf16[128,2048]{1,0:T(8,128)(2,1)} %og.5), channel_id=1, source_target_pairs={{0,248},{4,252},{8,0},{12,4},{16,8},{20,12},{24,16},{28,20},{32,24... | collective-permute-start | bytes 1572872 | tf_op jit(solution)/shard_map/ppermute | solution.py:26
  24.5 1.0 copy-start.1
  25.6 1.0 copy-start.3
  26.6 1.0 copy-start.5
  27.6 1.0 copy-start.8
  28.7 0.7 copy-start.13
  29.3 22.3 %copy-start.2 = (bf16[128,2048]{1,0:T(8,128)(2,1)S(1)}, bf16[128,2048]{1,0:T(8,128)(2,1)}, u32[]{:S(2)}) copy-start(bf16[128,2048]{1,0:T(8,128)(2,1)} %k0.5) | copy-start | bytes 1572868
  29.3 22.3 %copy-start.12 = (f32[2048]{0:T(1024)S(1)}, f32[2048]{0:T(1024)}, u32[]{:S(2)}) copy-start(f32[2048]{0:T(1024)} %param.13) | copy-start | bytes 24580
  33.6 18.0 %collective-permute-start.12 = (f32[16,128]{1,0:T(8,128)S(1)}, f32[16,128]{1,0:T(8,128)S(1)}, u32[]{:S(2)}, u32[]{:S(2)}) collective-permute-start(f32[16,128]{1,0:T(8,128)S(1)} %get-tuple-element.30), channel_id=1, source_target_pairs={{0,252},{4,0},{8,4},{12,8},{16,12},{20,16},{24,20},{28,24},{32,28}... | collective-permute-start | bytes 24584 | tf_op jit(solution)/shard_map/ppermute | solution.py:26
  39.1 12.5 %collective-permute-start.13 = (f32[16,128]{1,0:T(8,128)S(1)}, f32[16,128]{1,0:T(8,128)S(1)}, u32[]{:S(2)}, u32[]{:S(2)}) collective-permute-start(f32[16,128]{1,0:T(8,128)S(1)} %get-tuple-element.30), channel_id=1, source_target_pairs={{0,248},{4,252},{8,0},{12,4},{16,8},{20,12},{24,16},{28,20},{32,24... | collective-permute-start | bytes 24584 | tf_op jit(solution)/shard_map/ppermute | solution.py:26
  45.1 9.8 %collective-permute-start.3 = (f32[8,128]{1,0:T(8,128)S(1)}, f32[8,128]{1,0:T(8,128)S(1)}, u32[]{:S(2)}, u32[]{:S(2)}) collective-permute-start(f32[8,128]{1,0:T(8,128)S(1)} %get-tuple-element.26.s0), channel_id=1, source_target_pairs={{0,2},{1,3},{2,0},{3,1},{4,6},{5,7},{6,4},{7,5},{8,10},{9,11},{10,... | collective-permute-start | bytes 12296 | tf_op jit(solution)/shard_map/ppermute | solution.py:34
  48.4 9.0 %collective-permute-start.4 = (f32[8,128]{1,0:T(8,128)S(1)}, f32[8,128]{1,0:T(8,128)S(1)}, u32[]{:S(2)}, u32[]{:S(2)}) collective-permute-start(f32[8,128]{1,0:T(8,128)S(1)} %get-tuple-element.26.s0), channel_id=1, source_target_pairs={{0,1},{1,2},{2,3},{3,0},{4,5},{5,6},{6,7},{7,4},{8,9},{9,10},{10,1... | collective-permute-start | bytes 12296 | tf_op jit(solution)/shard_map/ppermute | solution.py:34
  49.0 8.3 %collective-permute-start.5 = (f32[8,128]{1,0:T(8,128)S(1)}, f32[8,128]{1,0:T(8,128)S(1)}, u32[]{:S(2)}, u32[]{:S(2)}) collective-permute-start(f32[8,128]{1,0:T(8,128)S(1)} %get-tuple-element.26.s0), channel_id=1, source_target_pairs={{0,3},{1,0},{2,1},{3,2},{4,7},{5,4},{6,5},{7,6},{8,11},{9,8},{10,9... | collective-permute-start | bytes 12296 | tf_op jit(solution)/shard_map/ppermute | solution.py:34
  53.9 5.2 %collective-permute-start.16 = (f32[8,128]{1,0:T(8,128)S(1)}, f32[8,128]{1,0:T(8,128)S(1)}, u32[]{:S(2)}, u32[]{:S(2)}) collective-permute-start(f32[8,128]{1,0:T(8,128)S(1)} %get-tuple-element.35.i0), channel_id=1, source_target_pairs={{0,2},{1,3},{2,0},{3,1},{4,6},{5,7},{6,4},{7,5},{8,10},{9,11},{10,... | collective-permute-start | bytes 12296 | tf_op jit(solution)/shard_map/ppermute | solution.py:34
  54.0 5.1 %collective-permute-start.17 = (f32[8,128]{1,0:T(8,128)S(1)}, f32[8,128]{1,0:T(8,128)S(1)}, u32[]{:S(2)}, u32[]{:S(2)}) collective-permute-start(f32[8,128]{1,0:T(8,128)S(1)} %get-tuple-element.35.i0), channel_id=1, source_target_pairs={{0,1},{1,2},{2,3},{3,0},{4,5},{5,6},{6,7},{7,4},{8,9},{9,10},{10,1... | collective-permute-start | bytes 12296 | tf_op jit(solution)/shard_map/ppermute | solution.py:34
  54.9 4.2 %collective-permute-start.18 = (f32[8,128]{1,0:T(8,128)S(1)}, f32[8,128]{1,0:T(8,128)S(1)}, u32[]{:S(2)}, u32[]{:S(2)}) collective-permute-start(f32[8,128]{1,0:T(8,128)S(1)} %get-tuple-element.35.i0), channel_id=1, source_target_pairs={{0,3},{1,0},{2,1},{3,2},{4,7},{5,4},{6,5},{7,6},{8,11},{9,8},{10,9... | collective-permute-start | bytes 12296 | tf_op jit(solution)/shard_map/ppermute | solution.py:34
  60.8 33.1 %copy-start.14 = (bf16[128,128]{1,0:T(8,128)(2,1)S(1)}, bf16[128,128]{1,0:T(8,128)(2,1)}, u32[]{:S(2)}) copy-start(bf16[128,128]{1,0:T(8,128)(2,1)} %param.12) | copy-start | bytes 98308
  60.8 36.5 %copy-start.4 = (bf16[128,2048]{1,0:T(8,128)(2,1)S(1)}, bf16[128,2048]{1,0:T(8,128)(2,1)}, u32[]{:S(2)}) copy-start(bf16[128,2048]{1,0:T(8,128)(2,1)} %og.5) | copy-start | bytes 1572868
  60.8 36.5 %copy-start.6 = (bf16[128,2048]{1,0:T(8,128)(2,1)S(1)}, bf16[128,2048]{1,0:T(8,128)(2,1)}, u32[]{:S(2)}) copy-start(bf16[128,2048]{1,0:T(8,128)(2,1)} %q.3) | copy-start | bytes 1572868
  64.2 1.3 %collective-permute-start.20 = (f32[128,128]{1,0:T(8,128)S(1)}, f32[128,128]{1,0:T(8,128)S(1)}, u32[]{:S(2)}, u32[]{:S(2)}) collective-permute-start(f32[128,128]{1,0:T(8,128)S(1)} %shard_map.153), channel_id=1, source_target_pairs={{0,4},{4,0},{1,5},{5,1},{2,6},{6,2},{3,7},{7,3},{8,12},{12,8},{9,1... | collective-permute-start | bytes 196616 | tf_op jit(solution)/shard_map/ppermute | solution.py:326
  65.6 5.6 %collective-permute-start.23 = (f32[128,128]{1,0:T(8,128)S(1)}, f32[128,128]{1,0:T(8,128)S(1)}, u32[]{:S(2)}, u32[]{:S(2)}) collective-permute-start(f32[128,128]{1,0:T(8,128)S(1)} %add.28), channel_id=1, source_target_pairs={{0,192},{8,200},{16,208},{24,216},{32,224},{40,232},{48,240},{56,2... | collective-permute-start | bytes 196616 | tf_op jit(solution)/shard_map/ppermute | solution.py:324
  66.2 8.5 %collective-permute-start.22 = (f32[128,128]{1,0:T(8,128)S(1)}, f32[128,128]{1,0:T(8,128)S(1)}, u32[]{:S(2)}, u32[]{:S(2)}) collective-permute-start(f32[128,128]{1,0:T(8,128)S(1)} %add.28), channel_id=1, source_target_pairs={{0,64},{8,72},{16,80},{24,88},{32,96},{40,104},{48,112},{56,120},{... | collective-permute-start | bytes 196616 | tf_op jit(solution)/shard_map/ppermute | solution.py:324
  68.9 5.8 %collective-permute-start.21 = (f32[128,128]{1,0:T(8,128)S(1)}, f32[128,128]{1,0:T(8,128)S(1)}, u32[]{:S(2)}, u32[]{:S(2)}) collective-permute-start(f32[128,128]{1,0:T(8,128)S(1)} %add.28), channel_id=1, source_target_pairs={{0,128},{8,136},{16,144},{24,152},{32,160},{40,168},{48,176},{56,1... | collective-permute-start | bytes 196616 | tf_op jit(solution)/shard_map/ppermute | solution.py:324
  70.0 27.4 %collective-permute-start.6 = (bf16[128,2048]{1,0:T(8,128)(2,1)S(1)}, bf16[128,2048]{1,0:T(8,128)(2,1)S(1)}, u32[]{:S(2)}, u32[]{:S(2)}) collective-permute-start(bf16[128,2048]{1,0:T(8,128)(2,1)S(1)} %shard_map.146.v0), channel_id=1, source_target_pairs={{0,4},{4,8},{8,12},{12,16},{16,20},{20,24},{24,28},{28,32},{32,36}... | collective-permute-start | bytes 1572872 | tf_op jit(solution)/shard_map/ppermute | solution.py:26
  70.1 27.3 %collective-permute-start.7 = (bf16[128,2048]{1,0:T(8,128)(2,1)S(1)}, bf16[128,2048]{1,0:T(8,128)(2,1)S(1)}, u32[]{:S(2)}, u32[]{:S(2)}) collective-permute-start(bf16[128,2048]{1,0:T(8,128)(2,1)S(1)} %shard_map.146.v0), channel_id=1, source_target_pairs={{0,8},{4,12},{8,16},{12,20},{16,24},{20,28},{24,32},{28,36},{32,40... | collective-permute-start | bytes 1572872 | tf_op jit(solution)/shard_map/ppermute | solution.py:26
  71.2 42.9 %collective-permute-start.19 = (bf16[128,2048]{1,0:T(8,128)(2,1)S(1)}, bf16[128,2048]{1,0:T(8,128)(2,1)S(1)}, u32[]{:S(2)}, u32[]{:S(2)}) collective-permute-start(bf16[128,2048]{1,0:T(8,128)(2,1)S(1)} %get-tuple-element.37.grad_signal), channel_id=1, source_target_pairs={{0,252},{4,0},{8,4},{12,8},{16,12},{20,16},{24,20},{28,24},{32,28}... | collective-permute-start | bytes 1572872 | tf_op jit(solution)/shard_map/ppermute | solution.py:26
  74.7 11.5 %collective-permute-start.24 = (f32[128,128]{1,0:T(8,128)S(1)}, f32[128,128]{1,0:T(8,128)S(1)}, u32[]{:S(2)}, u32[]{:S(2)}) collective-permute-start(f32[128,128]{1,0:T(8,128)S(1)} %add_add_fusion.1), channel_id=1, source_target_pairs={{0,32},{8,40},{16,48},{24,56},{32,0},{40,8},{48,16},{56,24},{64,96... | collective-permute-start | bytes 196616 | tf_op jit(solution)/shard_map/ppermute | solution.py:324
  86.2 23.0 %copy-start.9 = (bf16[128,2048]{1,0:T(8,128)(2,1)S(1)}, bf16[128,2048]{1,0:T(8,128)(2,1)}, u32[]{:S(2)}) copy-start(bf16[128,2048]{1,0:T(8,128)(2,1)} %copy-done.7) | copy-start | bytes 1572868
  86.2 4.4 %collective-permute-start.27 = (f32[128,128]{1,0:T(8,128)S(1)}, f32[128,128]{1,0:T(8,128)S(1)}, u32[]{:S(2)}, u32[]{:S(2)}) collective-permute-start(f32[128,128]{1,0:T(8,128)S(1)} %add.32), channel_id=1, source_target_pairs={{0,8},{8,0},{16,24},{24,16},{32,40},{40,32},{48,56},{56,48},{64,72... | collective-permute-start | bytes 196616 | tf_op jit(solution)/shard_map/ppermute | solution.py:324
  86.3 7.6 %collective-permute-start.26 = (f32[128,128]{1,0:T(8,128)S(1)}, f32[128,128]{1,0:T(8,128)S(1)}, u32[]{:S(2)}, u32[]{:S(2)}) collective-permute-start(f32[128,128]{1,0:T(8,128)S(1)} %add.32), channel_id=1, source_target_pairs={{0,16},{8,24},{16,0},{24,8},{32,48},{40,56},{48,32},{56,40},{64,80... | collective-permute-start | bytes 196616 | tf_op jit(solution)/shard_map/ppermute | solution.py:324
  90.6 6.1 %collective-permute-start.25 = (f32[128,128]{1,0:T(8,128)S(1)}, f32[128,128]{1,0:T(8,128)S(1)}, u32[]{:S(2)}, u32[]{:S(2)}) collective-permute-start(f32[128,128]{1,0:T(8,128)S(1)} %add.32), channel_id=1, source_target_pairs={{0,24},{8,16},{16,8},{24,0},{32,56},{40,48},{48,40},{56,32},{64,88... | collective-permute-start | bytes 196616 | tf_op jit(solution)/shard_map/ppermute | solution.py:324
  100.1 14.0 %copy-start.10 = (bf16[128,2048]{1,0:T(8,128)(2,1)S(1)}, bf16[128,2048]{1,0:T(8,128)(2,1)}, u32[]{:S(2)}) copy-start(bf16[128,2048]{1,0:T(8,128)(2,1)} %hyena_v.1) | copy-start | bytes 1572868
  100.2 14.0 %copy-start.11 = (bf16[128,2048]{1,0:T(8,128)(2,1)S(1)}, bf16[128,2048]{1,0:T(8,128)(2,1)}, u32[]{:S(2)}) copy-start(bf16[128,2048]{1,0:T(8,128)(2,1)} %hyena_k.1) | copy-start | bytes 1572868
  100.2 18.4 %collective-permute-start.14 = (f32[16,128]{1,0:T(8,128)S(1)}, f32[16,128]{1,0:T(8,128)S(1)}, u32[]{:S(2)}, u32[]{:S(2)}) collective-permute-start(f32[16,128]{1,0:T(8,128)S(1)} %get-tuple-element.27.delta_rows), channel_id=1, source_target_pairs={{0,252},{4,0},{8,4},{12,8},{16,12},{20,16},{24,20},{28,24},{32,28}... | collective-permute-start | bytes 24584 | tf_op jit(solution)/shard_map/ppermute | solution.py:26
  109.3 9.3 %collective-permute-start.15 = (f32[16,128]{1,0:T(8,128)S(1)}, f32[16,128]{1,0:T(8,128)S(1)}, u32[]{:S(2)}, u32[]{:S(2)}) collective-permute-start(f32[16,128]{1,0:T(8,128)S(1)} %get-tuple-element.27.delta_rows), channel_id=1, source_target_pairs={{0,248},{4,252},{8,0},{12,4},{16,8},{20,12},{24,16},{28,20},{32,24... | collective-permute-start | bytes 24584 | tf_op jit(solution)/shard_map/ppermute | solution.py:26
